TPU v7x, 32 devices: a whole 2x2x4 slice. The times are simulated.
32 devices in a mesh: batch: 8 (over z, y), group: 4 (over x, core).
Axes of the slice: x: 2, y: 2, z: 4, core: 2. Of those that a mesh axis runs over, the one named last changes fastest.
Arguments:
- inputs: bfloat16 [16, 32, 32, 768], P('batch', 'group'), may hold values from -6 to 6
- segments: int32 [16, 1024], P('batch'), may hold values from 0 to 3, never falling along the last dimension, each value on 1 to 384 neighbouring positions
- class_labels: int32 [16], P('batch'), may hold values from 0 to 999
- time_steps: int32 [16], P('batch'), may hold values from 0 to 999
- class_table: bfloat16 [1000, 768], replicated, may hold values from -6 to 6
- time_table: bfloat16 [1000, 768], replicated, may hold values from -6 to 6
- modulation_weight: bfloat16 [768, 4608], replicated, may hold values from -0.21875 to 0.21875
- project_weight: bfloat16 [768, 2304], replicated, may hold values from -0.21875 to 0.21875
- output_weight: bfloat16 [768, 768], replicated, may hold values from -0.875 to 0.875
- kernel_attention: bfloat16 [9, 768], replicated, may hold values from -2 to 2
- up_weight: bfloat16 [768, 3072], replicated, may hold values from -0.21875 to 0.21875
- kernel_feed: bfloat16 [9, 3072], replicated, may hold values from -2 to 2
- down_weight: bfloat16 [3072, 768], replicated, may hold values from -0.109375 to 0.109375
- cotangent: bfloat16 [16, 32, 32, 768], P('batch', 'group'), may hold values from -6 to 6
Outputs:
- result: bfloat16 [16, 32, 32, 768], P('batch', 'group')
- inputs_gradient: bfloat16 [16, 32, 32, 768], P('batch', 'group')
- class_table_gradient: float32 [1000, 768], P(None, 'batch')
- time_table_gradient: float32 [1000, 768], P(None, 'batch')
- modulation_weight_gradient: float32 [768, 4608], P('batch')
- project_weight_gradient: float32 [768, 2304], P('batch')
- output_weight_gradient: float32 [768, 768], P('batch')
- kernel_attention_gradient: float32 [9, 768], P(None, 'batch')
- up_weight_gradient: float32 [768, 3072], P('batch')
- kernel_feed_gradient: float32 [9, 3072], P(None, 'batch')
- down_weight_gradient: float32 [3072, 768], P('batch')
All inputs are finite; a program needn't handle non-finite values.
Results may differ from a plain program's by a relative error of at most 0.023.
The roundings to bfloat16 on the way count: a program that leaves them out, or rounds other values in their place, can miss the bound.
Values may be sent and summed in bfloat16 or wider, within the bound.
A program may use at most 192 MiB of HBM per device.

v0:
```python
from functools import partial

import jax
import jax.numpy as jnp
from jax import lax
from jax.sharding import PartitionSpec as P

HEADS = 12


highest = lax.Precision.HIGHEST


def padded_2(block, sides, width):
    for axis, dim in sides:
        count = lax.axis_size(axis)
        forward = [(i, i + 1) for i in range(count - 1)]
        backward = [(target, source) for source, target in forward]
        low = lax.ppermute(
            lax.slice_in_dim(block, block.shape[dim] - width, None, axis=dim), axis, forward
        )
        high = lax.ppermute(lax.slice_in_dim(block, 0, width, axis=dim), axis, backward)
        block = jnp.concatenate([low, block, high], axis=dim)
    return block


def layer_norm(values):
    center = values - jnp.mean(values, axis=-1, keepdims=True)
    second = jnp.mean(center * center, axis=-1, keepdims=True)
    return center * lax.rsqrt(second + 1e-06)


def modulate(values, shift, scale):
    return layer_norm(values) * (1.0 + scale) + shift


def pad_columns(values):
    return jnp.pad(values, ((0, 0), (0, 0), (1, 1), (0, 0)))


def depthwise(padded, kernel, height, across):
    total = jnp.zeros((padded.shape[0], height, across, padded.shape[3]), jnp.float32)
    for offset in range(9):
        down = offset // 3
        right = offset % 3
        total = (
            total
            + kernel[offset].astype(jnp.float32)
            * padded[:, down : down + height, right : right + across, :]
        )
    return total


def depthwise_back(padded, kernel, height, across):
    total = jnp.zeros((padded.shape[0], height, across, padded.shape[3]), jnp.float32)
    for offset in range(9):
        down = offset // 3
        right = offset % 3
        total = (
            total
            + kernel[offset].astype(jnp.float32)
            * padded[:, 2 - down : 2 - down + height, 2 - right : 2 - right + across, :]
        )
    return total


def kernel_terms(padded, upstream, height, across):
    rows_all = []
    for offset in range(9):
        down = offset // 3
        right = offset % 3
        rows_all.append(
            jnp.sum(
                padded[:, down : down + height, right : right + across, :] * upstream,
                axis=(0, 1, 2),
            )
        )
    return jnp.stack(rows_all)


def to_groups(values):
    count, height, across, channels = values.shape
    parted = values.reshape(count, height // 2, 2, across // 2, 2, channels)
    return parted.transpose(0, 2, 4, 1, 3, 5).reshape(count, 4, height // 2, across // 2, channels)


def finish_groups(received):
    count = received.shape[0]
    rows_half = received.shape[2]
    half = received.shape[3]
    channels = received.shape[4]
    parted = received.reshape(count, 2, 2, rows_half, half, channels)
    return parted.transpose(0, 3, 1, 4, 2, 5).reshape(count, 2 * rows_half, 2 * half, channels)


def attend_block(queries, keys, values, labels, score_scale):
    allowed = labels[:, :, None] == labels[:, None, :]
    scores = (
        jnp.einsum("blhe,bmhe->bhlm", queries, keys, preferred_element_type=jnp.float32)
        * score_scale
    )
    masked = jnp.where(allowed[:, None], scores, -1e30)
    top = jnp.max(masked, axis=-1, keepdims=True)
    total = jnp.sum(jnp.exp(masked - top), axis=-1, keepdims=True)
    logsum = top + jnp.log(total)
    weights = jnp.exp(masked - logsum).astype(jnp.bfloat16)
    attended = jnp.einsum("bhlm,bmhe->blhe", weights, values, preferred_element_type=jnp.float32)
    return (attended.astype(jnp.bfloat16), logsum)


def attend_back(queries, keys, values, labels, logsum, upstream, score_scale):
    allowed = labels[:, :, None] == labels[:, None, :]
    scores = (
        jnp.einsum("blhe,bmhe->bhlm", queries, keys, preferred_element_type=jnp.float32)
        * score_scale
    )
    masked = jnp.where(allowed[:, None], scores, -1e30)
    weights = jnp.exp(masked - logsum)
    weights_low = weights.astype(jnp.bfloat16)
    weights_grad = jnp.einsum(
        "blhe,bmhe->bhlm", upstream, values, preferred_element_type=jnp.float32
    )
    inner = jnp.sum(weights * weights_grad, axis=-1, keepdims=True)
    scores_grad = (weights * (weights_grad - inner)).astype(jnp.bfloat16)
    query_grad = (
        jnp.einsum("bhlm,bmhe->blhe", scores_grad, keys, preferred_element_type=jnp.float32)
        * score_scale
    )
    key_grad = (
        jnp.einsum("bhlm,blhe->bmhe", scores_grad, queries, preferred_element_type=jnp.float32)
        * score_scale
    )
    value_grad = jnp.einsum(
        "bhlm,blhe->bmhe", weights_low, upstream, preferred_element_type=jnp.float32
    )
    return jnp.stack([query_grad, key_grad, value_grad], axis=2).astype(jnp.bfloat16)


def body(
    inputs,
    segments,
    class_labels,
    time_steps,
    class_table,
    time_table,
    modulation_weight,
    project_weight,
    output_weight,
    kernel_attention,
    up_weight,
    kernel_feed,
    down_weight,
    cotangent,
):
    count, height, across, width = inputs.shape
    place = lax.axis_index("group")
    head_size = width // HEADS
    score_scale = head_size ** (-0.5)
    half = across // 2
    length = half * half
    blocks = count // 2
    class_hot = (class_labels[:, None] == jnp.arange(class_table.shape[0])[None, :]).astype(
        jnp.bfloat16
    )
    time_hot = (time_steps[:, None] == jnp.arange(time_table.shape[0])[None, :]).astype(
        jnp.bfloat16
    )
    cond = jnp.dot(class_hot, class_table, preferred_element_type=jnp.float32) + jnp.dot(
        time_hot, time_table, preferred_element_type=jnp.float32
    )
    cond_act, silu_back = jax.vjp(jax.nn.silu, cond)
    cond_low = cond_act.astype(jnp.bfloat16)
    modulation = jnp.dot(cond_low, modulation_weight, preferred_element_type=jnp.float32)
    pieces = [
        modulation[:, index * width : (index + 1) * width][:, None, None, :] for index in range(6)
    ]
    shift_one, scale_one, gate_one, shift_two, scale_two, gate_two = pieces
    values_in = inputs.astype(jnp.float32)
    attention_in = modulate(values_in, shift_one, scale_one).astype(jnp.bfloat16)
    padded_in = pad_columns(padded_2(attention_in, (("group", 1),), 1)).astype(jnp.float32)
    mixed = depthwise(padded_in, kernel_attention, height, across).astype(jnp.bfloat16)
    grouped = lax.all_to_all(to_groups(mixed), "group", split_axis=1, concat_axis=1, tiled=True)
    tokens = grouped.reshape(count, length, width)
    projected = jnp.dot(tokens, project_weight, preferred_element_type=jnp.float32).astype(
        jnp.bfloat16
    )
    split = projected.reshape(blocks, 2, length, 3, HEADS, head_size)
    queries = split[:, :, :, 0]
    keys = split[:, :, :, 1]
    values = split[:, :, :, 2]
    label_grid = (
        segments.reshape(count, half, 2, half, 2).transpose(0, 2, 4, 1, 3).reshape(count, 4, length)
    )
    labels = lax.dynamic_index_in_dim(label_grid, place, axis=1, keepdims=False).reshape(
        blocks, 2, length
    )

    def forward_block(items):
        return attend_block(items[0], items[1], items[2], items[3], score_scale)

    attended, logsum = lax.map(forward_block, (queries, keys, values, labels))
    attended_flat = attended.reshape(count, length, width)
    branch = jnp.dot(attended_flat, output_weight, preferred_element_type=jnp.float32).astype(
        jnp.bfloat16
    )
    returned = finish_groups(
        lax.all_to_all(
            branch.reshape(count, 4, height // 2, half, width),
            "group",
            split_axis=1,
            concat_axis=1,
            tiled=True,
        )
    )
    returned_wide = returned.astype(jnp.float32)
    middle = values_in + gate_one * returned_wide
    feed_in = modulate(middle, shift_two, scale_two).astype(jnp.bfloat16)
    hidden = jnp.dot(feed_in, up_weight, preferred_element_type=jnp.float32).astype(jnp.bfloat16)
    padded_hidden = pad_columns(padded_2(hidden, (("group", 1),), 1)).astype(jnp.float32)
    spread = depthwise(padded_hidden, kernel_feed, height, across)
    activated, gelu_back = jax.vjp(partial(jax.nn.gelu, approximate=False), spread)
    activated_low = activated.astype(jnp.bfloat16)
    branch_two = jnp.dot(activated_low, down_weight, preferred_element_type=jnp.float32)
    result = (middle + gate_two * branch_two).astype(jnp.bfloat16)
    upstream = cotangent.astype(jnp.float32)
    gate_two_grad = jnp.sum(upstream * branch_two, axis=(1, 2))
    branch_two_grad = (gate_two * upstream).astype(jnp.bfloat16)
    down_grad = jnp.einsum(
        "crsf,crsd->fd", activated_low, branch_two_grad, preferred_element_type=jnp.float32
    )
    activated_grad = jnp.einsum(
        "crsd,fd->crsf", branch_two_grad, down_weight, preferred_element_type=jnp.float32
    )
    spread_grad = gelu_back(activated_grad)[0].astype(jnp.bfloat16)
    padded_spread = pad_columns(padded_2(spread_grad, (("group", 1),), 1)).astype(jnp.float32)
    feed_kernel_grad = kernel_terms(padded_hidden, spread_grad.astype(jnp.float32), height, across)
    hidden_grad = depthwise_back(padded_spread, kernel_feed, height, across).astype(jnp.bfloat16)
    up_grad = jnp.einsum("crsd,crsf->df", feed_in, hidden_grad, preferred_element_type=jnp.float32)
    feed_in_grad = jnp.einsum(
        "crsf,df->crsd", hidden_grad, up_weight, preferred_element_type=jnp.float32
    )
    second_back = jax.vjp(modulate, middle, shift_two, scale_two)[1]
    middle_term, shift_two_grad, scale_two_grad = second_back(feed_in_grad)
    middle_grad = upstream + middle_term
    gate_one_grad = jnp.sum(middle_grad * returned_wide, axis=(1, 2))
    returned_grad = (gate_one * middle_grad).astype(jnp.bfloat16)
    branch_grad = lax.all_to_all(
        to_groups(returned_grad), "group", split_axis=1, concat_axis=1, tiled=True
    ).reshape(count, length, width)
    output_grad = jnp.einsum(
        "cld,cle->de", attended_flat, branch_grad, preferred_element_type=jnp.float32
    )
    attended_grad = jnp.einsum(
        "cle,de->cld", branch_grad, output_weight, preferred_element_type=jnp.float32
    ).astype(jnp.bfloat16)

    def backward_block(items):
        return attend_back(items[0], items[1], items[2], items[3], items[4], items[5], score_scale)

    projected_grad = lax.map(
        backward_block,
        (
            queries,
            keys,
            values,
            labels,
            logsum,
            attended_grad.reshape(blocks, 2, length, HEADS, head_size),
        ),
    )
    projected_grad = projected_grad.reshape(count, length, 3 * width)
    project_grad = jnp.einsum(
        "cld,cle->de", tokens, projected_grad, preferred_element_type=jnp.float32
    )
    tokens_grad = jnp.einsum(
        "cle,de->cld", projected_grad, project_weight, preferred_element_type=jnp.float32
    ).astype(jnp.bfloat16)
    mixed_grad = finish_groups(
        lax.all_to_all(
            tokens_grad.reshape(count, 4, height // 2, half, width),
            "group",
            split_axis=1,
            concat_axis=1,
            tiled=True,
        )
    )
    padded_mixed = pad_columns(padded_2(mixed_grad, (("group", 1),), 1)).astype(jnp.float32)
    attention_kernel_grad = kernel_terms(padded_in, mixed_grad.astype(jnp.float32), height, across)
    attention_in_grad = depthwise_back(padded_mixed, kernel_attention, height, across)
    first_back = jax.vjp(modulate, values_in, shift_one, scale_one)[1]
    input_term, shift_one_grad, scale_one_grad = first_back(attention_in_grad)
    inputs_gradient = (middle_grad + input_term).astype(jnp.bfloat16)
    modulation_grad = jnp.concatenate(
        [
            shift_one_grad.reshape(count, width),
            scale_one_grad.reshape(count, width),
            gate_one_grad,
            shift_two_grad.reshape(count, width),
            scale_two_grad.reshape(count, width),
            gate_two_grad,
        ],
        axis=1,
    )
    cond_act_grad = jnp.dot(
        modulation_grad, modulation_weight.astype(jnp.float32).T, precision=highest
    )
    cond_grad = silu_back(cond_act_grad)[0]
    modulation_grad_weight = jnp.dot(
        cond_low.astype(jnp.float32).T, modulation_grad, precision=highest
    )
    class_grad = jnp.dot(class_hot.astype(jnp.float32).T, cond_grad, precision=highest)
    time_grad = jnp.dot(time_hot.astype(jnp.float32).T, cond_grad, precision=highest)
    every_share = (
        lax.psum_scatter(
            class_grad.astype(jnp.bfloat16), "batch", scatter_dimension=1, tiled=True
        ).astype(jnp.float32),
        lax.psum_scatter(
            time_grad.astype(jnp.bfloat16), "batch", scatter_dimension=1, tiled=True
        ).astype(jnp.float32),
        lax.psum_scatter(
            modulation_grad_weight.astype(jnp.bfloat16), "batch", scatter_dimension=0, tiled=True
        ).astype(jnp.float32),
        lax.psum_scatter(
            project_grad.astype(jnp.bfloat16), "batch", scatter_dimension=0, tiled=True
        ).astype(jnp.float32),
        lax.psum_scatter(
            output_grad.astype(jnp.bfloat16), "batch", scatter_dimension=0, tiled=True
        ).astype(jnp.float32),
        lax.psum_scatter(
            attention_kernel_grad.astype(jnp.bfloat16), "batch", scatter_dimension=1, tiled=True
        ).astype(jnp.float32),
        lax.psum_scatter(
            up_grad.astype(jnp.bfloat16), "batch", scatter_dimension=0, tiled=True
        ).astype(jnp.float32),
        lax.psum_scatter(
            feed_kernel_grad.astype(jnp.bfloat16), "batch", scatter_dimension=1, tiled=True
        ).astype(jnp.float32),
        lax.psum_scatter(
            down_grad.astype(jnp.bfloat16), "batch", scatter_dimension=0, tiled=True
        ).astype(jnp.float32),
    )
    (
        class_total,
        time_total,
        modulation_total,
        project_total,
        output_total,
        attention_kernel_total,
        up_total,
        feed_kernel_total,
        down_total,
    ) = (
        lax.psum(every_share[0].astype(jnp.bfloat16), "group").astype(jnp.float32),
        lax.psum(every_share[1].astype(jnp.bfloat16), "group").astype(jnp.float32),
        lax.psum(every_share[2].astype(jnp.bfloat16), "group").astype(jnp.float32),
        lax.psum(every_share[3].astype(jnp.bfloat16), "group").astype(jnp.float32),
        lax.psum(every_share[4].astype(jnp.bfloat16), "group").astype(jnp.float32),
        lax.psum(every_share[5].astype(jnp.bfloat16), "group").astype(jnp.float32),
        lax.psum(every_share[6].astype(jnp.bfloat16), "group").astype(jnp.float32),
        lax.psum(every_share[7].astype(jnp.bfloat16), "group").astype(jnp.float32),
        lax.psum(every_share[8].astype(jnp.bfloat16), "group").astype(jnp.float32),
    )
    return (
        result,
        inputs_gradient,
        class_total,
        time_total,
        modulation_total,
        project_total,
        output_total,
        attention_kernel_total,
        up_total,
        feed_kernel_total,
        down_total,
    )


def solution(mesh):
    in_specs = (
        P("batch", "group", None, None),
        P("batch", None),
        P("batch"),
        P("batch"),
        P(),
        P(),
        P(),
        P(),
        P(),
        P(),
        P(),
        P(),
        P(),
        P("batch", "group", None, None),
    )
    out_specs = (
        P("batch", "group", None, None),
        P("batch", "group", None, None),
        P(None, "batch"),
        P(None, "batch"),
        P("batch", None),
        P("batch", None),
        P("batch", None),
        P(None, "batch"),
        P("batch", None),
        P(None, "batch"),
        P("batch", None),
    )
    return jax.shard_map(body, mesh=mesh, in_specs=in_specs, out_specs=out_specs, check_vma=False)
```

profile of v0, /device:TPU:0, one launch (start us, length us, event | category | flops | bytes accessed | tf_op | source)
XLA Modules:
  0.0 1126.3 jit_solution(10796002031985115826)
XLA Ops:
  12.5 4.1 fusion.105
  17.6 2.4 collective-permute-start
  21.6 3.8 collective-permute-done.1
  27.1 2.4 add_convert_fusion.4
  29.6 2.8 reshape.290
  34.5 4.5 all-to-all-start
  46.4 4.4 all-to-all-done
  52.8 3.4 convolution_convert_fusion.1
  56.3 4.3 copy.59
  60.5 2.6 fusion.28
  65.8 2.8 convolution_convert_fusion.6
  69.6 14.0 %all_to_all.20 = bf16[2,4,4,16,768]{4,3,2,0,1:T(8,128)(2,1)S(1)} all-to-all(bf16[2,4,4,16,768]{4,3,2,0,1:T(8,128)(2,1)S(1)} %copy.66), channel_id=1, replica_groups=mesh['batch'=8,'group'=4] {'group'}, dimensions={1} | all-to-all | bytes 1572864 | tf_op jit(solution)/shard_map/all_to_all | solution.py:207
  85.5 3.1 reshape.313
  91.0 5.5 fusion.37
  103.9 22.4 %multiply_convert_fusion.1 = (bf16[2,8,32,3072]{3,2,1,0:T(8,128)(2,1)}, f32[2,8,32,3072]{3,2,1,0:T(8,128)}, f32[2,8,32,3072]{3,2,1,0:T(8,128)}) fusion(f32[2,10,34,3072]{3,2,1,0:T(8,128)S(1)} %fusion.26, f32[3072]{0:T(1024)S(1)} %bitcast.194, f32[3072]{0:T(1024)S(1)} %bitcast.196, f32[3072]{0:T(1024)S(1)} %bitcast.182, f32[3072]{0:T(1024)S(1)} %bitcast.184, ...), kind=kLoop, calls=%fused_computation.48 | loop fusion | flops 128974848 | bytes 72462336 | tf_op jit(solution)/shard_map/convert_element_type | solution.py:222
  126.3 37.1 %fusion.10 = (bf16[3072]{0:T(1024)(128)(2,1)}, bf16[3072]{0:T(1024)(128)(2,1)}, bf16[3072]{0:T(1024)(128)(2,1)}, bf16[3072]{0:T(1024)(128)(2,1)}, bf16[3072]{0:T...) fusion(f32[2,10,34,3072]{3,2,1,0:T(8,128)} %copy-done.1, ...), kind=kOutput, calls=%fused_computation.26 | convolution fusion | flops 2468975616 | bytes 77918208 | tf_op jit(solution)/shard_map/crsd,fd->crsf/dot_general | solution.py:231
  164.6 7.9 collective-permute-start.4
  173.9 2.3 collective-permute-done.5
  176.2 6.1 fusion.25
  182.2 26.4 %fusion.12 = bf16[2,8,32,3072]{3,2,1,0:T(8,128)(2,1)} fusion(f32[2,10,34,3072]{3,2,1,0:T(8,128)} %fusion.25, f32[3072]{0:T(1024)S(1)} %bitcast.195, f32[3072]{0:T(1024)S(1)} %bitcast.197, f32[3072]{0:T(1024)S(1)} %bitcast.183, f32[3072]{0:T(1024)S(1)} %bitcast.185, f32[3072]{0:T(1024)S(1)} %bitcast.187, f32[3072]{0:T(1024)S(1)} %bitcast.189, ...), kind=kLoop, calls=%fused_computation.29 | loop fusion | flops 28311552 | bytes 59879424 | tf_op jit(solution)/shard_map/convert_element_type | solution.py:237
  208.7 6.9 multiply_reduce_fusion.1
  218.5 2.8 reshape.298
  222.7 18.3 %all_to_all.21 = bf16[2,4,4,16,768]{4,3,2,0,1:T(8,128)(2,1)S(1)} all-to-all(bf16[2,4,4,16,768]{4,3,2,0,1:T(8,128)(2,1)S(1)} %bitcast.167), channel_id=1, replica_groups=mesh['batch'=8,'group'=4] {'group'}, dimensions={1} | all-to-all | bytes 1572864 | tf_op jit(solution)/shard_map/all_to_all | solution.py:247
  246.0 4.6 convolution_bitcast_fusion
  250.7 5.8 multiply_reduce_fusion
  256.5 4.6 multiply_convert_fusion
  265.5 14.0 %all_to_all.22 = bf16[2,4,4,16,768]{4,3,2,0,1:T(8,128)(2,1)S(1)} all-to-all(bf16[2,4,4,16,768]{4,3,2,0,1:T(8,128)(2,1)S(1)} %copy.77), channel_id=1, replica_groups=mesh['batch'=8,'group'=4] {'group'}, dimensions={1} | all-to-all | bytes 1572864 | tf_op jit(solution)/shard_map/all_to_all | solution.py:279
  281.2 3.0 reshape.303
  289.1 3.2 bitcast_convert_fusion.3
  297.9 7.1 fusion.59
  305.1 5.5 fusion.117
  310.7 2.7 convolution_convert_fusion.2
  313.4 3.3 convolution_convert_fusion.3
  316.8 5.7 bitcast_convert_fusion.2
  323.2 7.0 bitcast_convert_fusion
  330.9 7.4 bitcast_convert_fusion.1
  338.4 8.6 convolution_convert_fusion
  362.6 8.0 fusion.68
  377.2 50.5 %reduce-scatter.16.cloned.1.call-done = bf16[1000,96]{0,1:T(8,128)(2,1)} async-done(((bf16[1000,768]{0,1:T(8,128)(2,1)}), bf16[1000,96]{0,1:T(8,128)(2,1)}) %reduce-scatter.16.cloned.1.call-update) | async-done | bytes 192016 | tf_op jit(solution)/shard_map/reduce_scatter | solution.py:317
  427.7 68.4 %reduce-scatter.14.cloned.1.call-done = bf16[1000,96]{0,1:T(8,128)(2,1)} async-done(((bf16[1000,768]{0,1:T(8,128)(2,1)}), bf16[1000,96]{0,1:T(8,128)(2,1)}) %reduce-scatter.14.cloned.1.call-update) | async-done | bytes 192016 | tf_op jit(solution)/shard_map/reduce_scatter | solution.py:314
  496.1 81.8 %reduce-scatter.20.cloned.1.call-done = bf16[96,2304]{1,0:T(8,128)(2,1)} async-done(((bf16[768,2304]{1,0:T(8,128)(2,1)}), bf16[96,2304]{1,0:T(8,128)(2,1)}) %reduce-scatter.20.cloned.1.call-update) | async-done | bytes 442384 | tf_op jit(solution)/shard_map/reduce_scatter | solution.py:323
  577.9 98.8 %reduce-scatter.26.cloned.1.call-done = bf16[384,768]{1,0:T(8,128)(2,1)} async-done(((bf16[3072,768]{1,0:T(8,128)(2,1)}), bf16[384,768]{1,0:T(8,128)(2,1)}) %reduce-scatter.26.cloned.1.call-update) | async-done | bytes 589840 | tf_op jit(solution)/shard_map/reduce_scatter | solution.py:338
  676.7 98.8 %reduce-scatter.24.cloned.1.call-done = bf16[96,3072]{1,0:T(8,128)(2,1)} async-done(((bf16[768,3072]{1,0:T(8,128)(2,1)}), bf16[96,3072]{1,0:T(8,128)(2,1)}) %reduce-scatter.24.cloned.1.call-update) | async-done | bytes 589840 | tf_op jit(solution)/shard_map/reduce_scatter | solution.py:332
  775.5 132.9 %reduce-scatter.18.cloned.1.call-done = bf16[96,4608]{1,0:T(8,128)(2,1)} async-done(((bf16[768,4608]{1,0:T(8,128)(2,1)}), bf16[96,4608]{1,0:T(8,128)(2,1)}) %reduce-scatter.18.cloned.1.call-update) | async-done | bytes 884752 | tf_op jit(solution)/shard_map/reduce_scatter | solution.py:320
  908.4 66.3 %reduce-scatter.30.cloned.1.call-done = bf16[384,9]{1,0:T(8,128)(2,1)} async-done(((bf16[3072,9]{1,0:T(8,128)(2,1)}), bf16[384,9]{1,0:T(8,128)(2,1)}) %reduce-scatter.30.cloned.1.call-update) | async-done | bytes 6928
  975.7 63.9 %reduce-scatter.28.cloned.1.call-done = bf16[96,9]{1,0:T(8,128)(2,1)} async-done(((bf16[768,9]{1,0:T(8,128)(2,1)}), bf16[96,9]{1,0:T(8,128)(2,1)}) %reduce-scatter.28.cloned.1.call-update) | async-done | bytes 1744
  1040.3 11.4 %all-reduce.4 = (bf16[9,96]{1,0:T(8,128)(2,1)}, bf16[9,384]{1,0:T(8,128)(2,1)}) all-reduce(bf16[9,96]{1,0:T(8,128)(2,1)S(1)} %copy.97, bf16[9,384]{1,0:T(8,128)(2,1)S(1)} %copy.99), channel_id=1, replica_groups=mesh['batch'=8,'group'=4] {'group'}, use_global_device_ids=true, to_apply=%region_37.38 | all-reduce | flops 4320 | bytes 17280 | tf_op jit(solution)/shard_map/psum | solution.py:358
  1054.3 54.0 %all-reduce.8.cloned.1.call-done = (bf16[1000,96]{0,1:T(8,128)(2,1)}, bf16[1000,96]{0,1:T(8,128)(2,1)}, bf16[96,4608]{1,0:T(8,128)(2,1)}, bf16[96,2304]{1,0:T(8,...) async-done(((bf16[1000,96]{0,1:T(8,128)(2,1)}, bf16[1000,96]{0,1:T(8,128)(2,1)}, bf16[96,4608]{1,0:T(8,128)(2,1)}, ...) | async-done | bytes 3038224 | tf_op jit(solution)/shard_map/psum | solution.py:353
  (279 shorter events, 102.7 us)
Async XLA Ops:
  7.2 45.7 %copy-start = (bf16[768,2304]{1,0:T(8,128)(2,1)S(1)}, bf16[768,2304]{1,0:T(8,128)(2,1)}, u32[]{:S(2)}) copy-start(bf16[768,2304]{1,0:T(8,128)(2,1)} %param.21) | copy-start | bytes 10616836
  7.2 4.9 copy-start.67
  7.2 4.9 copy-start.17
  10.4 6.9 copy-start.31
  12.5 4.7 copy-start.4
  12.5 8.8 copy-start.59
  17.6 3.9 collective-permute-start
  20.1 5.3 collective-permute-start.1
  34.5 16.2 %all-to-all-start = ((bf16[2,4,4,16,768]{4,3,2,0,1:T(8,128)(2,1)}), bf16[2,4,4,16,768]{4,3,2,0,1:T(8,128)(2,1)}, u32[]{:S(2)}, u32[]{:S(2)}) async-start(bf16[2,4,4,16,768]{4,3,2,0,1:T(8,128)(2,1)} %bitcast.165), calls=%async_computation | async-start | bytes 1572864 | tf_op jit(solution)/shard_map/all_to_all | solution.py:182
  39.0 338.2 %reduce-scatter.22.cloned.1.call-start = ((), (), s32[]{:S(2)}) async-start(), calls=%async_computation.17 | async-start | bytes 1327104 | tf_op jit(solution)/shard_map/reduce_scatter | solution.py:326
  68.6 15.0 %copy-start.71 = (bf16[2,12,64,256]{3,2,1,0:T(8,128)(2,1)}, bf16[2,12,64,256]{3,2,1,0:T(8,128)(2,1)S(1)}, u32[]{:S(2)}) copy-start(bf16[2,12,64,256]{3,2,1,0:T(8,128)(2,1)S(1)} %convolution_convert_fusion.6) | copy-start | bytes 2359300
  90.6 124.9 %copy-start.6 = (f32[2,8,32,768]{3,2,1,0:T(8,128)}, f32[2,8,32,768]{3,2,1,0:T(8,128)S(1)}, u32[]{:S(2)}) copy-start(f32[2,8,32,768]{3,2,1,0:T(8,128)S(1)} %get-tuple-element.108) | copy-start | bytes 4718596
  90.6 124.9 %copy-start.33 = (f32[2,8,32]{2,1,0:T(8,128)}, f32[2,8,32]{2,1,0:T(8,128)S(1)}, u32[]{:S(2)}) copy-start(f32[2,8,32]{2,1,0:T(8,128)S(1)} %broadcast_multiply_fusion) | copy-start | bytes 6148
  91.0 124.6 %copy-start.56 = (f32[2,8,32]{2,1,0:T(8,128)}, f32[2,8,32]{2,1,0:T(8,128)S(1)}, u32[]{:S(2)}) copy-start(f32[2,8,32]{2,1,0:T(8,128)S(1)} %fusion.92) | copy-start | bytes 6148
  91.0 8.8 copy-start.30
  96.6 3.3 collective-permute-start.2
  98.0 4.1 collective-permute-start.3
  103.9 22.4 %copy-start.1 = (f32[2,10,34,3072]{3,2,1,0:T(8,128)}, f32[2,10,34,3072]{3,2,1,0:T(8,128)S(1)}, u32[]{:S(2)}) copy-start(f32[2,10,34,3072]{3,2,1,0:T(8,128)S(1)} %fusion.26) | copy-start | bytes 25067524
  103.9 22.4 %copy-start.21 = (bf16[2,8,32,768]{3,2,1,0:T(8,128)(2,1)S(1)}, bf16[2,8,32,768]{3,2,1,0:T(8,128)(2,1)}, u32[]{:S(2)}) copy-start(bf16[2,8,32,768]{3,2,1,0:T(8,128)(2,1)} %param.27) | copy-start | bytes 2359300
  103.9 22.4 %copy-start.62 = (f32[2,768]{1,0:T(2,128)S(1)}, f32[2,768]{1,0:T(2,128)}, u32[]{:S(2)}) copy-start(f32[2,768]{1,0:T(2,128)} %get-tuple-element.128) | copy-start | bytes 18436
  164.6 9.2 collective-permute-start.4
  172.5 3.6 collective-permute-start.5
  221.4 20.6 %copy-start.70 = (bf16[768,768]{1,0:T(8,128)(2,1)S(1)}, bf16[768,768]{1,0:T(8,128)(2,1)}, u32[]{:S(2)}) copy-start(bf16[768,768]{1,0:T(8,128)(2,1)} %param.22) | copy-start | bytes 3538948
  246.0 4.6 copy-start.16
  246.0 4.7 copy-start.26
  246.0 10.4 slice-start
  250.7 5.8 slice-start.1
  285.8 6.8 collective-permute-start.6
  287.8 4.9 collective-permute-start.7
  292.3 135.4 %reduce-scatter.16.cloned.1.call-start = ((), (), s32[]{:S(2)}) async-start(), calls=%async_computation.14 | async-start | bytes 1769472 | tf_op jit(solution)/shard_map/reduce_scatter | solution.py:317
  294.4 10.6 slice-start.2
  297.8 7.1 copy-start.66
  297.8 7.1 copy-start.65
  297.8 7.2 slice-start.3
  305.0 5.6 copy-start.29
  305.1 5.6 copy-start.28
  305.1 5.6 copy-start.68
  313.3 182.8 %reduce-scatter.14.cloned.1.call-start = ((), (), s32[]{:S(2)}) async-start(), calls=%async_computation.13 | async-start | bytes 1769472 | tf_op jit(solution)/shard_map/reduce_scatter | solution.py:314
  316.7 261.1 %reduce-scatter.20.cloned.1.call-start = ((), (), s32[]{:S(2)}) async-start(), calls=%async_computation.16 | async-start | bytes 3981312 | tf_op jit(solution)/shard_map/reduce_scatter | solution.py:323
  322.6 354.1 %reduce-scatter.26.cloned.1.call-start = ((), (), s32[]{:S(2)}) async-start(), calls=%async_computation.19 | async-start | bytes 5308416 | tf_op jit(solution)/shard_map/reduce_scatter | solution.py:338
  330.2 445.2 %reduce-scatter.24.cloned.1.call-start = ((), (), s32[]{:S(2)}) async-start(), calls=%async_computation.18 | async-start | bytes 5308416 | tf_op jit(solution)/shard_map/reduce_scatter | solution.py:332
  338.4 570.0 %reduce-scatter.18.cloned.1.call-start = ((), (), s32[]{:S(2)}) async-start(), calls=%async_computation.15 | async-start | bytes 7962624 | tf_op jit(solution)/shard_map/reduce_scatter | solution.py:320
  347.1 627.7 %reduce-scatter.30.cloned.1.call-start = ((), (), s32[]{:S(2)}) async-start(), calls=%async_computation.21 | async-start | bytes 884736
  362.5 677.0 %reduce-scatter.28.cloned.1.call-start = ((), (), s32[]{:S(2)}) async-start(), calls=%async_computation.20 | async-start | bytes 221184
  377.2 731.1 %all-reduce.8.cloned.1.call-start = ((), (), s32[]{:S(2)}) async-start(), calls=%async_computation.22 | async-start | bytes 6094848 | tf_op jit(solution)/shard_map/psum | solution.py:353
  1108.3 7.2 copy-start.24
  1108.3 8.3 copy-start.23
  1108.3 9.4 copy-start.18
  (47 other events, 124.8 us)
Sparse Core Ops, SparseCore 0:
  292.4 67.2 reduce-scatter.21
  363.1 64.5 reduce-scatter.15
  431.7 64.3 reduce-scatter.13
  499.6 78.2 reduce-scatter.19
  581.4 95.2 reduce-scatter.25
  680.2 95.2 reduce-scatter.23
  779.2 129.1 reduce-scatter.17
  912.2 62.4 reduce-scatter.29
  978.5 60.9 reduce-scatter.27
  1042.2 65.9 all-reduce.7
where the time goes:
time: 1130 us
  waiting for transfers between devices  728 us (64%)
  matrix products  132 us (12%)
  other arithmetic  101 us (9%)
  local copies, waits for them, and re-layouts  67 us (6%)
  blocking collectives  57.8 us (5%)
  starting transfers between devices  24.9 us (2%)
  between operations  15.9 us (1%)
    reduce_scatter x1, waiting for transfers between devices, body(): lax.psum_scatter(modulation_grad_weight.astype(jnp.bfloat16), 'batch', sc...  133 us
    unnamed x12, waiting for transfers between devices  130 us
    reduce_scatter x1, waiting for transfers between devices, body(): lax.psum_scatter(up_grad.astype(jnp.bfloat16), 'batch', scatter_dimension...  98.8 us
    reduce_scatter x1, waiting for transfers between devices, body(): lax.psum_scatter(down_grad.astype(jnp.bfloat16), 'batch', scatter_dimensi...  98.8 us
    reduce_scatter x1, waiting for transfers between devices, body(): lax.psum_scatter(project_grad.astype(jnp.bfloat16), 'batch', scatter_dime...  81.8 us
    reduce_scatter x1, waiting for transfers between devices, body(): lax.psum_scatter(class_grad.astype(jnp.bfloat16), 'batch', scatter_dimens...  68.4 us
    psum x1, waiting for transfers between devices, body(): lax.psum(every_share[0].astype(jnp.bfloat16), 'group').astype(jnp.float32)  54 us
    reduce_scatter x1, waiting for transfers between devices, body(): lax.psum_scatter(time_grad.astype(jnp.bfloat16), 'batch', scatter_dimensi...  50.5 us
  transfers between devices with their start and end apart: 19, of which 13 were waited for; matrix products, arithmetic and copies ran while one was open for 9% of the time, Pallas kernels for 0%

commit v1 on v0

--- a/solution.py
+++ b/solution.py
@@ -3,6 +3,8 @@
 import jax
 import jax.numpy as jnp
 from jax import lax
+from jax.experimental import pallas as pl
+from jax.experimental.pallas import tpu as pltpu
 from jax.sharding import PartitionSpec as P
 
 HEADS = 12
@@ -134,6 +136,265 @@
         "bhlm,blhe->bmhe", weights_low, upstream, preferred_element_type=jnp.float32
     )
     return jnp.stack([query_grad, key_grad, value_grad], axis=2).astype(jnp.bfloat16)
+
+
+MESH = pl.DeviceIdType.MESH
+CHUNK = 384
+
+
+def reduce_kernel(
+    nb, units, proj, outw, up, down, mg,
+    o_proj, o_out, o_up, o_down, o_mg,
+    s0, r1, r2x, r2y, r3, r4, fin, mg_own, mg_r1, mg_r2, mg_all,
+    load_sem, s1, q1, s2, q2, s3, q3, s4, q4, s5, q5, s6, q6, out_sem,
+    mg_send, mg_recv, mz_send, mz_recv, mg_io,
+):
+    nz = nb // 2
+    chunks = len(units)
+    b = lax.axis_index("batch")
+    g = lax.axis_index("group")
+    cb, xb = lax.rem(g, 2), g // 2
+    yb, zb = lax.rem(b, 2), b // 2
+    core = (b, g + 1 - 2 * cb)
+    side = (b, g + 2 - 4 * xb)
+    across = (b + 1 - 2 * yb, g)
+    others = [lax.rem(zb + d, nz) for d in range(nz)]
+    far = [(2 * z + yb, g) for z in others]
+    arrays = {"proj": proj, "out": outw, "up": up, "down": down}
+    results = {"proj": o_proj, "out": o_out, "up": o_up, "down": o_down}
+
+    def window(name, part, column, ref, lead):
+        if name == "down":
+            return ref.at[(*lead, part, slice(None), pl.ds(column, CHUNK))]
+        return ref.at[(*lead, slice(None), pl.ds(column, CHUNK))]
+
+    def remote(src, dst, send, recv, target):
+        return pltpu.make_async_remote_copy(
+            src_ref=src, dst_ref=dst, send_sem=send, recv_sem=recv, device_id=target,
+            device_id_type=MESH,
+        )
+
+    def load(k, q):
+        name, part, column = units[k][q]
+        source = window(name, part, column, arrays[name], (slice(None), slice(None)))
+        return pltpu.make_async_copy(source, s0.at[k, q % 2, q // 2], load_sem.at[k, q])
+
+    def store(k, q):
+        name, part, column = units[k][q]
+        target = window(name, part, column, results[name], ())
+        return pltpu.make_async_copy(fin.at[k, q % 2, q // 2], target, out_sem.at[k, q])
+
+    def copy_1(k):
+        return remote(s0.at[k, 1 - cb], r1.at[k], s1.at[k], q1.at[k], core)
+
+    def copy_2(k):
+        if k % 2 == 0:
+            return remote(s0.at[k, cb, 1 - xb], r2x.at[k // 2], s2.at[k], q2.at[k], side)
+        return remote(
+            s0.at[k, cb, :, :, 1 - yb], r2y.at[k // 2], s2.at[k], q2.at[k], across
+        )
+
+    def copy_3(k):
+        if k % 2 == 0:
+            return remote(s0.at[k, cb, xb, :, 1 - yb], r3.at[k], s3.at[k], q3.at[k], across)
+        return remote(s0.at[k, cb, 1 - xb, :, yb], r3.at[k], s3.at[k], q3.at[k], side)
+
+    def copy_4(k, d):
+        return remote(
+            s0.at[k, cb, xb, others[d], yb], r4.at[k, d - 1], s4.at[k, d - 1], q4.at[k, d - 1],
+            far[d],
+        )
+
+    def copy_5(k, mine):
+        place = xb if mine else 1 - xb
+        return remote(fin.at[k, cb, place], fin.at[k, cb, place], s5.at[k], q5.at[k], side)
+
+    def copy_6(k, mine):
+        place = cb if mine else 1 - cb
+        return remote(fin.at[k, place], fin.at[k, place], s6.at[k], q6.at[k], core)
+
+    def add_1(k):
+        copy_1(k).wait_recv()
+
+        def step(i, carry):
+            x, z, y = i // (2 * nz), lax.rem(i // 2, nz), lax.rem(i, 2)
+            s0[k, cb, x, z, y] = s0[k, cb, x, z, y] + r1[k, x, z, y]
+            return carry
+
+        lax.fori_loop(0, 4 * nz, step, 0)
+        copy_2(k).start()
+
+    def add_2(k):
+        copy_2(k).wait_recv()
+
+        def step(i, carry):
+            if k % 2 == 0:
+                z, y = i // 2, lax.rem(i, 2)
+                s0[k, cb, xb, z, y] = s0[k, cb, xb, z, y] + r2x[k // 2, z, y]
+            else:
+                x, z = i // nz, lax.rem(i, nz)
+                s0[k, cb, x, z, yb] = s0[k, cb, x, z, yb] + r2y[k // 2, x, z]
+            return carry
+
+        lax.fori_loop(0, 2 * nz, step, 0)
+        copy_3(k).start()
+
+    def add_3(k):
+        copy_3(k).wait_recv()
+
+        def step(z, carry):
+            s0[k, cb, xb, z, yb] = s0[k, cb, xb, z, yb] + r3[k, z]
+            return carry
+
+        lax.fori_loop(0, nz, step, 0)
+        for d in range(1, nz):
+            copy_4(k, d).start()
+
+    def add_4(k):
+        total = s0[k, cb, xb, zb, yb].astype(jnp.float32)
+        for d in range(1, nz):
+            copy_4(k, d).wait_recv()
+            total = total + r4[k, d - 1].astype(jnp.float32)
+        fin[k, cb, xb] = total.astype(jnp.bfloat16)
+        copy_5(k, True).start()
+
+    def pass_5(k):
+        copy_5(k, False).wait_recv()
+        copy_6(k, True).start()
+
+    def pass_6(k):
+        copy_6(k, False).wait_recv()
+        for q in range(4):
+            store(k, q).start()
+
+    for k in range(chunks):
+        for q in range(4):
+            load(k, q).start()
+    mg_load = pltpu.make_async_copy(mg, mg_own, mg_io)
+    mg_load.start()
+
+    barrier = pltpu.get_barrier_semaphore()
+    partners = [core, side, across, *far[1:]]
+    for partner in partners:
+        pl.semaphore_signal(barrier, inc=1, device_id=partner, device_id_type=MESH)
+    pl.semaphore_wait(barrier, len(partners))
+
+    mg_load.wait()
+    small_1 = remote(mg_own, mg_r1, mg_send.at[0], mg_recv.at[0], core)
+    small_1.start()
+    for k in range(chunks):
+        for q in range(4):
+            load(k, q).wait()
+        copy_1(k).start()
+
+    small_1.wait()
+    mg_own[...] = mg_own[...] + mg_r1[...]
+    small_2 = remote(mg_own, mg_r2, mg_send.at[1], mg_recv.at[1], side)
+    small_2.start()
+    add_1(0)
+    small_2.wait()
+    mg_all[zb, yb] = mg_own[...] + mg_r2[...]
+    small_3 = remote(mg_all.at[zb, yb], mg_all.at[zb, yb], mg_send.at[2], mg_recv.at[2], across)
+    small_3.start()
+    stages = [add_1, add_2, add_3, add_4, pass_5, pass_6]
+    for t in range(1, chunks + len(stages) - 1):
+        for index, stage in enumerate(stages):
+            if 0 <= t - index < chunks:
+                stage(t - index)
+        if t == 1:
+            small_3.wait_send()
+            remote(
+                mg_all.at[zb, 1 - yb], mg_all.at[zb, 1 - yb], mg_send.at[2], mg_recv.at[2], across
+            ).wait_recv()
+            for d in range(1, nz):
+                remote(
+                    mg_all.at[zb], mg_all.at[zb], mz_send.at[d - 1], mz_recv.at[d - 1], far[d]
+                ).start()
+    for d in range(1, nz):
+        back = lax.rem(zb + nz - d, nz)
+        remote(
+            mg_all.at[back], mg_all.at[back], mz_send.at[d - 1], mz_recv.at[d - 1], far[d]
+        ).wait()
+    mg_store = pltpu.make_async_copy(mg_all, o_mg, mg_io)
+    mg_store.start()
+    mg_store.wait()
+    for k in range(chunks):
+        copy_1(k).wait_send()
+        copy_2(k).wait_send()
+        copy_3(k).wait_send()
+        for d in range(1, nz):
+            copy_4(k, d).wait_send()
+        copy_5(k, True).wait_send()
+        copy_6(k, True).wait_send()
+        for q in range(4):
+            store(k, q).wait()
+
+
+def reduce_all(proj, outw, up, down, mg):
+    nb = lax.axis_size("batch")
+    nz = nb // 2
+    rows = proj.shape[0] // nb
+    parts = down.shape[0] // (nb * rows)
+    spans = [("proj", 0, proj.shape[1]), ("out", 0, outw.shape[1]), ("up", 0, up.shape[1])]
+    spans = spans + [("down", part, down.shape[1]) for part in range(parts)]
+    flat = [
+        (name, part, column) for name, part, size in spans for column in range(0, size, CHUNK)
+    ]
+    chunks = len(flat) // 4
+    units = [[flat[q * chunks + k] for q in range(4)] for k in range(chunks)]
+    bf = jnp.bfloat16
+    dma = pltpu.SemaphoreType.DMA
+    many = max(nz - 1, 1)
+    scratch = [
+        pltpu.VMEM((chunks, 2, 2, nz, 2, rows, CHUNK), bf),
+        pltpu.VMEM((chunks, 2, nz, 2, rows, CHUNK), bf),
+        pltpu.VMEM(((chunks + 1) // 2, nz, 2, rows, CHUNK), bf),
+        pltpu.VMEM(((chunks + 1) // 2, 2, nz, rows, CHUNK), bf),
+        pltpu.VMEM((chunks, nz, rows, CHUNK), bf),
+        pltpu.VMEM((chunks, many, rows, CHUNK), bf),
+        pltpu.VMEM((chunks, 2, 2, rows, CHUNK), bf),
+        pltpu.VMEM(mg.shape, jnp.float32),
+        pltpu.VMEM(mg.shape, jnp.float32),
+        pltpu.VMEM(mg.shape, jnp.float32),
+        pltpu.VMEM((nz, 2, *mg.shape), jnp.float32),
+        dma((chunks, 4)),
+        *[dma((chunks,)) for _ in range(6)],
+        dma((chunks, many)),
+        dma((chunks, many)),
+        *[dma((chunks,)) for _ in range(4)],
+        dma((chunks, 4)),
+        dma((3,)),
+        dma((3,)),
+        dma((many,)),
+        dma((many,)),
+        dma,
+    ]
+    any_space = pl.BlockSpec(memory_space=pl.ANY)
+    shape = jax.ShapeDtypeStruct
+    results = pl.pallas_call(
+        partial(reduce_kernel, nb, units),
+        out_shape=(
+            shape((rows, proj.shape[1]), bf),
+            shape((rows, outw.shape[1]), bf),
+            shape((rows, up.shape[1]), bf),
+            shape((parts, rows, down.shape[1]), bf),
+            shape((nz, 2, *mg.shape), jnp.float32),
+        ),
+        in_specs=[any_space] * 5,
+        out_specs=[any_space] * 5,
+        scratch_shapes=scratch,
+        compiler_params=pltpu.CompilerParams(
+            collective_id=0, has_side_effects=True, vmem_limit_bytes=60 << 20
+        ),
+        name="reduce_grads",
+    )(
+        proj.reshape(nz, 2, rows, proj.shape[1]),
+        outw.reshape(nz, 2, rows, outw.shape[1]),
+        up.reshape(nz, 2, rows, up.shape[1]),
+        down.reshape(nz, 2, parts, rows, down.shape[1]),
+        mg,
+    )
+    return results
 
 
 def body(
@@ -301,65 +562,46 @@
         ],
         axis=1,
     )
-    cond_act_grad = jnp.dot(
-        modulation_grad, modulation_weight.astype(jnp.float32).T, precision=highest
-    )
-    cond_grad = silu_back(cond_act_grad)[0]
-    modulation_grad_weight = jnp.dot(
-        cond_low.astype(jnp.float32).T, modulation_grad, precision=highest
-    )
-    class_grad = jnp.dot(class_hot.astype(jnp.float32).T, cond_grad, precision=highest)
-    time_grad = jnp.dot(time_hot.astype(jnp.float32).T, cond_grad, precision=highest)
-    every_share = (
-        lax.psum_scatter(
-            class_grad.astype(jnp.bfloat16), "batch", scatter_dimension=1, tiled=True
-        ).astype(jnp.float32),
-        lax.psum_scatter(
-            time_grad.astype(jnp.bfloat16), "batch", scatter_dimension=1, tiled=True
-        ).astype(jnp.float32),
-        lax.psum_scatter(
-            modulation_grad_weight.astype(jnp.bfloat16), "batch", scatter_dimension=0, tiled=True
-        ).astype(jnp.float32),
-        lax.psum_scatter(
-            project_grad.astype(jnp.bfloat16), "batch", scatter_dimension=0, tiled=True
-        ).astype(jnp.float32),
-        lax.psum_scatter(
-            output_grad.astype(jnp.bfloat16), "batch", scatter_dimension=0, tiled=True
-        ).astype(jnp.float32),
-        lax.psum_scatter(
-            attention_kernel_grad.astype(jnp.bfloat16), "batch", scatter_dimension=1, tiled=True
-        ).astype(jnp.float32),
-        lax.psum_scatter(
-            up_grad.astype(jnp.bfloat16), "batch", scatter_dimension=0, tiled=True
-        ).astype(jnp.float32),
-        lax.psum_scatter(
-            feed_kernel_grad.astype(jnp.bfloat16), "batch", scatter_dimension=1, tiled=True
-        ).astype(jnp.float32),
-        lax.psum_scatter(
-            down_grad.astype(jnp.bfloat16), "batch", scatter_dimension=0, tiled=True
-        ).astype(jnp.float32),
-    )
-    (
-        class_total,
-        time_total,
-        modulation_total,
-        project_total,
-        output_total,
-        attention_kernel_total,
-        up_total,
-        feed_kernel_total,
-        down_total,
-    ) = (
-        lax.psum(every_share[0].astype(jnp.bfloat16), "group").astype(jnp.float32),
-        lax.psum(every_share[1].astype(jnp.bfloat16), "group").astype(jnp.float32),
-        lax.psum(every_share[2].astype(jnp.bfloat16), "group").astype(jnp.float32),
-        lax.psum(every_share[3].astype(jnp.bfloat16), "group").astype(jnp.float32),
-        lax.psum(every_share[4].astype(jnp.bfloat16), "group").astype(jnp.float32),
-        lax.psum(every_share[5].astype(jnp.bfloat16), "group").astype(jnp.float32),
-        lax.psum(every_share[6].astype(jnp.bfloat16), "group").astype(jnp.float32),
-        lax.psum(every_share[7].astype(jnp.bfloat16), "group").astype(jnp.float32),
-        lax.psum(every_share[8].astype(jnp.bfloat16), "group").astype(jnp.float32),
-    )
+    nb = lax.axis_size("batch")
+    members = lax.axis_size("group")
+    place_b = lax.axis_index("batch")
+    named = jnp.stack([class_labels, time_steps], axis=1).astype(jnp.float32)
+    row = jnp.concatenate([modulation_grad, jnp.pad(named, ((0, 0), (0, 510)))], axis=1)
+    bf = jnp.bfloat16
+    project_total, output_total, up_total, down_total, gathered = reduce_all(
+        project_grad.astype(bf), output_grad.astype(bf), up_grad.astype(bf), down_grad.astype(bf),
+        row.reshape(8, row.size // 8),
+    )
+    project_total = project_total.astype(jnp.float32)
+    output_total = output_total.astype(jnp.float32)
+    up_total = up_total.astype(jnp.float32)
+    down_total = down_total.reshape(-1, width).astype(jnp.float32)
+    gathered = gathered.reshape(nb * count, row.shape[1])
+    every_grad = gathered[:, : 6 * width]
+    every_name = (gathered[:, 6 * width : 6 * width + 2] / members).astype(jnp.int32)
+    own = width // nb
+    class_all = (every_name[:, :1] == jnp.arange(class_table.shape[0])[None, :]).astype(bf)
+    time_all = (every_name[:, 1:] == jnp.arange(time_table.shape[0])[None, :]).astype(bf)
+    class_part = lax.dynamic_slice_in_dim(class_table, place_b * own, own, axis=1)
+    time_part = lax.dynamic_slice_in_dim(time_table, place_b * own, own, axis=1)
+    cond_all = jnp.dot(class_all, class_part, preferred_element_type=jnp.float32) + jnp.dot(
+        time_all, time_part, preferred_element_type=jnp.float32
+    )
+    act_all, silu_all = jax.vjp(jax.nn.silu, cond_all)
+    low_all = act_all.astype(bf)
+    modulation_part = lax.dynamic_slice_in_dim(modulation_weight, place_b * own, own, axis=0)
+    cond_act_grad = jnp.dot(every_grad, modulation_part.astype(jnp.float32).T, precision=highest)
+    cond_grad = silu_all(cond_act_grad)[0]
+    modulation_total = jnp.dot(low_all.astype(jnp.float32).T, every_grad, precision=highest)
+    class_total = jnp.dot(class_all.astype(jnp.float32).T, cond_grad, precision=highest)
+    time_total = jnp.dot(time_all.astype(jnp.float32).T, cond_grad, precision=highest)
+    kernel_share = (
+        lax.psum(attention_kernel_grad, ("batch", "group")),
+        lax.psum(feed_kernel_grad, ("batch", "group")),
+    )
+    attention_kernel_total = lax.dynamic_slice_in_dim(kernel_share[0], place_b * own, own, axis=1)
+    wide = feed_kernel_grad.shape[1] // nb
+    feed_kernel_total = lax.dynamic_slice_in_dim(kernel_share[1], place_b * wide, wide, axis=1)
     return (
         result,
         inputs_gradient,

time: 1130 us -> 627 us (0.55)
  waiting for transfers between devices: 728 us -> 144 us
  Pallas kernels: 0 us -> 92.6 us
  blocking collectives: 57.8 us -> 42 us
  starting transfers between devices: 24.9 us -> 36.8 us
    reduce_scatter x7 -> x0, waiting for transfers between devices: 531 us -> none  [the longest x1 133 us: body(): lax.psum_scatter(modulation_grad_weight.astype(jnp.bfloat16), 'batch', sc...]
    unnamed x12 -> x1, waiting for transfers between devices: 130 us -> 0.02 us
    pallas_call x0 -> x1, Pallas kernels: none -> 92.6 us  [reduce_all(): pl.pallas_call(partial(reduce_kernel, nb, units), out_shape=(shape((rows,...]
    psum x1, waiting for transfers between devices: 54 us -> 112 us  [body(): lax.psum(feed_kernel_grad, ('batch', 'group'))]
    all_to_all x3 -> x0, blocking collectives: 46.4 us -> none  [the longest x1 18.3 us: body(): lax.all_to_all(to_groups(returned_grad), 'group', split_axis=1, concat_ax...]
    psum x1, blocking collectives: 11.4 us -> 42 us  [body(): lax.psum(attention_kernel_grad, ('batch', 'group'))]
    all_to_all x0 -> x3, waiting for transfers between devices: none -> 17.7 us  [the longest x1 9.04 us: body(): lax.all_to_all(branch.reshape(count, 4, height // 2, half, width), 'group...]
    all_to_all x0 -> x3, starting transfers between devices: none -> 12.7 us  [the longest x1 4.36 us: body(): lax.all_to_all(to_groups(returned_grad), 'group', split_axis=1, concat_ax...]
  transfers between devices with their start and end apart: 19 -> 13, of which waited for: 13 -> 8; matrix products, arithmetic and copies ran while one was open for 9% -> 6% of each run, Pallas kernels for 0% -> 0%
where the time goes in v1:
time: 627 us; the launch traced here: 620 us
  waiting for transfers between devices  144 us (23%)
  matrix products  121 us (19%)
  other arithmetic  93.9 us (15%)
  Pallas kernels  92.6 us (15%)
  local copies, waits for them, and re-layouts  73.6 us (12%)
  blocking collectives  42 us (7%)
  starting transfers between devices  36.8 us (6%)
  between operations  15.7 us (3%)
    psum x1, waiting for transfers between devices, body(): lax.psum(feed_kernel_grad, ('batch', 'group'))  112 us
    pallas_call x1, Pallas kernels, reduce_all(): pl.pallas_call(partial(reduce_kernel, nb, units), out_shape=(shape((rows,...  92.6 us
    psum x1, blocking collectives, body(): lax.psum(attention_kernel_grad, ('batch', 'group'))  42 us
    dot_general x1, matrix products, body(): jnp.einsum('crsd,fd->crsf', branch_two_grad, down_weight, preferred_eleme...  37.1 us
    convert_element_type x1, other arithmetic, body(): depthwise_back(padded_spread, kernel_feed, height, across)  25.1 us
    convert_element_type x1, other arithmetic, body(): activated_low = activated.astype(jnp.bfloat16)  22.4 us
    ppermute x4, starting transfers between devices, padded_2(): lax.ppermute(lax.slice_in_dim(block, block.shape[dim] - width, None, axis...  13.9 us
  transfers between devices with their start and end apart: 13, of which 8 were waited for; matrix products, arithmetic and copies ran while one was open for 6% of the time, Pallas kernels for 0%

profile of v1, /device:TPU:0, one launch (start us, length us, event | category | flops | bytes accessed | tf_op | source)
XLA Modules:
  0.0 619.6 jit_solution(15071023648485361714)
XLA Ops:
  9.1 5.6 fusion.123
  21.1 2.4 collective-permute-start
  25.0 3.8 collective-permute-done.1
  30.6 2.4 add_convert_fusion.4
  33.0 2.8 reshape.311
  38.0 4.7 all-to-all-start
  49.8 4.6 all-to-all-done
  56.4 3.4 convolution_convert_fusion
  59.9 4.3 copy.63
  64.1 2.6 fusion.28
  69.4 2.8 convolution_convert_fusion.3
  74.1 4.2 all-to-all-start.1
  80.9 9.0 %all-to-all-done.1 = bf16[2,4,4,16,768]{4,3,2,0,1:T(8,128)(2,1)} async-done(((bf16[2,4,4,16,768]{4,3,2,0,1:T(8,128)(2,1)}), bf16[2,4,4,16,768]{4,3,2,0,1:T(8,128)(2,1)}, u32[]{:S(2)}, u32[]{:S(2)}) %all-to-all-start.1) | async-done | bytes 786464 | tf_op jit(solution)/shard_map/all_to_all | solution.py:468
  90.0 3.1 copy.110
  93.0 3.1 reshape.340
  99.2 5.3 fusion.37
  107.8 2.4 collective-permute-done.3
  112.0 22.4 %multiply_convert_fusion.1 = (bf16[2,8,32,3072]{3,2,1,0:T(8,128)(2,1)}, f32[2,8,32,3072]{3,2,1,0:T(8,128)}, f32[2,8,32,3072]{3,2,1,0:T(8,128)}) fusion(f32[2,10,34,3072]{3,2,1,0:T(8,128)S(1)} %fusion.26, f32[3072]{0:T(1024)S(1)} %bitcast.211, f32[3072]{0:T(1024)S(1)} %bitcast.213, f32[3072]{0:T(1024)S(1)} %bitcast.199, f32[3072]{0:T(1024)S(1)} %bitcast.201, ...), kind=kLoop, calls=%fused_computation.47 | loop fusion | flops 128974848 | bytes 72462336 | tf_op jit(solution)/shard_map/convert_element_type | solution.py:483
  134.4 37.1 %fusion.10 = (f32[3072]{0:T(1024)}, f32[3072]{0:T(1024)}, f32[3072]{0:T(1024)}, f32[3072]{0:T(1024)}, f32[3072]{0:T(1024)}, /*index=5*/f32[3072]{0:T(1024)}, f32...) fusion(f32[2,10,34,3072]{3,2,1,0:T(8,128)} %copy-done.1, ...), kind=kOutput, calls=%fused_computation.25 | convolution fusion | flops 2468975616 | bytes 77973504 | tf_op jit(solution)/shard_map/crsd,fd->crsf/dot_general | solution.py:492
  171.6 3.0 stack.105
  176.6 8.6 %collective-permute-start.4 = (bf16[2,1,32,3072]{3,2,1,0:T(8,128)(2,1)}, bf16[2,1,32,3072]{3,2,1,0:T(8,128)(2,1)}, u32[]{:S(2)}, u32[]{:S(2)}) collective-permute-start(bf16[2,1,32,3072]{3,2,1,0:T(8,128)(2,1)} %get-tuple-element.110), channel_id=1, source_target_pairs={{0,1},{1,2},{2,3},{4,5},{5,6},{6,7},{8,9},{9,10},{10,11},{12,13},{... | collective-permute-start | bytes 1179656 | tf_op jit(solution)/shard_map/ppermute | solution.py:21
  186.5 6.9 %bitcast_convert_fusion = bf16[3072,768]{1,0:T(8,128)(2,1)} fusion(bf16[2,8,32,3072]{3,2,1,0:T(8,128)(2,1)} %get-tuple-element.105, bf16[2,8,32,768]{3,2,1,0:T(8,128)(2,1)} %param.27, f32[2,768]{1,0:T(2,128)} %get-tuple-element.129), kind=kOutput, calls=%fused_computation.13 | convolution fusion | flops 2419458048 | bytes 8656896 | tf_op jit(solution)/shard_map/crsf,crsd->fd/dot_general | solution.py:489
  193.4 111.9 %all-reduce.7.cloned.1.call-done = f32[9,3072]{1,0:T(8,128)} async-done(((f32[9,3072]{1,0:T(8,128)}), f32[9,3072]{1,0:T(8,128)}) %all-reduce.7.cloned.1.call-update) | async-done | bytes 110608 | tf_op jit(solution)/shard_map/psum | solution.py:600
  306.7 6.9 %fusion.25 = f32[2,10,34,3072]{3,2,1,0:T(8,128)} fusion(bf16[2,1,32,3072]{3,2,1,0:T(8,128)(2,1)} %collective-permute-done.5, bf16[2,8,32,3072]{3,2,1,0:T(8,128)(2,1)} %get-tuple-element.142, bf16[2,1,32,3072]{3,2,1,0:T(8,128)(2,1)} %collective-permute-done.4), kind=kLoop, calls=%fused_computation.66 | loop fusion | flops 25067520 | bytes 12288000 | tf_op jit(solution)/shard_map/convert_element_type | solution.py:496
  313.6 25.1 %fusion.12 = bf16[2,8,32,3072]{3,2,1,0:T(8,128)(2,1)S(1)} fusion(f32[2,10,34,3072]{3,2,1,0:T(8,128)} %fusion.25, f32[3072]{0:T(1024)} %bitcast.212, f32[3072]{0:T(1024)} %bitcast.214, f32[3072]{0:T(1024)S(1)} %bitcast.200, f32[3072]{0:T(1024)S(1)} %bitcast.202, f32[3072]{0:T(1024)S(1)} %bitcast.204, f32[3072]{0:T(1024)} %bitcast.206, f32[3072]{0:T(1024)} %bitcast.208, ...), kind=kLoop, calls=%fused_computation.28 | loop fusion | flops 28311552 | bytes 59879424 | tf_op jit(solution)/shard_map/convert_element_type | solution.py:498
  338.8 7.1 %multiply_reduce_fusion.1 = (f32[2,768]{1,0:T(2,128)}, f32[2,8,32]{2,1,0:T(8,128)S(1)}, f32[2,768]{1,0:T(2,128)}, f32[2,8,32,768]{3,2,1,0:T(8,128)S(1)}) fusion(f32[2,8,32,768]{3,2,1,0:T(8,128)S(1)} %copy-done.6, f32[2,8,32]{2,1,0:T(8,128)} %copy-done.77, f32[2,8,32]{2,1,0:T(8,128)} %copy-done.49, f32[2,768]{1,0:T(2,128)} %copy-done.80, ...), kind=kOutput, calls=%fused_computation.149 | convolution fusion | flops 2419061248 | bytes 11034624 | tf_op jit(solution)/shard_map/crsf,df->crsd/dot_general | solution.py:500
  348.9 2.8 reshape.319
  353.9 4.4 all-to-all-start.2
  358.2 7.4 %bitcast_convert_fusion.1 = bf16[768,3072]{1,0:T(8,128)(2,1)} fusion(bf16[2,8,32,3072]{3,2,1,0:T(8,128)(2,1)} %copy-done.12, f32[2,8,32,768]{3,2,1,0:T(8,128)} %copy-done.5, f32[2,768]{1,0:T(2,128)} %get-tuple-element.130, f32[2,768]{1,0:T(2,128)} %copy-done.80, f32[2,8,32]{2,1,0:T(8,128)S(1)} %copy-done.78, f32[2,8,32]{2,1,0:T(8,128)S(1)} %copy-done.50), kind=kOutput, calls=%fused_computation.14 | convolution fusion | flops 2420244480 | bytes 9453568 | tf_op jit(solution)/shard_map/crsd,crsf->df/dot_general | solution.py:499
  365.7 4.1 all-to-all-done.2
  371.8 3.0 convolution_convert_fusion.1
  374.8 2.3 copy.75
  377.1 7.9 %multiply_reduce_fusion = (f32[2,12,256]{2,1,0:T(8,128)S(1)}, f32[2,12,256,256]{2,3,1,0:T(8,128)}) fusion(f32[2,12,256,256]{2,3,1,0:T(8,128)} %copy-done.3, f32[2,12,256]{2,1,0:T(8,128)} %copy-done.28, pred[2,256,256]{1,2,0:T(8,128)(4,1)} %broadcast_compare_fusion, bf16[2,256,12,64]{1,3,2,0:T(8,128)(2,1)} %bitcast.182, ...), kind=kOutput, calls=%fused_computation.45 | convolution fusion | flops 209184768 | bytes 14344192 | tf_op jit(solution)/shard_map/while/body/eval_jaxpr/blhe,bmhe->bhlm/dot_general | solution.py:122
  385.1 4.8 multiply_convert_fusion
  397.0 4.2 all-to-all-start.3
  401.2 3.3 bitcast_convert_fusion.3
  404.5 3.8 bitcast_convert_fusion.2
  408.3 4.5 all-to-all-done.3
  412.9 2.8 copy.83
  415.7 3.0 reshape.324
  418.6 8.0 %fusion.68 = (f32[768]{0:T(1024)S(1)}, f32[768]{0:T(1024)S(1)}, f32[768]{0:T(1024)S(1)}, f32[768]{0:T(1024)S(1)}, f32[768]{0:T(1024)S(1)}, /*index=5*/f32[768]{0...) fusion(bf16[2,8,32,768]{3,2,1,0:T(8,128)(2,1)} %reshape.324, f32[2,10,34,768]{3,2,1,0:T(8,128)} %copy-done.2), kind=kLoop, calls=%fused_computation.130 | loop fusion | flops 7464192 | bytes 14969856 | tf_op jit(solution)/shard_map/reduce_sum | solution.py:75
  433.6 2.7 stack.95
  436.3 42.0 %psum.14 = f32[9,768]{1,0:T(8,128)} all-reduce(f32[9,768]{1,0:T(8,128)} %stack.95), channel_id=1, replica_groups=mesh['batch'=8,'group'=4] {'batch','group'}, use_global_device_ids=true, to_apply=%region_26.27 | all-reduce | flops 6912 | bytes 55296 | tf_op jit(solution)/shard_map/psum | solution.py:599
  482.4 3.2 collective-permute-done.7
  487.3 2.5 fusion.57
  491.4 6.7 %fusion.59 = (f32[2,768]{1,0:T(2,128)S(1)}, f32[2,768]{1,0:T(2,128)S(1)}, bf16[2,8,32,768]{3,2,1,0:T(8,128)(2,1)}, bf16[2,8,32,768]{3,2,1,0:T(8,128)(2,1)}) fusion(bf16[2,8,32,768]{3,2,1,0:T(8,128)(2,1)S(1)} %copy-done.24, f32[2,8,32,768]{3,2,1,0:T(8,128)S(1)} %copy-done.9, f32[2,8,32,768]{3,2,1,0:T(8,128)S(1)} %copy-done.11, ...), kind=kOutput, calls=%fused_computation.121 | convolution fusion | flops 2423780352 | bytes 17336320 | tf_op jit(solution)/shard_map/dot_general | solution.py:484
  503.2 92.6 %reduce_grads.1 = (bf16[96,2304]{1,0:T(8,128)(2,1)}, bf16[96,768]{1,0:T(8,128)(2,1)}, bf16[96,3072]{1,0:T(8,128)(2,1)}, bf16[4,96,768]{2,1,0:T(8,128)(2,1)}, f32[4,2,8,1280]{3,2,1,0:T(8,128)}) custom-call(bf16[4,2,96,2304]{3,2,1,0:T(8,128)(2,1)} %bitcast.181, bf16[4,2,96,768]{3,2,1,0:T(8,128)(2,1)} %bitcast.190, bf16[4,2,96,3072]{3,2,1,0:T(8,128)(2,1)} %bitcast.180, ...), custom_call_target="tpu_custom_call" | custom-call | tf_op jit(solution)/shard_map/reduce_grads/pallas_call | solution.py:374
  601.1 3.1 fusion.92
  (281 shorter events, 89.2 us)
Async XLA Ops:
  7.2 49.3 %copy-start = (bf16[768,2304]{1,0:T(8,128)(2,1)S(1)}, bf16[768,2304]{1,0:T(8,128)(2,1)}, u32[]{:S(2)}) copy-start(bf16[768,2304]{1,0:T(8,128)(2,1)} %param.21) | copy-start | bytes 10616836
  14.7 10.1 %copy-start.79 = (bf16[9,768]{1,0:T(8,128)(2,1)S(1)}, bf16[9,768]{1,0:T(8,128)(2,1)}, u32[]{:S(2)}) copy-start(bf16[9,768]{1,0:T(8,128)(2,1)} %param.23) | copy-start | bytes 41476
  16.1 8.9 %copy-start.45 = (f32[2,768]{1,0:T(2,128)}, f32[2,768]{1,0:T(2,128)S(1)}, u32[]{:S(2)}) copy-start(f32[2,768]{1,0:T(2,128)S(1)} %get-tuple-element.133) | copy-start | bytes 18436
  16.1 80.1 %copy-start.55 = (f32[2,768]{1,0:T(2,128)}, f32[2,768]{1,0:T(2,128)S(1)}, u32[]{:S(2)}) copy-start(f32[2,768]{1,0:T(2,128)S(1)} %get-tuple-element.134) | copy-start | bytes 18436
  16.1 83.1 %copy-start.80 = (f32[2,768]{1,0:T(2,128)}, f32[2,768]{1,0:T(2,128)S(1)}, u32[]{:S(2)}) copy-start(f32[2,768]{1,0:T(2,128)S(1)} %get-tuple-element.131) | copy-start | bytes 18436
  17.5 7.6 %copy-start.30 = (f32[2,8,32]{2,1,0:T(8,128)}, f32[2,8,32]{2,1,0:T(8,128)S(1)}, u32[]{:S(2)}) copy-start(f32[2,8,32]{2,1,0:T(8,128)S(1)} %broadcast_multiply_fusion.1) | copy-start | bytes 6148
  21.1 3.9 collective-permute-start
  23.5 5.3 collective-permute-start.1
  38.0 16.4 %all-to-all-start = ((bf16[2,4,4,16,768]{4,3,2,0,1:T(8,128)(2,1)}), bf16[2,4,4,16,768]{4,3,2,0,1:T(8,128)(2,1)}, u32[]{:S(2)}, u32[]{:S(2)}) async-start(bf16[2,4,4,16,768]{4,3,2,0,1:T(8,128)(2,1)} %bitcast.184), calls=%async_computation | async-start | bytes 1572864 | tf_op jit(solution)/shard_map/all_to_all | solution.py:443
  74.1 15.9 %all-to-all-start.1 = ((bf16[2,4,4,16,768]{4,3,2,0,1:T(8,128)(2,1)}), bf16[2,4,4,16,768]{4,3,2,0,1:T(8,128)(2,1)}, u32[]{:S(2)}, u32[]{:S(2)}) async-start(bf16[2,4,4,16,768]{4,3,2,0,1:T(8,128)(2,1)} %copy.70), calls=%async_computation.1 | async-start | bytes 1572864 | tf_op jit(solution)/shard_map/all_to_all | solution.py:468
  78.3 227.1 %all-reduce.7.cloned.1.call-start = ((), (), s32[]{:S(2)}) async-start(), calls=%async_computation.4 | async-start | bytes 393216 | tf_op jit(solution)/shard_map/psum | solution.py:600
  99.2 8.4 %copy-start.33 = (bf16[9,3072]{1,0:T(8,128)(2,1)S(1)}, bf16[9,3072]{1,0:T(8,128)(2,1)}, u32[]{:S(2)}) copy-start(bf16[9,3072]{1,0:T(8,128)(2,1)} %param.25) | copy-start | bytes 165892
  104.6 3.2 collective-permute-start.2
  106.1 4.1 collective-permute-start.3
  111.9 22.5 %copy-start.1 = (f32[2,10,34,3072]{3,2,1,0:T(8,128)}, f32[2,10,34,3072]{3,2,1,0:T(8,128)S(1)}, u32[]{:S(2)}) copy-start(f32[2,10,34,3072]{3,2,1,0:T(8,128)S(1)} %fusion.26) | copy-start | bytes 25067524
  112.0 22.4 %copy-start.22 = (bf16[2,8,32,768]{3,2,1,0:T(8,128)(2,1)S(1)}, bf16[2,8,32,768]{3,2,1,0:T(8,128)(2,1)}, u32[]{:S(2)}) copy-start(bf16[2,8,32,768]{3,2,1,0:T(8,128)(2,1)} %param.27) | copy-start | bytes 2359300
  112.0 22.4 %copy-start.82 = (f32[2,768]{1,0:T(2,128)S(1)}, f32[2,768]{1,0:T(2,128)}, u32[]{:S(2)}) copy-start(f32[2,768]{1,0:T(2,128)} %get-tuple-element.129) | copy-start | bytes 18436
  176.6 130.1 %collective-permute-start.4 = (bf16[2,1,32,3072]{3,2,1,0:T(8,128)(2,1)}, bf16[2,1,32,3072]{3,2,1,0:T(8,128)(2,1)}, u32[]{:S(2)}, u32[]{:S(2)}) collective-permute-start(bf16[2,1,32,3072]{3,2,1,0:T(8,128)(2,1)} %get-tuple-element.110), channel_id=1, source_target_pairs={{0,1},{1,2},{2,3},{4,5},{5,6},{6,7},{8,9},{9,10},{10,11},{12,13},{... | collective-permute-start | bytes 1179656 | tf_op jit(solution)/shard_map/ppermute | solution.py:21
  185.2 121.5 %collective-permute-start.5 = (bf16[2,1,32,3072]{3,2,1,0:T(8,128)(2,1)}, bf16[2,1,32,3072]{3,2,1,0:T(8,128)(2,1)}, u32[]{:S(2)}, u32[]{:S(2)}) collective-permute-start(bf16[2,1,32,3072]{3,2,1,0:T(8,128)(2,1)} %get-tuple-element.111), channel_id=1, source_target_pairs={{1,0},{2,1},{3,2},{5,4},{6,5},{7,6},{9,8},{10,9},{11,10},{13,12},{... | collective-permute-start | bytes 1179656 | tf_op jit(solution)/shard_map/ppermute | solution.py:24
  313.6 25.1 %copy-start.6 = (f32[2,8,32,768]{3,2,1,0:T(8,128)S(1)}, f32[2,8,32,768]{3,2,1,0:T(8,128)}, u32[]{:S(2)}) copy-start(f32[2,8,32,768]{3,2,1,0:T(8,128)} %copy-done.5) | copy-start | bytes 4718596
  338.8 7.2 %copy-start.50 = (f32[2,8,32]{2,1,0:T(8,128)S(1)}, f32[2,8,32]{2,1,0:T(8,128)}, u32[]{:S(2)}) copy-start(f32[2,8,32]{2,1,0:T(8,128)} %copy-done.49) | copy-start | bytes 6148
  338.8 7.2 %copy-start.78 = (f32[2,8,32]{2,1,0:T(8,128)S(1)}, f32[2,8,32]{2,1,0:T(8,128)}, u32[]{:S(2)}) copy-start(f32[2,8,32]{2,1,0:T(8,128)} %copy-done.77) | copy-start | bytes 6148
  353.9 15.9 %all-to-all-start.2 = ((bf16[2,4,4,16,768]{4,3,2,0,1:T(8,128)(2,1)}), bf16[2,4,4,16,768]{4,3,2,0,1:T(8,128)(2,1)}, u32[]{:S(2)}, u32[]{:S(2)}) async-start(bf16[2,4,4,16,768]{4,3,2,0,1:T(8,128)(2,1)} %bitcast.185), calls=%async_computation.2 | async-start | bytes 1572864 | tf_op jit(solution)/shard_map/all_to_all | solution.py:508
  377.1 7.9 %slice-start = ((s8[6291456]{0:T(1024)(128)(4,1)}), s8[4194304]{0:T(1024)(128)(4,1)S(1)}, s32[]{:S(2)}) async-start(s8[6291456]{0:T(1024)(128)(4,1)} %bitcast.171), calls=%async_computation.5 | async-start | bytes 8388608
  377.1 7.9 %slice-start.1 = ((s8[6291456]{0:T(1024)(128)(4,1)}), s8[2097152]{0:T(1024)(128)(4,1)S(1)}, s32[]{:S(2)}) async-start(s8[6291456]{0:T(1024)(128)(4,1)} %bitcast.171), calls=%async_computation.6 | async-start | bytes 4194304
  377.1 7.9 %copy-start.18 = (pred[2,256,256]{1,2,0:T(8,128)(4,1)S(1)}, pred[2,256,256]{1,2,0:T(8,128)(4,1)}, u32[]{:S(2)}) copy-start(pred[2,256,256]{1,2,0:T(8,128)(4,1)} %broadcast_compare_fusion) | copy-start | bytes 393220
  377.1 7.9 %copy-start.29 = (f32[2,12,256]{2,1,0:T(8,128)S(1)}, f32[2,12,256]{2,1,0:T(8,128)}, u32[]{:S(2)}) copy-start(f32[2,12,256]{2,1,0:T(8,128)} %copy-done.28) | copy-start | bytes 73732
  397.0 15.9 %all-to-all-start.3 = ((bf16[2,4,4,16,768]{4,3,2,0,1:T(8,128)(2,1)}), bf16[2,4,4,16,768]{4,3,2,0,1:T(8,128)(2,1)}, u32[]{:S(2)}, u32[]{:S(2)}) async-start(bf16[2,4,4,16,768]{4,3,2,0,1:T(8,128)(2,1)} %copy.81), calls=%async_computation.3 | async-start | bytes 1572864 | tf_op jit(solution)/shard_map/all_to_all | solution.py:540
  426.6 60.5 %copy-start.31 = (f32[2,8,32]{2,1,0:T(8,128)S(1)}, f32[2,8,32]{2,1,0:T(8,128)}, u32[]{:S(2)}) copy-start(f32[2,8,32]{2,1,0:T(8,128)} %copy-done.30) | copy-start | bytes 6148
  426.6 60.5 %copy-start.46 = (f32[2,768]{1,0:T(2,128)S(1)}, f32[2,768]{1,0:T(2,128)}, u32[]{:S(2)}) copy-start(f32[2,768]{1,0:T(2,128)} %copy-done.45) | copy-start | bytes 18436
  478.2 8.9 %copy-start.4 = (bf16[2,8,32,768]{3,2,1,0:T(8,128)(2,1)S(1)}, bf16[2,8,32,768]{3,2,1,0:T(8,128)(2,1)}, u32[]{:S(2)}) copy-start(bf16[2,8,32,768]{3,2,1,0:T(8,128)(2,1)} %param.14) | copy-start | bytes 2359300
  478.2 8.9 %copy-start.58 = (f32[768]{0:T(1024)S(1)}, f32[768]{0:T(1024)}, u32[]{:S(2)}) copy-start(f32[768]{0:T(1024)} %copy-done.57) | copy-start | bytes 9220
  478.2 8.9 %copy-start.60 = (f32[768]{0:T(1024)S(1)}, f32[768]{0:T(1024)}, u32[]{:S(2)}) copy-start(f32[768]{0:T(1024)} %copy-done.59) | copy-start | bytes 9220
  478.2 8.9 %copy-start.62 = (f32[768]{0:T(1024)S(1)}, f32[768]{0:T(1024)}, u32[]{:S(2)}) copy-start(f32[768]{0:T(1024)} %copy-done.61) | copy-start | bytes 9220
  478.2 8.9 %copy-start.64 = (f32[768]{0:T(1024)S(1)}, f32[768]{0:T(1024)}, u32[]{:S(2)}) copy-start(f32[768]{0:T(1024)} %copy-done.63) | copy-start | bytes 9220
  478.2 8.9 %copy-start.66 = (f32[768]{0:T(1024)S(1)}, f32[768]{0:T(1024)}, u32[]{:S(2)}) copy-start(f32[768]{0:T(1024)} %copy-done.65) | copy-start | bytes 9220
  478.2 8.9 %copy-start.68 = (f32[768]{0:T(1024)S(1)}, f32[768]{0:T(1024)}, u32[]{:S(2)}) copy-start(f32[768]{0:T(1024)} %copy-done.67) | copy-start | bytes 9220
  478.3 8.9 %copy-start.70 = (f32[768]{0:T(1024)S(1)}, f32[768]{0:T(1024)}, u32[]{:S(2)}) copy-start(f32[768]{0:T(1024)} %copy-done.69) | copy-start | bytes 9220
  478.3 8.9 %copy-start.72 = (f32[768]{0:T(1024)S(1)}, f32[768]{0:T(1024)}, u32[]{:S(2)}) copy-start(f32[768]{0:T(1024)} %copy-done.71) | copy-start | bytes 9220
  478.3 8.9 %copy-start.74 = (f32[768]{0:T(1024)S(1)}, f32[768]{0:T(1024)}, u32[]{:S(2)}) copy-start(f32[768]{0:T(1024)} %copy-done.73) | copy-start | bytes 9220
  478.3 4.1 collective-permute-start.6
  479.7 5.9 collective-permute-start.7
  491.4 8.0 %copy-start.86 = (f32[2,768]{1,0:T(2,128)S(1)}, f32[2,768]{1,0:T(2,128)}, u32[]{:S(2)}) copy-start(f32[2,768]{1,0:T(2,128)} %get-tuple-element.88) | copy-start | bytes 18436
  491.4 8.6 %copy-start.85 = (f32[2,768]{1,0:T(2,128)S(1)}, f32[2,768]{1,0:T(2,128)}, u32[]{:S(2)}) copy-start(f32[2,768]{1,0:T(2,128)} %get-tuple-element.84) | copy-start | bytes 18436
  491.4 9.7 %copy-start.87 = (f32[2,2]{1,0:T(2,128)S(1)}, f32[2,2]{1,0:T(2,128)}, u32[]{:S(2)}) copy-start(f32[2,2]{1,0:T(2,128)} %copy.107) | copy-start | bytes 52
  598.4 10.1 %copy-start.26 = (bf16[4,96,768]{2,1,0:T(8,128)(2,1)S(1)}, bf16[4,96,768]{2,1,0:T(8,128)(2,1)}, u32[]{:S(2)}) copy-start(bf16[4,96,768]{2,1,0:T(8,128)(2,1)} %get-tuple-element.65) | copy-start | bytes 1769476
  598.4 11.3 %copy-start.25 = (bf16[96,3072]{1,0:T(8,128)(2,1)S(1)}, bf16[96,3072]{1,0:T(8,128)(2,1)}, u32[]{:S(2)}) copy-start(bf16[96,3072]{1,0:T(8,128)(2,1)} %get-tuple-element.64) | copy-start | bytes 1769476
  604.2 7.6 %copy-start.32 = (bf16[96,768]{1,0:T(8,128)(2,1)S(1)}, bf16[96,768]{1,0:T(8,128)(2,1)}, u32[]{:S(2)}) copy-start(bf16[96,768]{1,0:T(8,128)(2,1)} %get-tuple-element.63) | copy-start | bytes 442372
  (57 other events, 214.2 us)
Sparse Core Ops, SparseCore 0:
  174.7 130.6 all-reduce.6

commit v2 on v1

v2 whole, which is shorter than its diff:
```python
from functools import partial

import jax
import jax.numpy as jnp
from jax import lax
from jax.experimental import pallas as pl
from jax.experimental.pallas import tpu as pltpu
from jax.sharding import PartitionSpec as P

HEADS = 12
MESH = pl.DeviceIdType.MESH
LANES = 128
CHUNK = 384
TILE = 512
f32 = jnp.float32
bf16 = jnp.bfloat16
highest = lax.Precision.HIGHEST


def dot_nn(a, b):
    return lax.dot_general(a, b, (((1,), (0,)), ((), ())), preferred_element_type=f32)


def dot_nt(a, b):
    return lax.dot_general(a, b, (((1,), (1,)), ((), ())), preferred_element_type=f32)


def dot_tn(a, b):
    return lax.dot_general(a, b, (((0,), (0,)), ((), ())), preferred_element_type=f32)


def remote(src, dst, send, recv, target):
    return pltpu.make_async_remote_copy(
        src_ref=src, dst_ref=dst, send_sem=send, recv_sem=recv, device_id=target,
        device_id_type=MESH,
    )


def meet(partners):
    barrier = pltpu.get_barrier_semaphore()
    for partner in partners:
        pl.semaphore_signal(barrier, inc=1, device_id=partner, device_id_type=MESH)
    pl.semaphore_wait(barrier, len(partners))


def normalize(values):
    center = values - jnp.mean(values, axis=-1, keepdims=True)
    second = jnp.mean(center * center, axis=-1, keepdims=True)
    scale = lax.rsqrt(second + 1e-06)
    return center * scale, scale


def normalize_back(grad, normal, scale):
    return scale * (
        grad
        - jnp.mean(grad, axis=-1, keepdims=True)
        - normal * jnp.mean(grad * normal, axis=-1, keepdims=True)
    )


def column_shifts(row):
    across = row.shape[0]
    column = lax.broadcasted_iota(jnp.int32, row.shape, 0)
    before = jnp.where(column == 0, 0.0, pltpu.roll(row, 1, 0))
    after = jnp.where(column == across - 1, 0.0, pltpu.roll(row, across - 1, 0))
    return before, after


def fold(values):
    rows, width = values.shape
    return jnp.sum(values.reshape(rows // 8, 8, width), axis=0)


def permutation(inverse):
    n = 512
    to = lax.broadcasted_iota(jnp.int32, (n, n), 1 if inverse else 0)
    source = lax.broadcasted_iota(jnp.int32, (n, n), 0 if inverse else 1)
    wanted = lax.shift_left(lax.shift_right_logical(to & 255, 4), 5) + 2 * (to & 15) + (
        lax.shift_right_logical(to, 8)
    )
    return jnp.where(source == wanted, 1.0, 0.0).astype(bf16)


def mask_bias(row, column):
    return jnp.where(row == column, 0.0, -1e30)


def front_kernel(
    x_in, cot_in, mod, kern, wqkv_in, wo_in, lab_row, lab_col,
    o_x, o_cot, o_ret, o_tok, o_proj, o_att, o_lse,
    xf, wqkv, wo, shifts, mixed, rows_m, perm, bias, tok, proj, att, lse, brm,
    load_sem, x_send, x_recv, c_send, c_recv, ex_send, ex_recv, own_sem, out_sem,
):
    b = lax.axis_index("batch")
    g = lax.axis_index("group")
    c, p = lax.rem(g, 2), g // 2
    core, side, corner = (b, g + 1 - 2 * c), (b, g + 2 - 4 * p), (b, 3 - g)
    inner = jnp.logical_or(g == 1, g == 2)
    width = xf.shape[-1]
    across = xf.shape[1]

    def spread_out(src, dst, send, recv, waiting):
        main = c * 8 + p * 2
        other_main = remote(
            src.at[1 - p], dst.at[pl.ds(main, 8)], send.at[0], recv.at[c], (b, 2 - p)
        )
        edge = 6 * (2 - g)
        edge_to = 16 * (g - 1)
        other_edge = remote(
            src.at[1 - p, pl.ds(edge, 2)], dst.at[pl.ds(edge_to, 2)], send.at[1], recv.at[2], side
        )
        own_main = remote(src.at[p], dst.at[pl.ds(main, 8)], send.at[2], recv.at[c], core)
        own_edge = pltpu.make_async_copy(
            src.at[p, pl.ds(edge, 2)], dst.at[pl.ds(edge_to, 2)], recv.at[2]
        )
        stay_main = pltpu.make_async_copy(src.at[p], dst.at[pl.ds(main, 8)], recv.at[c])
        if waiting:
            other_main.wait_send()

            @pl.when(inner)
            def _():
                other_edge.wait_send()
                own_main.wait_send()

        else:
            other_main.start()

            @pl.when(inner)
            def _():
                other_edge.start()
                own_main.start()
                own_edge.start()

            @pl.when(jnp.logical_not(inner))
            def _():
                stay_main.start()

    def arrived(dst, recv):
        for j in range(2):
            place = dst.at[pl.ds(8 * j + 2 * c, 8)]
            pltpu.make_async_copy(place, place, recv.at[j]).wait()
        place = dst.at[pl.ds(16 * (1 - c), 2)]
        pltpu.make_async_copy(place, place, recv.at[2]).wait()

    loads = [
        pltpu.make_async_copy(wqkv_in, wqkv, load_sem.at[0]),
        pltpu.make_async_copy(wo_in, wo, load_sem.at[1]),
    ]
    for load in loads:
        load.start()
    meet([core, side, corner])
    spread_out(x_in, xf, x_send, x_recv, False)
    perm[0] = permutation(False)
    perm[1] = permutation(True)
    for half in range(2):
        bias[half] = mask_bias(lab_row[half], lab_col[half])
    arrived(xf, x_recv)
    spread_out(cot_in, o_cot, c_send, c_recv, False)
    x_out = pltpu.make_async_copy(xf, o_x, out_sem.at[0])
    x_out.start()

    shift = mod[0:1, :]
    scale = 1.0 + mod[1:2, :]

    def first(i, carry):
        normal, _ = normalize(xf[c + i].astype(f32))
        value = (normal * scale + shift).astype(bf16).astype(f32)
        before, after = column_shifts(value)
        shifts[0, 1 - c + i] = before
        shifts[1, 1 - c + i] = value
        shifts[2, 1 - c + i] = after
        return carry

    lax.fori_loop(0, 17, first, 0)
    for s in range(3):
        shifts[s, 17 * c] = jnp.zeros((across, width), f32)

    def conv(step, parity):
        o = 2 * step + parity
        for lane in range(0, width, LANES):
            cut = slice(lane, lane + LANES)
            total = jnp.zeros((across, LANES), f32)
            for r in range(3):
                for s in range(3):
                    tap = kern[3 * r + s : 3 * r + s + 1, cut].astype(f32)
                    total = total + tap * shifts[s, o + r, :, cut]
            mixed[step, parity, :, cut] = total.astype(bf16)

    def conv_away(step, carry):
        conv(step, 1 - c)
        return carry

    def conv_own(step, carry):
        conv(step, c)
        return carry

    lax.fori_loop(0, 8, conv_away, 0)
    mixed_away = remote(
        mixed.at[:, 1 - c], rows_m.at[pl.ds(8 * c, 8)], ex_send.at[0], ex_recv.at[0], core
    )
    mixed_away.start()
    lax.fori_loop(0, 8, conv_own, 0)
    mixed_own = pltpu.make_async_copy(mixed.at[:, c], rows_m.at[pl.ds(8 * c, 8)], own_sem.at[0])
    mixed_own.start()
    mixed_own.wait()
    mixed_away.wait()
    flat = rows_m[...].reshape(16 * across, width)
    tok[...] = dot_nn(perm[0], flat).astype(bf16)
    tok_out = pltpu.make_async_copy(tok, o_tok, out_sem.at[1])
    tok_out.start()
    loads[0].wait()
    for part in range(3):
        cut = slice(part * width, (part + 1) * width)
        proj[:, cut] = dot_nn(tok[...], wqkv[:, cut]).astype(bf16)
    proj_out = pltpu.make_async_copy(proj, o_proj, out_sem.at[2])
    proj_out.start()

    pairs = width // LANES
    size = tok.shape[0] // 2
    low_lane = lax.broadcasted_iota(jnp.int32, (size, LANES), 1) < LANES // 2
    lane_id = lax.broadcasted_iota(jnp.int32, (size, LANES), 1)
    zero = jnp.zeros((), bf16)

    def attend(index, carry):
        half, pair = index // pairs, lax.rem(index, pairs)
        rows = pl.ds(pl.multiple_of(half * size, size), size)

        def part(n):
            return proj[rows, pl.ds(pl.multiple_of(n * width + pair * LANES, LANES), LANES)]

        q, k, v = part(0) * jnp.asarray(0.125, bf16), part(1), part(2)
        total = jnp.zeros((size, LANES), f32)
        sums = lse[half]
        for h in range(2):
            mine = low_lane if h == 0 else jnp.logical_not(low_lane)
            scores = dot_nt(q, jnp.where(mine, k, zero)) + bias[half]
            top = jnp.max(scores, axis=-1, keepdims=True)
            powers = jnp.exp(scores - top)
            mass = jnp.sum(powers, axis=-1, keepdims=True)
            weights = (powers * (1.0 / mass)).astype(bf16)
            total = total + dot_nn(weights, jnp.where(mine, v, zero))
            sums = jnp.where(lane_id == 2 * pair + h, top + jnp.log(mass), sums)
        lse[half] = sums
        att[rows, pl.ds(pl.multiple_of(pair * LANES, LANES), LANES)] = total.astype(bf16)
        return carry

    lse[...] = jnp.zeros(lse.shape, f32)
    lax.fori_loop(0, 2 * pairs, attend, 0)
    att_out = pltpu.make_async_copy(att, o_att, out_sem.at[3])
    att_out.start()
    lse_out = pltpu.make_async_copy(lse, o_lse, out_sem.at[4])
    lse_out.start()
    loads[1].wait()
    branch = dot_nn(att[...], wo[...]).astype(bf16)
    brm[...] = dot_nn(perm[1], branch).astype(bf16).reshape(16, across, width)
    ret_away = remote(
        brm.at[pl.ds(7 * (1 - c), 9)], o_ret.at[:, c], ex_send.at[1], ex_recv.at[1], core
    )
    ret_away.start()
    ret_own = pltpu.make_async_copy(brm.at[pl.ds(7 * c, 9)], o_ret.at[:, c], own_sem.at[1])
    ret_own.start()
    for out in (x_out, tok_out, proj_out, att_out, lse_out, ret_own):
        out.wait()
    ret_away.wait()
    spread_out(x_in, xf, x_send, x_recv, True)
    spread_out(cot_in, o_cot, c_send, c_recv, True)
    arrived(o_cot, c_recv)


def front(inputs, cotangent, mod, kern, wqkv, wo, lab_row, lab_col):
    across, width = inputs.shape[2], inputs.shape[3]
    tokens = 16 * across
    any_space = pl.BlockSpec(memory_space=pl.ANY)
    vmem = pl.BlockSpec(memory_space=pltpu.VMEM)
    shape = jax.ShapeDtypeStruct
    dma = pltpu.SemaphoreType.DMA
    return pl.pallas_call(
        front_kernel,
        out_shape=(
            shape((18, across, width), bf16),
            shape((18, across, width), bf16),
            shape((9, 2, across, width), bf16),
            shape((tokens, width), bf16),
            shape((tokens, 3 * width), bf16),
            shape((tokens, width), bf16),
            shape((2, tokens // 2, LANES), f32),
        ),
        in_specs=[any_space, any_space, vmem, vmem, any_space, any_space, vmem, vmem],
        out_specs=[any_space] * 7,
        scratch_shapes=[
            pltpu.VMEM((18, across, width), bf16),
            pltpu.VMEM(wqkv.shape, bf16),
            pltpu.VMEM(wo.shape, bf16),
            pltpu.VMEM((3, 18, across, width), f32),
            pltpu.VMEM((8, 2, across, width), bf16),
            pltpu.VMEM((16, across, width), bf16),
            pltpu.VMEM((2, tokens, tokens), bf16),
            pltpu.VMEM((2, tokens // 2, tokens // 2), f32),
            pltpu.VMEM((tokens, width), bf16),
            pltpu.VMEM((tokens, 3 * width), bf16),
            pltpu.VMEM((tokens, width), bf16),
            pltpu.VMEM((2, tokens // 2, LANES), f32),
            pltpu.VMEM((16, across, width), bf16),
            dma((2,)), dma((3,)), dma((3,)), dma((3,)), dma((3,)), dma((2,)), dma((2,)),
            dma((2,)), dma((5,)),
        ],
        compiler_params=pltpu.CompilerParams(
            collective_id=1, has_side_effects=True, vmem_limit_bytes=60 << 20
        ),
        name="front",
    )(inputs, cotangent, mod, kern, wqkv, wo, lab_row, lab_col)


def gelu_parts(x):
    size = jnp.abs(x)
    t = 1.0 / (1.0 + (0.3275911 * 0.7071067811865476) * size)
    bell = jnp.exp(-0.5 * x * x)
    series = t * (
        0.254829592
        + t * (-0.284496736 + t * (1.421413741 + t * (-1.453152027 + t * 1.061405429)))
    )
    tail = 0.5 * series * bell
    mass = jnp.where(x >= 0, 1.0 - tail, tail)
    return x * mass, mass + x * bell * 0.3989422804014327


def feed_kernel(
    x_in, ret_in, cot_in, mod, up, kern, down,
    o_up, o_down, o_kern, o_res, o_mid, o_rg, o_small,
    feed_in, feed_t, btg, out_acc, back_acc, hid, hs, gs, act, slope, hg,
):
    j = pl.program_id(0)
    c = lax.rem(lax.axis_index("group"), 2)
    across = 32
    width = feed_in.shape[1]
    tile = up.shape[1]
    frame_rows = feed_in.shape[0] // across
    own = pl.ds(pl.multiple_of(2 * c * across, 64), 16 * across)

    def middle_of(row):
        place = pl.ds(pl.multiple_of(row * across, across), across)
        returned = ret_in[place, :].astype(f32)
        return x_in[place, :].astype(f32) + mod[2:3, :] * returned, returned

    @pl.when(j == 0)
    def _():
        def prepare(row, carry):
            place = pl.ds(pl.multiple_of(row * across, across), across)
            normal, _ = normalize(middle_of(row)[0])
            feed_in[place, :] = (normal * (1.0 + mod[4:5, :]) + mod[3:4, :]).astype(bf16)
            btg[place, :] = (mod[5:6, :] * cot_in[place, :].astype(f32)).astype(bf16)
            return carry

        lax.fori_loop(0, frame_rows, prepare, 0)
        feed_t[...] = feed_in[own, :].T
        out_acc[...] = jnp.zeros(out_acc.shape, f32)
        back_acc[...] = jnp.zeros(back_acc.shape, f32)
        for s in range(3):
            hs[s, 18 * c] = jnp.zeros((across, tile), f32)
            gs[s, 17 * c] = jnp.zeros((across, tile), f32)

    hid[...] = dot_nn(feed_in[...], up[...]).astype(bf16)

    def lay_hidden(row, carry):
        value = hid[pl.ds(pl.multiple_of(row * across, across), across), :].astype(f32)
        before, after = column_shifts(value)
        hs[0, 1 - c + row] = before
        hs[1, 1 - c + row] = value
        hs[2, 1 - c + row] = after
        return carry

    lax.fori_loop(0, frame_rows, lay_hidden, 0)

    for lane in range(0, tile, LANES):
        cut = slice(lane, lane + LANES)
        taps = [kern[n : n + 1, cut].astype(f32) for n in range(9)]

        def forward(row, carry):
            total = jnp.zeros((across, LANES), f32)
            for r in range(3):
                for s in range(3):
                    total = total + taps[3 * r + s] * hs[s, row + r, :, cut]
            place = pl.ds(pl.multiple_of(row * across, across), across)
            value, steep = gelu_parts(total)
            act[place, cut] = value.astype(bf16)
            slope[place, cut] = steep
            return carry

        lax.fori_loop(0, 17, forward, 0)

    inside = pl.ds(pl.multiple_of(c * across, across), 16 * across)
    around = pl.ds(pl.multiple_of(c * across, across), 17 * across)
    own_act = act[inside, :]
    out_acc[...] += dot_nn(own_act, down[...])
    o_down[...] = dot_tn(own_act, btg[own, :]).astype(bf16)
    slope[...] = slope[...] * dot_nt(btg[around, :], down[...])

    def lay_grad(row, carry):
        value = slope[pl.ds(pl.multiple_of(row * across, across), across), :]
        value = value.astype(bf16).astype(f32)
        before, after = column_shifts(value)
        gs[0, 1 - c + row] = after
        gs[1, 1 - c + row] = value
        gs[2, 1 - c + row] = before
        return carry

    lax.fori_loop(0, 17, lay_grad, 0)

    for lane in range(0, tile, LANES):
        cut = slice(lane, lane + LANES)
        taps = [kern[n : n + 1, cut].astype(f32) for n in range(9)]

        def backward(row, sums):
            total = jnp.zeros((across, LANES), f32)
            value = hs[1, row + c + 1, :, cut]
            later = []
            for r in range(3):
                for s in range(3):
                    grad = gs[s, row + 2 - r, :, cut]
                    total = total + taps[3 * r + s] * grad
                    later.append(sums[3 * r + s] + fold(value * grad))
            hg[pl.ds(pl.multiple_of(row * across, across), across), cut] = total.astype(bf16)
            return tuple(later)

        sums = lax.fori_loop(
            0, 16, backward, tuple(jnp.zeros((8, LANES), f32) for _ in range(9))
        )
        for n in range(9):
            o_kern[n : n + 1, cut] = jnp.sum(sums[n], axis=0, keepdims=True)

    o_kern[9:16, :] = jnp.zeros((7, tile), f32)
    o_up[...] = dot_nn(feed_t[...], hg[...]).astype(bf16)
    back_acc[...] += dot_nt(hg[...], up[...])

    @pl.when(j == pl.num_programs(0) - 1)
    def _():
        def finish(row, sums):
            frame = row + 2 * c
            place = pl.ds(pl.multiple_of(row * across, across), across)
            at = pl.ds(pl.multiple_of(frame * across, across), across)
            middle, returned = middle_of(frame)
            cot = cot_in[at, :].astype(f32)
            branch = out_acc[place, :]
            o_res[place, :] = (middle + mod[5:6, :] * branch).astype(bf16)
            normal, scale = normalize(middle)
            grad = back_acc[place, :]
            mid = cot + normalize_back(grad * (1.0 + mod[4:5, :]), normal, scale)
            o_mid[place, :] = mid
            o_rg[place, :] = (mod[2:3, :] * mid).astype(bf16)
            terms = (mid * returned, grad, grad * normal, cot * branch)
            return tuple(total + fold(term) for total, term in zip(sums, terms))

        sums = lax.fori_loop(
            0, 16, finish, tuple(jnp.zeros((8, width), f32) for _ in range(4))
        )
        o_small[...] = jnp.zeros((8, width), f32)
        for n in range(4):
            o_small[n + 2 : n + 3, :] = jnp.sum(sums[n], axis=0, keepdims=True)


def feed(x_frame, returned, cot_frame, mod, up, kern, down):
    width, units = up.shape
    frame = x_frame.shape[0]
    across = frame // 18
    tokens = 16 * across
    shape = jax.ShapeDtypeStruct
    tile = min(TILE, units)

    def still(*size):
        return pl.BlockSpec(size, lambda j: (0, 0), pipeline_mode=pl.Buffered(1))

    columns = pl.BlockSpec((width, tile), lambda j: (0, j))
    rows = pl.BlockSpec((tile, width), lambda j: (j, 0))
    work = 6 * 2 * tokens * width * units
    return pl.pallas_call(
        feed_kernel,
        grid=(units // tile,),
        out_shape=(
            shape((width, units), bf16),
            shape((units, width), bf16),
            shape((16, units), f32),
            shape((tokens, width), bf16),
            shape((tokens, width), f32),
            shape((tokens, width), bf16),
            shape((8, width), f32),
        ),
        in_specs=[
            still(frame, width), still(frame, width), still(frame, width), still(8, width),
            columns, pl.BlockSpec((9, tile), lambda j: (0, j)), rows,
        ],
        out_specs=[
            columns, rows, pl.BlockSpec((16, tile), lambda j: (0, j)),
            still(tokens, width), still(tokens, width), still(tokens, width), still(8, width),
        ],
        scratch_shapes=[
            pltpu.VMEM((frame, width), bf16),
            pltpu.VMEM((width, tokens), bf16),
            pltpu.VMEM((frame, width), bf16),
            pltpu.VMEM((tokens, width), f32),
            pltpu.VMEM((tokens, width), f32),
            pltpu.VMEM((frame, tile), bf16),
            pltpu.VMEM((3, 19, across, tile), f32),
            pltpu.VMEM((3, 18, across, tile), f32),
            pltpu.VMEM((17 * across, tile), bf16),
            pltpu.VMEM((17 * across, tile), f32),
            pltpu.VMEM((tokens, tile), bf16),
        ],
        compiler_params=pltpu.CompilerParams(
            dimension_semantics=("arbitrary",), vmem_limit_bytes=60 << 20
        ),
        cost_estimate=pl.CostEstimate(
            flops=work, bytes_accessed=8 * width * units, transcendentals=tokens * units
        ),
        name="feed",
    )(x_frame, returned, cot_frame, mod, up, kern, down)


def back_kernel(
    mid_in, rg_in, tok_in, proj_in, att_in, lse, x_in, mod, small, kern, wqkv_in, wo_in,
    lab_row, lab_col, res_in,
    o_wqkv, o_wo, o_res, o_ig, o_kern, o_small,
    mid, tok, proj, att, xf, wqkv, wo, rows_m, perm, bias, grad, datt, dproj, wgrad, wgrad_o,
    brm, frame, gs, value, agrad, ig,
    load_sem, r_send, r_recv, i_send, i_recv, ex_send, ex_recv, own_sem, out_sem,
):
    b = lax.axis_index("batch")
    g = lax.axis_index("group")
    c, p = lax.rem(g, 2), g // 2
    core, side, corner = (b, g + 1 - 2 * c), (b, g + 2 - 4 * p), (b, 3 - g)
    inner = jnp.logical_or(g == 1, g == 2)
    across, width = xf.shape[1], xf.shape[2]
    pairs = width // LANES
    tokens = tok.shape[0]
    size = tokens // 2

    def send_home(src, dst, send, recv, waiting):
        moves = [
            remote(
                src.at[pl.ds(8 * n, 8)], dst.at[p], send.at[n], recv.at[p], (b, 2 * c + n)
            )
            for n in range(2)
        ]
        away = remote(
            src.at[pl.ds(8 * (1 - c), 8)], dst.at[p], send.at[0], recv.at[p], core
        )
        stay = pltpu.make_async_copy(src.at[pl.ds(8 * c, 8)], dst.at[p], recv.at[p])

        @pl.when(inner)
        def _():
            for move in moves:
                if waiting:
                    move.wait_send()
                else:
                    move.start()

        @pl.when(jnp.logical_not(inner))
        def _():
            if waiting:
                away.wait_send()
            else:
                away.start()
                stay.start()

    def home(dst, recv):
        for n in range(2):
            pltpu.make_async_copy(dst.at[n], dst.at[n], recv.at[n]).wait()

    pieces = [
        (wo_in, wo), (att_in, att), (proj_in, proj), (tok_in, tok), (wqkv_in, wqkv), (x_in, xf),
        (mid_in, mid),
    ]
    loads = [
        pltpu.make_async_copy(src, dst, load_sem.at[n]) for n, (src, dst) in enumerate(pieces)
    ]
    for load in loads:
        load.start()
    meet([core, side, corner])
    grad_away = remote(
        rg_in.at[:, 1 - c], rows_m.at[pl.ds(8 * c, 8)], ex_send.at[0], ex_recv.at[0], core
    )
    grad_away.start()
    grad_own = pltpu.make_async_copy(rg_in.at[:, c], rows_m.at[pl.ds(8 * c, 8)], own_sem.at[0])
    grad_own.start()
    send_home(res_in, o_res, r_send, r_recv, False)
    perm[0] = permutation(False)
    perm[1] = permutation(True)
    for half in range(2):
        bias[half] = mask_bias(lab_row[half], lab_col[half])
    grad_own.wait()
    grad_away.wait()
    grad[...] = dot_nn(perm[0], rows_m[...].reshape(tokens, width)).astype(bf16)
    loads[0].wait()
    loads[1].wait()
    datt[...] = dot_nt(grad[...], wo[...]).astype(bf16)
    wgrad_o[...] = dot_tn(att[...], grad[...]).astype(bf16)
    wo_out = pltpu.make_async_copy(wgrad_o, o_wo, out_sem.at[0])
    wo_out.start()
    loads[2].wait()

    low_lane = lax.broadcasted_iota(jnp.int32, (size, LANES), 1) < LANES // 2
    lane_id = lax.broadcasted_iota(jnp.int32, (size, LANES), 1)
    zero = jnp.zeros((), bf16)

    def attend(index, carry):
        half, pair = index // pairs, lax.rem(index, pairs)
        rows = pl.ds(pl.multiple_of(half * size, size), size)

        def cut(n):
            return pl.ds(pl.multiple_of(n * width + pair * LANES, LANES), LANES)

        q = proj[rows, cut(0)] * jnp.asarray(0.125, bf16)
        k, v, up = proj[rows, cut(1)], proj[rows, cut(2)], datt[rows, cut(0)]
        sums = lse[half]
        dq = jnp.zeros((size, LANES), f32)
        dk = jnp.zeros((size, LANES), f32)
        dv = jnp.zeros((size, LANES), f32)
        for h in range(2):
            mine = low_lane if h == 0 else jnp.logical_not(low_lane)
            key = jnp.where(mine, k, zero)
            scores = dot_nt(q, key) + bias[half]
            mass = jnp.sum(
                jnp.where(lane_id == 2 * pair + h, sums, 0.0), axis=-1, keepdims=True
            )
            weights = jnp.exp(scores - mass)
            pull = dot_nt(up, jnp.where(mine, v, zero))
            mean = jnp.sum(weights * pull, axis=-1, keepdims=True)
            spare = (weights * (pull - mean)).astype(bf16)
            dq = dq + dot_nn(spare, key)
            dk = dk + dot_tn(spare, jnp.where(mine, q, zero))
            dv = dv + dot_tn(weights.astype(bf16), jnp.where(mine, up, zero))
        dproj[rows, cut(0)] = (dq * 0.125).astype(bf16)
        dproj[rows, cut(1)] = dk.astype(bf16)
        dproj[rows, cut(2)] = dv.astype(bf16)
        return carry

    lax.fori_loop(0, 2 * pairs, attend, 0)
    loads[4].wait()
    back = dot_nt(dproj[...], wqkv[...]).astype(bf16)
    brm[...] = dot_nn(perm[1], back).astype(bf16).reshape(16, across, width)
    mixed_away = remote(
        brm.at[pl.ds(7 * (1 - c), 9)], frame.at[:, c], ex_send.at[1], ex_recv.at[1], core
    )
    mixed_away.start()
    mixed_own = pltpu.make_async_copy(brm.at[pl.ds(7 * c, 9)], frame.at[:, c], own_sem.at[1])
    mixed_own.start()
    loads[3].wait()
    for part in range(3):
        span = slice(part * width, (part + 1) * width)
        wgrad[:, span] = dot_tn(tok[...], dproj[:, span]).astype(bf16)
    wqkv_out = pltpu.make_async_copy(wgrad, o_wqkv, out_sem.at[1])
    wqkv_out.start()
    loads[5].wait()
    loads[6].wait()

    shift = mod[0:1, :]
    scale_in = 1.0 + mod[1:2, :]

    def again(row, carry):
        normal, _ = normalize(xf[2 * c + row].astype(f32))
        value[row] = (normal * scale_in + shift).astype(bf16).astype(f32)
        return carry

    lax.fori_loop(0, 16, again, 0)
    mixed_own.wait()
    mixed_away.wait()

    def lay(row, carry):
        at = c + row
        line = frame[at // 2, lax.rem(at, 2)].astype(f32)
        before, after = column_shifts(line)
        gs[0, 1 - c + row] = after
        gs[1, 1 - c + row] = line
        gs[2, 1 - c + row] = before
        return carry

    lax.fori_loop(0, 17, lay, 0)
    for s in range(3):
        gs[s, 17 * c] = jnp.zeros((across, width), f32)

    for lane in range(0, width, LANES):
        span = slice(lane, lane + LANES)
        taps = [kern[n : n + 1, span].astype(f32) for n in range(9)]

        def backward(row, sums):
            total = jnp.zeros((across, LANES), f32)
            own = value[row, :, span]
            later = []
            for r in range(3):
                for s in range(3):
                    line = gs[s, row + 2 - r, :, span]
                    total = total + taps[3 * r + s] * line
                    later.append(sums[3 * r + s] + fold(own * line))
            agrad[row, :, span] = total
            return tuple(later)

        sums = lax.fori_loop(
            0, 16, backward, tuple(jnp.zeros((8, LANES), f32) for _ in range(9))
        )
        for n in range(9):
            o_kern[n : n + 1, span] = jnp.sum(sums[n], axis=0, keepdims=True)
    o_kern[9:16, :] = jnp.zeros((7, width), f32)

    def finish(row, sums):
        normal, scale = normalize(xf[2 * c + row].astype(f32))
        line = agrad[row]
        place = pl.ds(pl.multiple_of(row * across, across), across)
        total = mid[place, :] + normalize_back(line * scale_in, normal, scale)
        ig[row] = total.astype(bf16)
        return (sums[0] + fold(line), sums[1] + fold(line * normal))

    sums = lax.fori_loop(0, 16, finish, tuple(jnp.zeros((8, width), f32) for _ in range(2)))
    send_home(ig, o_ig, i_send, i_recv, False)
    o_small[...] = small[...]
    for n in range(2):
        o_small[n : n + 1, :] = jnp.sum(sums[n], axis=0, keepdims=True)
    o_small[6:7, :] = mod[6:7, :]
    wo_out.wait()
    wqkv_out.wait()
    send_home(res_in, o_res, r_send, r_recv, True)
    send_home(ig, o_ig, i_send, i_recv, True)
    home(o_res, r_recv)
    home(o_ig, i_recv)


def back(mid, rg, tok, proj, att, lse, x_frame, mod, small, kern, wqkv, wo, lab_row, lab_col, res):
    across, width = x_frame.shape[1], x_frame.shape[2]
    tokens = 16 * across
    any_space = pl.BlockSpec(memory_space=pl.ANY)
    vmem = pl.BlockSpec(memory_space=pltpu.VMEM)
    shape = jax.ShapeDtypeStruct
    dma = pltpu.SemaphoreType.DMA
    return pl.pallas_call(
        back_kernel,
        out_shape=(
            shape((width, 3 * width), bf16),
            shape((width, width), bf16),
            shape((2, 8, across, width), bf16),
            shape((2, 8, across, width), bf16),
            shape((16, width), f32),
            shape((8, width), f32),
        ),
        in_specs=[any_space] * 5 + [vmem, any_space, vmem, vmem, vmem, any_space, any_space,
                                    vmem, vmem, any_space],
        out_specs=[any_space] * 4 + [vmem, vmem],
        scratch_shapes=[
            pltpu.VMEM((tokens, width), f32),
            pltpu.VMEM((tokens, width), bf16),
            pltpu.VMEM((tokens, 3 * width), bf16),
            pltpu.VMEM((tokens, width), bf16),
            pltpu.VMEM((18, across, width), bf16),
            pltpu.VMEM(wqkv.shape, bf16),
            pltpu.VMEM(wo.shape, bf16),
            pltpu.VMEM((16, across, width), bf16),
            pltpu.VMEM((2, tokens, tokens), bf16),
            pltpu.VMEM((2, tokens // 2, tokens // 2), f32),
            pltpu.VMEM((tokens, width), bf16),
            pltpu.VMEM((tokens, width), bf16),
            pltpu.VMEM((tokens, 3 * width), bf16),
            pltpu.VMEM((width, 3 * width), bf16),
            pltpu.VMEM((width, width), bf16),
            pltpu.VMEM((16, across, width), bf16),
            pltpu.VMEM((9, 2, across, width), bf16),
            pltpu.VMEM((3, 18, across, width), f32),
            pltpu.VMEM((16, across, width), f32),
            pltpu.VMEM((16, across, width), f32),
            pltpu.VMEM((16, across, width), bf16),
            dma((7,)), dma((2,)), dma((2,)), dma((2,)), dma((2,)), dma((2,)), dma((2,)),
            dma((2,)), dma((2,)),
        ],
        compiler_params=pltpu.CompilerParams(
            collective_id=2, has_side_effects=True, vmem_limit_bytes=62 << 20
        ),
        name="back",
    )(mid, rg, tok, proj, att, lse, x_frame, mod, small, kern, wqkv, wo, lab_row, lab_col, res)


def reduce_kernel(
    nb, units, proj, outw, up, down, mg, kern_one, kern_two,
    o_proj, o_out, o_up, o_down, o_mg, o_one, o_two,
    s0, r1, r2x, r2y, r3, r4, fin, mg_r1, mg_all, kk, kr, kz,
    load_sem, s1, q1, s2, q2, s3, q3, s4, q4, s5, q5, s6, q6, out_sem,
    mg_send, mg_recv, mz_send, mz_recv, mg_io, k_send, k_recv, kz_send, kz_recv,
):
    nz = nb // 2
    chunks = len(units)
    b = lax.axis_index("batch")
    g = lax.axis_index("group")
    cb, xb = lax.rem(g, 2), g // 2
    yb, zb = lax.rem(b, 2), b // 2
    core = (b, g + 1 - 2 * cb)
    side = (b, g + 2 - 4 * xb)
    across = (b + 1 - 2 * yb, g)
    others = [lax.rem(zb + d, nz) for d in range(nz)]
    far = [(2 * z + yb, g) for z in others]
    arrays = {"proj": proj, "out": outw, "up": up, "down": down}
    results = {"proj": o_proj, "out": o_out, "up": o_up, "down": o_down}

    def window(name, part, column, ref, lead):
        if name == "down":
            return ref.at[(*lead, part, slice(None), pl.ds(column, CHUNK))]
        return ref.at[(*lead, slice(None), pl.ds(column, CHUNK))]

    def load(k, q):
        name, part, column = units[k][q]
        source = window(name, part, column, arrays[name], (slice(None), slice(None)))
        return pltpu.make_async_copy(source, s0.at[k, q % 2, q // 2], load_sem.at[k, q])

    def store(k, q):
        name, part, column = units[k][q]
        target = window(name, part, column, results[name], ())
        return pltpu.make_async_copy(fin.at[k, q % 2, q // 2], target, out_sem.at[k, q])

    def copy_1(k):
        return remote(s0.at[k, 1 - cb], r1.at[k], s1.at[k], q1.at[k], core)

    def copy_2(k):
        if k % 2 == 0:
            return remote(s0.at[k, cb, 1 - xb], r2x.at[k // 2], s2.at[k], q2.at[k], side)
        return remote(
            s0.at[k, cb, :, :, 1 - yb], r2y.at[k // 2], s2.at[k], q2.at[k], across
        )

    def copy_3(k):
        if k % 2 == 0:
            return remote(s0.at[k, cb, xb, :, 1 - yb], r3.at[k], s3.at[k], q3.at[k], across)
        return remote(s0.at[k, cb, 1 - xb, :, yb], r3.at[k], s3.at[k], q3.at[k], side)

    def copy_4(k, d):
        return remote(
            s0.at[k, cb, xb, others[d], yb], r4.at[k, d - 1], s4.at[k, d - 1], q4.at[k, d - 1],
            far[d],
        )

    def copy_5(k, mine):
        place = xb if mine else 1 - xb
        return remote(fin.at[k, cb, place], fin.at[k, cb, place], s5.at[k], q5.at[k], side)

    def copy_6(k, mine):
        place = cb if mine else 1 - cb
        return remote(fin.at[k, place], fin.at[k, place], s6.at[k], q6.at[k], core)

    def add_1(k):
        copy_1(k).wait_recv()

        def step(i, carry):
            x, z, y = i // (2 * nz), lax.rem(i // 2, nz), lax.rem(i, 2)
            s0[k, cb, x, z, y] = s0[k, cb, x, z, y] + r1[k, x, z, y]
            return carry

        lax.fori_loop(0, 4 * nz, step, 0)
        copy_2(k).start()

    def add_2(k):
        copy_2(k).wait_recv()

        def step(i, carry):
            if k % 2 == 0:
                z, y = i // 2, lax.rem(i, 2)
                s0[k, cb, xb, z, y] = s0[k, cb, xb, z, y] + r2x[k // 2, z, y]
            else:
                x, z = i // nz, lax.rem(i, nz)
                s0[k, cb, x, z, yb] = s0[k, cb, x, z, yb] + r2y[k // 2, x, z]
            return carry

        lax.fori_loop(0, 2 * nz, step, 0)
        copy_3(k).start()

    def add_3(k):
        copy_3(k).wait_recv()

        def step(z, carry):
            s0[k, cb, xb, z, yb] = s0[k, cb, xb, z, yb] + r3[k, z]
            return carry

        lax.fori_loop(0, nz, step, 0)
        for d in range(1, nz):
            copy_4(k, d).start()

    def add_4(k):
        total = s0[k, cb, xb, zb, yb].astype(f32)
        for d in range(1, nz):
            copy_4(k, d).wait_recv()
            total = total + r4[k, d - 1].astype(f32)
        fin[k, cb, xb] = total.astype(bf16)
        copy_5(k, True).start()

    def pass_5(k):
        copy_5(k, False).wait_recv()
        copy_6(k, True).start()

    def pass_6(k):
        copy_6(k, False).wait_recv()
        for q in range(4):
            store(k, q).start()

    for k in range(chunks):
        for q in range(4):
            load(k, q).start()

    meet([core, side, across, *far[1:]])
    split = kern_one.shape[1]
    kk[0, :, :split] = kern_one[...].astype(bf16)
    kk[0, :, split:] = kern_two[...].astype(bf16)
    here = (zb, yb, xb)
    peers = [core, side, across]

    def small_copy(stage):
        if stage == 0:
            return remote(mg, mg_r1, mg_send.at[0], mg_recv.at[0], core)
        place = mg_all.at[here] if stage == 1 else mg_all.at[zb, yb]
        return remote(place, place, mg_send.at[stage], mg_recv.at[stage], peers[stage])

    def small_come(stage):
        place = mg_all.at[zb, yb, 1 - xb] if stage == 1 else mg_all.at[zb, 1 - yb]
        remote(place, place, mg_send.at[stage], mg_recv.at[stage], peers[stage]).wait_recv()

    def small_far(d, z):
        return remote(mg_all.at[z], mg_all.at[z], mz_send.at[d - 1], mz_recv.at[d - 1], far[d])

    def kern_copy(stage):
        return remote(kk.at[stage], kr.at[stage], k_send.at[stage], k_recv.at[stage], peers[stage])

    def kern_far(d):
        return remote(kk.at[3], kz.at[d - 1], kz_send.at[d - 1], kz_recv.at[d - 1], far[d])

    def kern_add(stage):
        kern_copy(stage).wait_recv()
        kk[stage + 1] = (kk[stage].astype(f32) + kr[stage].astype(f32)).astype(bf16)

    def small_steps(t):
        if t == 1:
            small_copy(0).wait_recv()
            mg_all[here] = mg[...] + mg_r1[...]
            small_copy(1).start()
            kern_add(0)
            kern_copy(1).start()
        if t == 2:
            small_come(1)
            small_copy(2).start()
            kern_add(1)
            kern_copy(2).start()
        if t == 3:
            small_come(2)
            for d in range(1, nz):
                small_far(d, zb).start()
            kern_add(2)
            for d in range(1, nz):
                kern_far(d).start()

    small_copy(0).start()
    kern_copy(0).start()
    for k in range(chunks):
        for q in range(4):
            load(k, q).wait()
        copy_1(k).start()
    stages = [add_1, add_2, add_3, add_4, pass_5, pass_6]
    for t in range(chunks + len(stages) - 1):
        for index, stage in enumerate(stages):
            if 0 <= t - index < chunks:
                stage(t - index)
        small_steps(t)
    for d in range(1, nz):
        small_far(d, lax.rem(zb + nz - d, nz)).wait_recv()
        small_far(d, zb).wait_send()
    mg_store = pltpu.make_async_copy(mg_all, o_mg, mg_io)
    mg_store.start()
    total = kk[3].astype(f32)
    for d in range(1, nz):
        kern_far(d).wait()
        total = total + kz[d - 1].astype(f32)
    o_one[...] = total[:, :split]
    o_two[...] = total[:, split:]
    for stage in range(3):
        small_copy(stage).wait_send()
        kern_copy(stage).wait_send()
    mg_store.wait()
    for k in range(chunks):
        copy_1(k).wait_send()
        copy_2(k).wait_send()
        copy_3(k).wait_send()
        for d in range(1, nz):
            copy_4(k, d).wait_send()
        copy_5(k, True).wait_send()
        copy_6(k, True).wait_send()
        for q in range(4):
            store(k, q).wait()


def reduce_all(proj, outw, up, down, mg, kern_one, kern_two):
    nb = lax.axis_size("batch")
    nz = nb // 2
    rows = proj.shape[0] // nb
    parts = down.shape[0] // (nb * rows)
    spans = [("proj", 0, proj.shape[1]), ("out", 0, outw.shape[1]), ("up", 0, up.shape[1])]
    spans = spans + [("down", part, down.shape[1]) for part in range(parts)]
    flat = [
        (name, part, column) for name, part, size in spans for column in range(0, size, CHUNK)
    ]
    chunks = len(flat) // 4
    units = [[flat[q * chunks + k] for q in range(4)] for k in range(chunks)]
    bf = bf16
    extra = kern_one.shape[1] + kern_two.shape[1]
    dma = pltpu.SemaphoreType.DMA
    many = max(nz - 1, 1)
    scratch = [
        pltpu.VMEM((chunks, 2, 2, nz, 2, rows, CHUNK), bf),
        pltpu.VMEM((chunks, 2, nz, 2, rows, CHUNK), bf),
        pltpu.VMEM(((chunks + 1) // 2, nz, 2, rows, CHUNK), bf),
        pltpu.VMEM(((chunks + 1) // 2, 2, nz, rows, CHUNK), bf),
        pltpu.VMEM((chunks, nz, rows, CHUNK), bf),
        pltpu.VMEM((chunks, many, rows, CHUNK), bf),
        pltpu.VMEM((chunks, 2, 2, rows, CHUNK), bf),
        pltpu.VMEM(mg.shape, f32),
        pltpu.VMEM((nz, 2, 2, *mg.shape), f32),
        pltpu.VMEM((4, 16, extra), bf),
        pltpu.VMEM((3, 16, extra), bf),
        pltpu.VMEM((many, 16, extra), bf),
        dma((chunks, 4)),
        *[dma((chunks,)) for _ in range(6)],
        dma((chunks, many)),
        dma((chunks, many)),
        *[dma((chunks,)) for _ in range(4)],
        dma((chunks, 4)),
        dma((3,)),
        dma((3,)),
        dma((many,)),
        dma((many,)),
        dma,
        dma((3,)),
        dma((3,)),
        dma((many,)),
        dma((many,)),
    ]
    any_space = pl.BlockSpec(memory_space=pl.ANY)
    vmem = pl.BlockSpec(memory_space=pltpu.VMEM)
    shape = jax.ShapeDtypeStruct
    results = pl.pallas_call(
        partial(reduce_kernel, nb, units),
        out_shape=(
            shape((rows, proj.shape[1]), bf),
            shape((rows, outw.shape[1]), bf),
            shape((rows, up.shape[1]), bf),
            shape((parts, rows, down.shape[1]), bf),
            shape((nz, 2, 2, *mg.shape), f32),
            shape(kern_one.shape, f32),
            shape(kern_two.shape, f32),
        ),
        in_specs=[any_space] * 4 + [vmem] * 3,
        out_specs=[any_space] * 5 + [vmem] * 2,
        scratch_shapes=scratch,
        compiler_params=pltpu.CompilerParams(
            collective_id=0, has_side_effects=True, vmem_limit_bytes=60 << 20
        ),
        name="reduce_grads",
    )(
        proj.reshape(nz, 2, rows, proj.shape[1]),
        outw.reshape(nz, 2, rows, outw.shape[1]),
        up.reshape(nz, 2, rows, up.shape[1]),
        down.reshape(nz, 2, parts, rows, down.shape[1]),
        mg, kern_one, kern_two,
    )
    return results


def body(
    inputs,
    segments,
    class_labels,
    time_steps,
    class_table,
    time_table,
    modulation_weight,
    project_weight,
    output_weight,
    kernel_attention,
    up_weight,
    kernel_feed,
    down_weight,
    cotangent,
):
    count, height, across, width = inputs.shape
    nb = lax.axis_size("batch")
    place_b = lax.axis_index("batch")
    group = lax.axis_index("group")
    canvas, core = group // 2, lax.rem(group, 2)
    half = across // 2

    label = lax.dynamic_index_in_dim(class_labels, canvas, 0, keepdims=False)
    moment = lax.dynamic_index_in_dim(time_steps, canvas, 0, keepdims=False)
    cond = lax.dynamic_slice_in_dim(class_table, label, 1, axis=0).astype(
        f32
    ) + lax.dynamic_slice_in_dim(time_table, moment, 1, axis=0).astype(f32)
    cond_low = jax.nn.silu(cond).astype(bf16)
    modulation = jnp.dot(cond_low, modulation_weight, preferred_element_type=f32)
    named = jnp.stack([label, moment]).astype(f32)
    mod = jnp.concatenate(
        [modulation.reshape(6, width), jnp.pad(named, (0, width - 2))[None], jnp.zeros((1, width), f32)]
    )
    grid = lax.dynamic_index_in_dim(segments, canvas, 0, keepdims=False)
    grid = grid.reshape(half, 2, half, 2).transpose(1, 3, 0, 2).reshape(2, 2, half * half)
    labels = lax.dynamic_index_in_dim(grid, core, 0, keepdims=False)
    lab_row, lab_col = labels[:, None, :], labels[:, :, None]

    x_frame, cot_frame, returned, tok, proj, att, lse = front(
        inputs, cotangent, mod, kernel_attention, project_weight, output_weight, lab_row, lab_col
    )
    flat = (18 * across, width)
    up_grad, down_grad, feed_kernel_grad, res, mid, rg, small = feed(
        x_frame.reshape(flat), returned.reshape(flat), cot_frame.reshape(flat), mod, up_weight,
        kernel_feed, down_weight,
    )
    project_grad, output_grad, result, inputs_gradient, attention_kernel_grad, small = back(
        mid, rg.reshape(8, 2, across, width), tok, proj, att, lse, x_frame, mod, small,
        kernel_attention, project_weight, output_weight, lab_row, lab_col,
        res.reshape(16, across, width),
    )
    (
        project_total, output_total, up_total, down_total, gathered, kernel_one, kernel_two
    ) = reduce_all(
        project_grad, output_grad, up_grad, down_grad, small, attention_kernel_grad,
        feed_kernel_grad,
    )
    project_total = project_total.astype(f32)
    output_total = output_total.astype(f32)
    up_total = up_total.astype(f32)
    down_total = down_total.reshape(-1, width).astype(f32)
    gathered = gathered.reshape(nb * count, 8, width)
    every_grad = gathered[:, :6].reshape(nb * count, 6 * width)
    every_name = (gathered[:, 6, :2] * 0.5).astype(jnp.int32)
    own = width // nb
    class_all = (every_name[:, :1] == jnp.arange(class_table.shape[0])[None, :]).astype(bf16)
    time_all = (every_name[:, 1:] == jnp.arange(time_table.shape[0])[None, :]).astype(bf16)
    class_part = lax.dynamic_slice_in_dim(class_table, place_b * own, own, axis=1)
    time_part = lax.dynamic_slice_in_dim(time_table, place_b * own, own, axis=1)
    cond_all = jnp.dot(class_all, class_part, preferred_element_type=f32) + jnp.dot(
        time_all, time_part, preferred_element_type=f32
    )
    act_all, silu_all = jax.vjp(jax.nn.silu, cond_all)
    low_all = act_all.astype(bf16)
    modulation_part = lax.dynamic_slice_in_dim(modulation_weight, place_b * own, own, axis=0)
    cond_act_grad = jnp.dot(every_grad, modulation_part.astype(f32).T, precision=highest)
    cond_grad = silu_all(cond_act_grad)[0]
    modulation_total = jnp.dot(low_all.astype(f32).T, every_grad, precision=highest)
    class_total = jnp.dot(class_all.astype(f32).T, cond_grad, precision=highest)
    time_total = jnp.dot(time_all.astype(f32).T, cond_grad, precision=highest)
    wide = feed_kernel_grad.shape[1] // nb
    attention_kernel_total = lax.dynamic_slice(kernel_one, (0, place_b * own), (9, own)).astype(f32)
    feed_kernel_total = lax.dynamic_slice(kernel_two, (0, place_b * wide), (9, wide)).astype(f32)
    return (
        result,
        inputs_gradient,
        class_total,
        time_total,
        modulation_total,
        project_total,
        output_total,
        attention_kernel_total,
        up_total,
        feed_kernel_total,
        down_total,
    )


def solution(mesh):
    in_specs = (
        P("batch", "group", None, None),
        P("batch", None),
        P("batch"),
        P("batch"),
        P(),
        P(),
        P(),
        P(),
        P(),
        P(),
        P(),
        P(),
        P(),
        P("batch", "group", None, None),
    )
    out_specs = (
        P("batch", "group", None, None),
        P("batch", "group", None, None),
        P(None, "batch"),
        P(None, "batch"),
        P("batch", None),
        P("batch", None),
        P("batch", None),
        P(None, "batch"),
        P("batch", None),
        P(None, "batch"),
        P("batch", None),
    )
    return jax.shard_map(body, mesh=mesh, in_specs=in_specs, out_specs=out_specs, check_vma=False)
```

time: 627 us -> 300 us (0.48)
  Pallas kernels: 92.6 us -> 252 us
  waiting for transfers between devices: 144 us -> 0 us
  matrix products: 121 us -> 13.9 us
  other arithmetic: 93.9 us -> 6.02 us
  local copies, waits for them, and re-layouts: 73.6 us -> 21.5 us
  blocking collectives: 42 us -> 0 us
  starting transfers between devices: 36.8 us -> 0 us
  between operations: 15.7 us -> 4.66 us
    pallas_call x0 -> x3, Pallas kernels: none -> 143 us  [the longest x1 69.6 us: feed(): pl.pallas_call(feed_kernel, grid=(units // tile,), out_shape=(shape((widt...]
    psum x1 -> x0, waiting for transfers between devices: 112 us -> none  [body(): lax.psum(feed_kernel_grad, ('batch', 'group'))]
    dot_general x26 -> x7, matrix products: 121 us -> 13.9 us  [the longest x1 4.95 us: body(): jnp.dot(cond_low, modulation_weight, preferred_element_type=f32)]
    convert_element_type x19 -> x6, other arithmetic: 73.4 us -> 5.34 us  [the longest x1 1.39 us: body(): named = jnp.stack([label, moment]).astype(f32)]
    psum x1 -> x0, blocking collectives: 42 us -> none  [body(): lax.psum(attention_kernel_grad, ('batch', 'group'))]
    all_to_all x4 -> x0, waiting for transfers between devices: 22.2 us -> none  [the longest x1 9.04 us: body(): lax.all_to_all(branch.reshape(count, 4, height // 2, half, width), 'group...]
    ppermute x8 -> x0, starting transfers between devices: 19.3 us -> none  [the longest x4 13.9 us: padded_2(): lax.ppermute(lax.slice_in_dim(block, block.shape[dim] - width, None, axis...]
    reshape x10 -> x2, local copies, waits for them, and re-layouts: 19.4 us -> 0.3 us  [body(): grid.reshape(half, 2, half, 2).transpose(1, 3, 0, 2)]
  transfers between devices with their start and end apart: 13 -> 0, of which waited for: 8 -> 0; matrix products, arithmetic and copies ran while one was open for 6% -> 0% of each run, Pallas kernels for 0% -> 0%
where the time goes in v2:
time: 300 us; the launch traced here: 299 us
  Pallas kernels  252 us (84%)
  local copies, waits for them, and re-layouts  21.5 us (7%)
  matrix products  13.9 us (5%)
  other arithmetic  6.02 us (2%)
  between operations  4.66 us (2%)
    pallas_call x1, Pallas kernels, reduce_all(): pl.pallas_call(partial(reduce_kernel, nb, units), out_shape=(shape((rows,...  109 us
    pallas_call x1, Pallas kernels, feed(): pl.pallas_call(feed_kernel, grid=(units // tile,), out_shape=(shape((widt...  69.6 us
    pallas_call x1, Pallas kernels, back(): pl.pallas_call(back_kernel, out_shape=(shape((width, 3 * width), bf16), s...  40.4 us
    pallas_call x1, Pallas kernels, front(): pl.pallas_call(front_kernel, out_shape=(shape((18, across, width), bf16),...  33.5 us
    unnamed x21, local copies, waits for them, and re-layouts  13.3 us

profile of v2, /device:TPU:0, one launch (start us, length us, event | category | flops | bytes accessed | tf_op | source)
XLA Modules:
  0.0 298.5 jit_solution(18076664248816548582)
XLA Ops:
  0.6 0.0 copy-start
  0.7 1.2 dynamic_slice.36
  3.9 1.2 dynamic_slice.38
  7.1 10.3 %copy.35 = bf16[768,4608]{0,1:T(8,128)(2,1)} copy(bf16[768,4608]{1,0:T(8,128)(2,1)} %param.20) | data formatting | bytes 14155776 | tf_op args[6]
  17.3 5.0 %fusion.17 = f32[1,6,768]{2,0,1:T(1,128)S(1)} fusion(bf16[6,768,768]{2,1,0:T(8,128)(2,1)} %bitcast.44, bf16[1000,768]{1,0:T(8,128)(2,1)} %param.19, s32[]{:T(128)S(6)} %select_n.34, bf16[1000,768]{1,0:T(8,128)(2,1)} %param.18, s32[]{:T(128)S(6)} %select_n.33), kind=kOutput, calls=%fused_computation.26 | convolution fusion | flops 7084032 | bytes 7102472 | tf_op jit(solution)/shard_map/dot_general | solution.py:1094
  22.3 1.4 add_convert_fusion
  23.7 0.1 pad.7.clone
  23.8 0.7 maximum_maximum_fusion.mod
  24.5 0.0 copy-done
  24.5 0.2 reshape.78
  24.7 0.2 copy.36
  24.9 0.1 reshape.79
  25.1 0.9 copy.37.lab_col
  25.9 0.6 broadcast_in_dim.16.lab_row
  26.5 33.5 %front.1 = (bf16[18,32,768]{2,1,0:T(8,128)(2,1)}, bf16[18,32,768]{2,1,0:T(8,128)(2,1)}, bf16[9,2,32,768]{3,2,1,0:T(8,128)(2,1)}, bf16[512,768]{1,0:T(8,128)(2,1)...) custom-call(bf16[2,8,32,768]{3,2,1,0:T(8,128)(2,1)} %x_in.1, ...), custom_call_target="tpu_custom_call" | custom-call | tf_op jit(solution)/shard_map/front/pallas_call | solution.py:277
  60.0 69.6 %feed.1 = (bf16[768,3072]{1,0:T(8,128)(2,1)}, bf16[3072,768]{1,0:T(8,128)(2,1)}, f32[16,3072]{1,0:T(8,128)}, bf16[512,768]{1,0:T(8,128)(2,1)}, f32[512,768]{1,0:...) custom-call(bf16[576,768]{1,0:T(8,128)(2,1)} %bitcast.52, bf16[576,768]{1,0:T(8,128)(2,1)} %bitcast.59, ...), custom_call_target="tpu_custom_call" | custom-call | flops 14495514624 | bytes 18874368 | tf_op jit(solution)/shard_map/feed/pallas_call | solution.py:475
  129.7 40.4 %back.1 = (bf16[768,2304]{1,0:T(8,128)(2,1)}, bf16[768,768]{1,0:T(8,128)(2,1)}, bf16[2,8,32,768]{3,2,1,0:T(8,128)(2,1)}, bf16[2,8,32,768]{3,2,1,0:T(8,128)(2,1)}, f32[16,768]{1,0:T(8,128)}, /*index=5*/f32[8,768]{1,0:T(8,128)}) custom-call(f32[512,768]{1,0:T(8,128)} %get-tuple-element.41.mid_in, bf16[8,2,32,768]{3,2,1,0:T(8,128)(2,1)} %bitcast.54, ...), custom_call_target="tpu_custom_call" | custom-call | tf_op jit(solution)/shard_map/back/pallas_call | solution.py:732
  170.0 108.9 %reduce_grads.1 = (bf16[96,2304]{1,0:T(8,128)(2,1)}, bf16[96,768]{1,0:T(8,128)(2,1)}, bf16[96,3072]{1,0:T(8,128)(2,1)}, bf16[4,96,768]{2,1,0:T(8,128)(2,1)}, f32...) custom-call(bf16[4,2,96,2304]{3,2,1,0:T(8,128)(2,1)} %bitcast.47, ...), custom_call_target="tpu_custom_call" | custom-call | tf_op jit(solution)/shard_map/reduce_grads/pallas_call | solution.py:1037
  278.9 0.0 copy-start.5
  278.9 1.1 copy.42
  280.1 0.8 slice.16
  280.9 0.1 copy.41
  281.0 1.3 fusion.3
  282.3 1.3 convolution_add_fusion
  283.6 2.1 fusion.15
  285.8 0.0 copy-done.5
  285.8 1.1 bitcast_convert_fusion
  286.9 0.0 copy-start.6
  286.9 0.0 copy-done.4
  286.9 1.1 convert_element_type.53
  288.0 0.0 copy-start.7
  288.0 0.0 copy-start.3
  288.0 2.0 fusion.12
  290.0 1.1 fusion.5
  291.2 0.0 copy-done.6
  291.2 0.0 copy-start.2
  291.2 1.0 convert_element_type.51
  292.2 1.1 fusion.6
  293.3 0.0 copy-start.1
  293.3 0.0 copy-done.7
  293.3 0.7 convert_element_type.52
  294.0 1.3 constant_dynamic-slice_fusion
  295.4 1.4 constant_dynamic-slice_fusion.1
  296.7 0.0 copy-done.3
  296.7 0.9 copy.47
  297.6 0.0 copy-done.2
  297.6 0.9 copy.48
  298.5 0.0 copy-done.1
  (9 shorter events, 0.1 us)
Async XLA Ops:
  0.6 23.8 %copy-start = (s32[2,1024]{1,0:T(2,128)S(1)}, s32[2,1024]{1,0:T(2,128)}, u32[]{:S(2)}) copy-start(s32[2,1024]{1,0:T(2,128)} %param.15) | copy-start | bytes 24580
  278.9 6.8 %copy-start.5 = (bf16[4,96,768]{2,1,0:T(8,128)(2,1)S(1)}, bf16[4,96,768]{2,1,0:T(8,128)(2,1)}, u32[]{:S(2)}) copy-start(bf16[4,96,768]{2,1,0:T(8,128)(2,1)} %get-tuple-element.64) | copy-start | bytes 1769476
  283.6 3.3 %copy-start.4 = (bf16[96,3072]{1,0:T(8,128)(2,1)S(1)}, bf16[96,3072]{1,0:T(8,128)(2,1)}, u32[]{:S(2)}) copy-start(bf16[96,3072]{1,0:T(8,128)(2,1)} %get-tuple-element.62) | copy-start | bytes 1769476
  286.9 4.3 %copy-start.6 = (bf16[96,2304]{1,0:T(8,128)(2,1)S(1)}, bf16[96,2304]{1,0:T(8,128)(2,1)}, u32[]{:S(2)}) copy-start(bf16[96,2304]{1,0:T(8,128)(2,1)} %get-tuple-element.59) | copy-start | bytes 1327108
  288.0 5.3 %copy-start.7 = (bf16[96,768]{1,0:T(8,128)(2,1)S(1)}, bf16[96,768]{1,0:T(8,128)(2,1)}, u32[]{:S(2)}) copy-start(bf16[96,768]{1,0:T(8,128)(2,1)} %get-tuple-element.60) | copy-start | bytes 442372
  288.0 8.7 %copy-start.3 = (bf16[2,8,32,768]{3,2,1,0:T(8,128)(2,1)S(1)}, bf16[2,8,32,768]{3,2,1,0:T(8,128)(2,1)}, u32[]{:S(2)}) copy-start(bf16[2,8,32,768]{3,2,1,0:T(8,128)(2,1)} %get-tuple-element.78) | copy-start | bytes 2359300
  291.2 6.4 %copy-start.2 = (bf16[2,8,32,768]{3,2,1,0:T(8,128)(2,1)S(1)}, bf16[2,8,32,768]{3,2,1,0:T(8,128)(2,1)}, u32[]{:S(2)}) copy-start(bf16[2,8,32,768]{3,2,1,0:T(8,128)(2,1)} %get-tuple-element.79) | copy-start | bytes 2359300
  293.3 5.2 %copy-start.1 = (s32[2,1024]{1,0:T(2,128)S(1)}, s32[2,1024]{1,0:T(2,128)}, u32[]{:S(2)}) copy-start(s32[2,1024]{1,0:T(2,128)} %param.15) | copy-start | bytes 24580

commit v3 on v2

v3 whole, which is shorter than its diff:
```python
from functools import partial

import jax
import jax.numpy as jnp
from jax import lax
from jax.experimental import pallas as pl
from jax.experimental.pallas import tpu as pltpu
from jax.sharding import PartitionSpec as P

HEADS = 12
MESH = pl.DeviceIdType.MESH
LANES = 128
f32 = jnp.float32
bf16 = jnp.bfloat16
highest = lax.Precision.HIGHEST


def dot_nn(a, b):
    return lax.dot_general(a, b, (((1,), (0,)), ((), ())), preferred_element_type=f32)


def dot_nt(a, b):
    return lax.dot_general(a, b, (((1,), (1,)), ((), ())), preferred_element_type=f32)


def dot_tn(a, b):
    return lax.dot_general(a, b, (((0,), (0,)), ((), ())), preferred_element_type=f32)


def remote(src, dst, send, recv, target):
    return pltpu.make_async_remote_copy(
        src_ref=src, dst_ref=dst, send_sem=send, recv_sem=recv, device_id=target,
        device_id_type=MESH,
    )


def meet(partners):
    barrier = pltpu.get_barrier_semaphore()
    for partner in partners:
        pl.semaphore_signal(barrier, inc=1, device_id=partner, device_id_type=MESH)
    pl.semaphore_wait(barrier, len(partners))


def normalize(values):
    center = values - jnp.mean(values, axis=-1, keepdims=True)
    second = jnp.mean(center * center, axis=-1, keepdims=True)
    scale = lax.rsqrt(second + 1e-06)
    return center * scale, scale


def normalize_back(grad, normal, scale):
    return scale * (
        grad
        - jnp.mean(grad, axis=-1, keepdims=True)
        - normal * jnp.mean(grad * normal, axis=-1, keepdims=True)
    )


def column_shifts(row):
    across = row.shape[0]
    column = lax.broadcasted_iota(jnp.int32, row.shape, 0)
    before = jnp.where(column == 0, 0.0, pltpu.roll(row, 1, 0))
    after = jnp.where(column == across - 1, 0.0, pltpu.roll(row, across - 1, 0))
    return before, after


def fold(values):
    rows, width = values.shape
    return jnp.sum(values.reshape(rows // 8, 8, width), axis=0)


def permutation(inverse):
    n = 512
    to = lax.broadcasted_iota(jnp.int32, (n, n), 1 if inverse else 0)
    source = lax.broadcasted_iota(jnp.int32, (n, n), 0 if inverse else 1)
    wanted = lax.shift_left(lax.shift_right_logical(to & 255, 4), 5) + 2 * (to & 15) + (
        lax.shift_right_logical(to, 8)
    )
    return jnp.where(source == wanted, 1.0, 0.0).astype(bf16)


def front_kernel(
    x_in, cot_in, names, moments, segments, kern, class_in, time_in, wmod_in, wqkv_in, wo_in,
    o_x, o_cot, o_ret, o_tok, o_proj, o_att, o_lse, o_bias, mod,
    xf, table, wmod, wqkv, wo, shifts, mixed, rows_m, perm, bias, tok, proj, att, lse, brm,
    load_sem, x_send, x_recv, c_send, c_recv, ex_send, ex_recv, own_sem, out_sem,
):
    b = lax.axis_index("batch")
    g = lax.axis_index("group")
    c, p = lax.rem(g, 2), g // 2
    core, side, corner = (b, g + 1 - 2 * c), (b, g + 2 - 4 * p), (b, 3 - g)
    inner = jnp.logical_or(g == 1, g == 2)
    width = xf.shape[-1]
    across = xf.shape[1]

    def spread_out(src, dst, send, recv, waiting):
        main = c * 8 + p * 2
        other_main = remote(
            src.at[1 - p], dst.at[pl.ds(main, 8)], send.at[0], recv.at[c], (b, 2 - p)
        )
        edge = 6 * (2 - g)
        edge_to = 16 * (g - 1)
        other_edge = remote(
            src.at[1 - p, pl.ds(edge, 2)], dst.at[pl.ds(edge_to, 2)], send.at[1], recv.at[2], side
        )
        own_main = remote(src.at[p], dst.at[pl.ds(main, 8)], send.at[2], recv.at[c], core)
        own_edge = pltpu.make_async_copy(
            src.at[p, pl.ds(edge, 2)], dst.at[pl.ds(edge_to, 2)], recv.at[2]
        )
        stay_main = pltpu.make_async_copy(src.at[p], dst.at[pl.ds(main, 8)], recv.at[c])
        if waiting:
            other_main.wait_send()

            @pl.when(inner)
            def _():
                other_edge.wait_send()
                own_main.wait_send()

        else:
            other_main.start()

            @pl.when(inner)
            def _():
                other_edge.start()
                own_main.start()
                own_edge.start()

            @pl.when(jnp.logical_not(inner))
            def _():
                stay_main.start()

    def arrived(dst, recv):
        for j in range(2):
            place = dst.at[pl.ds(8 * j + 2 * c, 8)]
            pltpu.make_async_copy(place, place, recv.at[j]).wait()
        place = dst.at[pl.ds(16 * (1 - c), 2)]
        pltpu.make_async_copy(place, place, recv.at[2]).wait()

    pieces = [
        (wqkv_in, wqkv), (wo_in, wo), (class_in, table.at[0]), (time_in, table.at[1]),
        (wmod_in, wmod),
    ]
    loads = [
        pltpu.make_async_copy(src, dst, load_sem.at[n]) for n, (src, dst) in enumerate(pieces)
    ]
    for n in (2, 3, 4, 0, 1):
        loads[n].start()
    meet([core, side, corner])
    spread_out(x_in, xf, x_send, x_recv, False)
    perm[0] = permutation(False)
    perm[1] = permutation(True)
    n = tok.shape[0]
    wide = segments.shape[1]
    to = lax.broadcasted_iota(jnp.int32, (n, wide), 0)
    source = lax.broadcasted_iota(jnp.int32, (n, wide), 1)
    wanted = lax.shift_left(2 * lax.shift_right_logical(to & 255, 4) + c, 5) + 2 * (to & 15) + (
        lax.shift_right_logical(to, 8)
    )
    chosen = source == wanted
    one_line = jnp.where(p == 0, segments[0:1, :], segments[1:2, :]).astype(f32)
    lines = jnp.broadcast_to(one_line, (8, wide)).astype(bf16)
    lab_row = dot_nt(lines, jnp.where(chosen, 1.0, 0.0).astype(bf16))
    lab_col = jnp.sum(jnp.where(chosen, one_line, 0.0), axis=-1, keepdims=True)
    for half in range(2):
        cut = slice(half * (n // 2), (half + 1) * (n // 2))
        bias[half] = jnp.where(lab_row[0:1, cut] == lab_col[cut], 0.0, -1e30)
    bias_out = pltpu.make_async_copy(bias, o_bias, out_sem.at[5])
    bias_out.start()
    name = jnp.where(p == 0, names[0], names[1])
    moment = jnp.where(p == 0, moments[0], moments[1])
    loads[2].wait()
    loads[3].wait()
    rows_all = lax.broadcasted_iota(jnp.int32, (8, table.shape[1]), 1)
    cond = dot_nn(jnp.where(rows_all == name, 1.0, 0.0).astype(bf16), table[0]) + dot_nn(
        jnp.where(rows_all == moment, 1.0, 0.0).astype(bf16), table[1]
    )
    cond_low = (cond / (1.0 + jnp.exp(-cond))).astype(bf16)
    loads[4].wait()
    for part in range(6):
        cut = slice(part * width, (part + 1) * width)
        mod[part : part + 1, :] = dot_nn(cond_low, wmod[:, cut])[0:1, :]
    lane_of = lax.broadcasted_iota(jnp.int32, (1, width), 1)
    mod[6:7, :] = jnp.where(
        lane_of == 0, name.astype(f32), jnp.where(lane_of == 1, moment.astype(f32), 0.0)
    )
    mod[7:8, :] = cond[0:1, :]
    arrived(xf, x_recv)
    spread_out(cot_in, o_cot, c_send, c_recv, False)
    x_out = pltpu.make_async_copy(xf, o_x, out_sem.at[0])
    x_out.start()

    shift = mod[0:1, :]
    scale = 1.0 + mod[1:2, :]

    def first(i, carry):
        normal, _ = normalize(xf[c + i].astype(f32))
        value = (normal * scale + shift).astype(bf16).astype(f32)
        before, after = column_shifts(value)
        shifts[0, 1 - c + i] = before
        shifts[1, 1 - c + i] = value
        shifts[2, 1 - c + i] = after
        return carry

    lax.fori_loop(0, 17, first, 0)
    for s in range(3):
        shifts[s, 17 * c] = jnp.zeros((across, width), f32)

    def conv(step, parity):
        o = 2 * step + parity
        for lane in range(0, width, LANES):
            cut = slice(lane, lane + LANES)
            total = jnp.zeros((across, LANES), f32)
            for r in range(3):
                for s in range(3):
                    tap = kern[3 * r + s : 3 * r + s + 1, cut].astype(f32)
                    total = total + tap * shifts[s, o + r, :, cut]
            mixed[step, parity, :, cut] = total.astype(bf16)

    def conv_away(step, carry):
        conv(step, 1 - c)
        return carry

    def conv_own(step, carry):
        conv(step, c)
        return carry

    lax.fori_loop(0, 8, conv_away, 0)
    mixed_away = remote(
        mixed.at[:, 1 - c], rows_m.at[pl.ds(8 * c, 8)], ex_send.at[0], ex_recv.at[0], core
    )
    mixed_away.start()
    lax.fori_loop(0, 8, conv_own, 0)
    mixed_own = pltpu.make_async_copy(mixed.at[:, c], rows_m.at[pl.ds(8 * c, 8)], own_sem.at[0])
    mixed_own.start()
    mixed_own.wait()
    mixed_away.wait()
    flat = rows_m[...].reshape(16 * across, width)
    tok[...] = dot_nn(perm[0], flat).astype(bf16)
    tok_out = pltpu.make_async_copy(tok, o_tok, out_sem.at[1])
    tok_out.start()
    loads[0].wait()
    for part in range(3):
        cut = slice(part * width, (part + 1) * width)
        proj[:, cut] = dot_nn(tok[...], wqkv[:, cut]).astype(bf16)
    proj_out = pltpu.make_async_copy(proj, o_proj, out_sem.at[2])
    proj_out.start()

    pairs = width // LANES
    size = tok.shape[0] // 2
    low_lane = lax.broadcasted_iota(jnp.int32, (size, LANES), 1) < LANES // 2
    lane_id = lax.broadcasted_iota(jnp.int32, (size, LANES), 1)
    zero = jnp.zeros((), bf16)

    def attend(index, carry):
        half, pair = index // pairs, lax.rem(index, pairs)
        rows = pl.ds(pl.multiple_of(half * size, size), size)

        def part(n):
            return proj[rows, pl.ds(pl.multiple_of(n * width + pair * LANES, LANES), LANES)]

        q, k, v = part(0) * jnp.asarray(0.125, bf16), part(1), part(2)
        total = jnp.zeros((size, LANES), f32)
        sums = lse[half]
        for h in range(2):
            mine = low_lane if h == 0 else jnp.logical_not(low_lane)
            scores = dot_nt(q, jnp.where(mine, k, zero)) + bias[half]
            top = jnp.max(scores, axis=-1, keepdims=True)
            powers = jnp.exp(scores - top)
            mass = jnp.sum(powers, axis=-1, keepdims=True)
            weights = (powers * (1.0 / mass)).astype(bf16)
            total = total + dot_nn(weights, jnp.where(mine, v, zero))
            sums = jnp.where(lane_id == 2 * pair + h, top + jnp.log(mass), sums)
        lse[half] = sums
        att[rows, pl.ds(pl.multiple_of(pair * LANES, LANES), LANES)] = total.astype(bf16)
        return carry

    lse[...] = jnp.zeros(lse.shape, f32)
    lax.fori_loop(0, 2 * pairs, attend, 0)
    att_out = pltpu.make_async_copy(att, o_att, out_sem.at[3])
    att_out.start()
    lse_out = pltpu.make_async_copy(lse, o_lse, out_sem.at[4])
    lse_out.start()
    loads[1].wait()
    branch = dot_nn(att[...], wo[...]).astype(bf16)
    brm[...] = dot_nn(perm[1], branch).astype(bf16).reshape(16, across, width)
    ret_away = remote(
        brm.at[pl.ds(7 * (1 - c), 9)], o_ret.at[:, c], ex_send.at[1], ex_recv.at[1], core
    )
    ret_away.start()
    ret_own = pltpu.make_async_copy(brm.at[pl.ds(7 * c, 9)], o_ret.at[:, c], own_sem.at[1])
    ret_own.start()
    for out in (x_out, tok_out, proj_out, att_out, lse_out, bias_out, ret_own):
        out.wait()
    ret_away.wait()
    spread_out(x_in, xf, x_send, x_recv, True)
    spread_out(cot_in, o_cot, c_send, c_recv, True)
    arrived(o_cot, c_recv)


def front(inputs, cotangent, names, moments, segments, kern, classes, times, wmod, wqkv, wo):
    across, width = inputs.shape[2], inputs.shape[3]
    tokens = 16 * across
    any_space = pl.BlockSpec(memory_space=pl.ANY)
    vmem = pl.BlockSpec(memory_space=pltpu.VMEM)
    smem = pl.BlockSpec(memory_space=pltpu.SMEM)
    shape = jax.ShapeDtypeStruct
    dma = pltpu.SemaphoreType.DMA
    return pl.pallas_call(
        front_kernel,
        out_shape=(
            shape((18, across, width), bf16),
            shape((18, across, width), bf16),
            shape((9, 2, across, width), bf16),
            shape((tokens, width), bf16),
            shape((tokens, 3 * width), bf16),
            shape((tokens, width), bf16),
            shape((2, tokens // 2, LANES), f32),
            shape((2, tokens // 2, tokens // 2), f32),
            shape((8, width), f32),
        ),
        in_specs=[any_space] * 2 + [smem] * 2 + [vmem] * 2 + [any_space] * 5,
        out_specs=[any_space] * 8 + [vmem],
        scratch_shapes=[
            pltpu.VMEM((18, across, width), bf16),
            pltpu.VMEM((2, *classes.shape), bf16),
            pltpu.VMEM(wmod.shape, bf16),
            pltpu.VMEM(wqkv.shape, bf16),
            pltpu.VMEM(wo.shape, bf16),
            pltpu.VMEM((3, 18, across, width), f32),
            pltpu.VMEM((8, 2, across, width), bf16),
            pltpu.VMEM((16, across, width), bf16),
            pltpu.VMEM((2, tokens, tokens), bf16),
            pltpu.VMEM((2, tokens // 2, tokens // 2), f32),
            pltpu.VMEM((tokens, width), bf16),
            pltpu.VMEM((tokens, 3 * width), bf16),
            pltpu.VMEM((tokens, width), bf16),
            pltpu.VMEM((2, tokens // 2, LANES), f32),
            pltpu.VMEM((16, across, width), bf16),
            dma((5,)), dma((3,)), dma((3,)), dma((3,)), dma((3,)), dma((2,)), dma((2,)),
            dma((2,)), dma((6,)),
        ],
        compiler_params=pltpu.CompilerParams(
            collective_id=1, has_side_effects=True, vmem_limit_bytes=60 << 20
        ),
        name="front",
    )(inputs, cotangent, names, moments, segments, kern, classes, times, wmod, wqkv, wo)


def gelu_parts(x):
    size = jnp.abs(x)
    t = 1.0 / (1.0 + (0.3275911 * 0.7071067811865476) * size)
    bell = jnp.exp(-0.5 * x * x)
    series = t * (
        0.254829592
        + t * (-0.284496736 + t * (1.421413741 + t * (-1.453152027 + t * 1.061405429)))
    )
    tail = 0.5 * series * bell
    mass = jnp.where(x >= 0, 1.0 - tail, tail)
    return x * mass, mass + x * bell * 0.3989422804014327


def feed_kernel(
    x_in, ret_in, cot_in, mod, up, kern, down,
    o_up, o_down, o_up_last, o_down_last, o_kern, o_res, o_mid, o_rg, o_small,
    feed_in, feed_t, btg, out_acc, back_acc, hid, hs, gs, act, slope, hg, wu, wd, ru, rd, xu, xd,
    u1_send, u1_recv, d1_send, d1_recv, u2_send, u2_recv, d2_send, d2_recv, u_out, d_out, l_out,
):
    j = pl.program_id(0)
    tiles = pl.num_programs(0)
    b = lax.axis_index("batch")
    g = lax.axis_index("group")
    c, p = lax.rem(g, 2), g // 2
    core, side = (b, g + 1 - 2 * c), (b, g + 2 - 4 * p)
    parts, grain = wd.shape[3], wd.shape[4]

    def up_1(t):
        return remote(wu.at[t, 1 - c], ru.at[t], u1_send.at[t], u1_recv.at[t], core)

    def down_1(t):
        return remote(wd.at[t, 1 - c], rd.at[t], d1_send.at[t], d1_recv.at[t], core)

    def up_2(t):
        return remote(wu.at[t, c, 1 - p], xu.at[t], u2_send.at[t], u2_recv.at[t], side)

    def down_2(t):
        return remote(wd.at[t, c, 1 - p], xd.at[t], d2_send.at[t], d2_recv.at[t], side)

    def up_store(t):
        spot = pl.ds(pl.multiple_of(t * LANES, LANES), LANES)
        return pltpu.make_async_copy(wu.at[t, c, p], o_up.at[:, spot], u_out.at[t])

    def down_store(t):
        return pltpu.make_async_copy(
            wd.at[t, c, p], o_down.at[pl.ds(t * parts, parts)], d_out.at[t]
        )

    def add_core(t):
        down_1(t).wait_recv()
        up_1(t).wait_recv()

        def step(i, carry):
            x, n = i // 8, lax.rem(i, 8)
            spot = pl.ds(pl.multiple_of(n * 96, 32), 96)
            wu[t, c, x, spot] = wu[t, c, x, spot] + ru[t, x, spot]
            for k in range(parts // 8):
                wd[t, c, x, n * (parts // 8) + k] = (
                    wd[t, c, x, n * (parts // 8) + k] + rd[t, x, n * (parts // 8) + k]
                )
            return carry

        lax.fori_loop(0, 16, step, 0)

    def add_side(t):
        down_2(t).wait_recv()
        up_2(t).wait_recv()

        def step(n, carry):
            spot = pl.ds(pl.multiple_of(n * 96, 32), 96)
            wu[t, c, p, spot] = wu[t, c, p, spot] + xu[t, spot]
            for k in range(parts // 8):
                wd[t, c, p, n * (parts // 8) + k] = (
                    wd[t, c, p, n * (parts // 8) + k] + xd[t, n * (parts // 8) + k]
                )
            return carry

        lax.fori_loop(0, 8, step, 0)
        up_store(t).start()
        down_store(t).start()
    across = 32
    width = feed_in.shape[1]
    tile = up.shape[1]
    frame_rows = feed_in.shape[0] // across
    own = pl.ds(pl.multiple_of(2 * c * across, 64), 16 * across)

    def middle_of(row):
        place = pl.ds(pl.multiple_of(row * across, across), across)
        returned = ret_in[place, :].astype(f32)
        return x_in[place, :].astype(f32) + mod[2:3, :] * returned, returned

    @pl.when(j == 0)
    def _():
        meet([core, side])

        def prepare(row, carry):
            place = pl.ds(pl.multiple_of(row * across, across), across)
            normal, _ = normalize(middle_of(row)[0])
            feed_in[place, :] = (normal * (1.0 + mod[4:5, :]) + mod[3:4, :]).astype(bf16)
            btg[place, :] = (mod[5:6, :] * cot_in[place, :].astype(f32)).astype(bf16)
            return carry

        lax.fori_loop(0, frame_rows, prepare, 0)
        feed_t[...] = feed_in[own, :].T
        out_acc[...] = jnp.zeros(out_acc.shape, f32)
        back_acc[...] = jnp.zeros(back_acc.shape, f32)
        for s in range(3):
            hs[s, 18 * c] = jnp.zeros((across, tile), f32)
            gs[s, 17 * c] = jnp.zeros((across, tile), f32)

    hid[...] = dot_nn(feed_in[...], up[...]).astype(bf16)

    def lay_hidden(row, carry):
        value = hid[pl.ds(pl.multiple_of(row * across, across), across), :].astype(f32)
        before, after = column_shifts(value)
        hs[0, 1 - c + row] = before
        hs[1, 1 - c + row] = value
        hs[2, 1 - c + row] = after
        return carry

    lax.fori_loop(0, frame_rows, lay_hidden, 0)

    for lane in range(0, tile, LANES):
        cut = slice(lane, lane + LANES)
        taps = [kern[n : n + 1, cut].astype(f32) for n in range(9)]

        def forward(row, carry):
            total = jnp.zeros((across, LANES), f32)
            for r in range(3):
                for s in range(3):
                    total = total + taps[3 * r + s] * hs[s, row + r, :, cut]
            place = pl.ds(pl.multiple_of(row * across, across), across)
            value, steep = gelu_parts(total)
            act[place, cut] = value.astype(bf16)
            slope[place, cut] = steep
            return carry

        lax.fori_loop(0, 17, forward, 0)

    @pl.when(j >= 1)
    def _():
        add_core(j - 1)
        up_2(j - 1).start()
        down_2(j - 1).start()

    inside = pl.ds(pl.multiple_of(c * across, across), 16 * across)
    around = pl.ds(pl.multiple_of(c * across, across), 17 * across)
    own_act = act[inside, :]
    out_acc[...] += dot_nn(own_act, down[...])
    grad_down = dot_tn(own_act, btg[own, :]).reshape(parts, 4, grain, width)
    for q in range(4):
        wd[j, q % 2, q // 2] = grad_down[:, q].astype(bf16)
    down_1(j).start()
    slope[...] = slope[...] * dot_nt(btg[around, :], down[...])

    def lay_grad(row, carry):
        value = slope[pl.ds(pl.multiple_of(row * across, across), across), :]
        value = value.astype(bf16).astype(f32)
        before, after = column_shifts(value)
        gs[0, 1 - c + row] = after
        gs[1, 1 - c + row] = value
        gs[2, 1 - c + row] = before
        return carry

    lax.fori_loop(0, 17, lay_grad, 0)

    for lane in range(0, tile, LANES):
        cut = slice(lane, lane + LANES)
        taps = [kern[n : n + 1, cut].astype(f32) for n in range(9)]

        def backward(row, sums):
            total = jnp.zeros((across, LANES), f32)
            value = hs[1, row + c + 1, :, cut]
            later = []
            for r in range(3):
                for s in range(3):
                    grad = gs[s, row + 2 - r, :, cut]
                    total = total + taps[3 * r + s] * grad
                    later.append(sums[3 * r + s] + fold(value * grad))
            hg[pl.ds(pl.multiple_of(row * across, across), across), cut] = total.astype(bf16)
            return tuple(later)

        sums = lax.fori_loop(
            0, 16, backward, tuple(jnp.zeros((8, LANES), f32) for _ in range(9))
        )
        for n in range(9):
            o_kern[n : n + 1, cut] = jnp.sum(sums[n], axis=0, keepdims=True)

    o_kern[9:16, :] = jnp.zeros((7, tile), f32)
    grad_up = dot_nn(feed_t[...], hg[...]).astype(bf16)
    for q in range(4):
        wu[j, q % 2, q // 2] = grad_up[:, q * LANES : (q + 1) * LANES]
    up_1(j).start()
    back_acc[...] += dot_nt(hg[...], up[...])

    @pl.when(j >= 1)
    def _():
        add_side(j - 1)

    @pl.when(j == tiles - 1)
    def _():
        def finish(row, sums):
            frame = row + 2 * c
            place = pl.ds(pl.multiple_of(row * across, across), across)
            at = pl.ds(pl.multiple_of(frame * across, across), across)
            middle, returned = middle_of(frame)
            cot = cot_in[at, :].astype(f32)
            branch = out_acc[place, :]
            o_res[place, :] = (middle + mod[5:6, :] * branch).astype(bf16)
            normal, scale = normalize(middle)
            grad = back_acc[place, :]
            mid = cot + normalize_back(grad * (1.0 + mod[4:5, :]), normal, scale)
            o_mid[place, :] = mid
            o_rg[place, :] = (mod[2:3, :] * mid).astype(bf16)
            terms = (mid * returned, grad, grad * normal, cot * branch)
            return tuple(total + fold(term) for total, term in zip(sums, terms))

        sums = lax.fori_loop(
            0, 16, finish, tuple(jnp.zeros((8, width), f32) for _ in range(4))
        )
        o_small[...] = jnp.zeros((8, width), f32)
        for n in range(4):
            o_small[n + 2 : n + 3, :] = jnp.sum(sums[n], axis=0, keepdims=True)
        add_core(j)
        last = (
            pltpu.make_async_copy(wu.at[j, c], o_up_last, l_out.at[0]),
            pltpu.make_async_copy(wd.at[j, c], o_down_last, l_out.at[1]),
        )
        for move in last:
            move.start()

        def settle(t, carry):
            up_2(t).wait_send()
            down_2(t).wait_send()
            up_1(t).wait_send()
            down_1(t).wait_send()
            up_store(t).wait()
            down_store(t).wait()
            return carry

        lax.fori_loop(0, tiles - 1, settle, 0)
        up_1(j).wait_send()
        down_1(j).wait_send()
        for move in last:
            move.wait()


def feed(x_frame, returned, cot_frame, mod, up, kern, down, grain):
    width, units = up.shape
    frame = x_frame.shape[0]
    across = frame // 18
    tokens = 16 * across
    shape = jax.ShapeDtypeStruct
    dma = pltpu.SemaphoreType.DMA
    any_space = pl.BlockSpec(memory_space=pl.ANY)
    tile = 4 * LANES
    tiles = units // tile
    parts = tile // (4 * grain)

    def still(*size):
        return pl.BlockSpec(size, lambda j: (0, 0), pipeline_mode=pl.Buffered(1))

    columns = pl.BlockSpec((width, tile), lambda j: (0, j))
    rows = pl.BlockSpec((tile, width), lambda j: (j, 0))
    work = 6 * 2 * tokens * width * units
    return pl.pallas_call(
        feed_kernel,
        grid=(units // tile,),
        out_shape=(
            shape((width, units // 4), bf16),
            shape((tiles * parts, grain, width), bf16),
            shape((2, width, LANES), bf16),
            shape((2, parts, grain, width), bf16),
            shape((16, units), f32),
            shape((tokens, width), bf16),
            shape((tokens, width), f32),
            shape((tokens, width), bf16),
            shape((8, width), f32),
        ),
        in_specs=[
            still(frame, width), still(frame, width), still(frame, width), still(8, width),
            columns, pl.BlockSpec((9, tile), lambda j: (0, j)), rows,
        ],
        out_specs=[
            *[any_space] * 4, pl.BlockSpec((16, tile), lambda j: (0, j)),
            still(tokens, width), still(tokens, width), still(tokens, width), still(8, width),
        ],
        scratch_shapes=[
            pltpu.VMEM((frame, width), bf16),
            pltpu.VMEM((width, tokens), bf16),
            pltpu.VMEM((frame, width), bf16),
            pltpu.VMEM((tokens, width), f32),
            pltpu.VMEM((tokens, width), f32),
            pltpu.VMEM((frame, tile), bf16),
            pltpu.VMEM((3, 19, across, tile), f32),
            pltpu.VMEM((3, 18, across, tile), f32),
            pltpu.VMEM((17 * across, tile), bf16),
            pltpu.VMEM((17 * across, tile), f32),
            pltpu.VMEM((tokens, tile), bf16),
            pltpu.VMEM((tiles, 2, 2, width, LANES), bf16),
            pltpu.VMEM((tiles, 2, 2, parts, grain, width), bf16),
            pltpu.VMEM((tiles, 2, width, LANES), bf16),
            pltpu.VMEM((tiles, 2, parts, grain, width), bf16),
            pltpu.VMEM((tiles, width, LANES), bf16),
            pltpu.VMEM((tiles, parts, grain, width), bf16),
            *[dma((tiles,)) for _ in range(10)],
            dma((2,)),
        ],
        compiler_params=pltpu.CompilerParams(
            dimension_semantics=("arbitrary",), collective_id=3, has_side_effects=True,
            vmem_limit_bytes=62 << 20,
        ),
        cost_estimate=pl.CostEstimate(
            flops=work, bytes_accessed=8 * width * units, transcendentals=tokens * units
        ),
        name="feed",
    )(x_frame, returned, cot_frame, mod, up, kern, down)


def back_kernel(
    mid_in, rg_in, tok_in, proj_in, att_in, lse, bias, x_in, mod, small, kern, wqkv_in, wo_in,
    res_in, uq_in, dq_in, ul_in, dl_in, kern_two,
    o_fu, o_fd, o_fp, o_res, o_ig, o_one, o_two, o_mg,
    mid, tok, tok_t, proj, att, xf, wqkv, wo, rows_m, perm, grad, datt, dproj,
    brm, frame, gs, value, agrad, ig,
    wp, p_r1, p_r2x, p_r2y, p_r3, p_r4, fin_p,
    fu, fd, fy_u, fy_d, fz_u, fz_d, fin_u, fin_d, lu, ld, lx_u, lx_d,
    mg_own, mg_r1, mg_all, kk_1, kr_1, kz_1, kk_2, kr_2, kz_2,
    load_sem, r_send, r_recv, i_send, i_recv, ex_send, ex_recv, own_sem, send_sem, recv_sem, out_sem,
):
    b = lax.axis_index("batch")
    g = lax.axis_index("group")
    nz = fu.shape[0]
    c, p = lax.rem(g, 2), g // 2
    yb, zb = lax.rem(b, 2), b // 2
    core, side, corner = (b, g + 1 - 2 * c), (b, g + 2 - 4 * p), (b, 3 - g)
    beside = (b + 1 - 2 * yb, g)
    others = [lax.rem(zb + d, nz) for d in range(nz)]
    far = [(2 * z + yb, g) for z in others]
    inner = jnp.logical_or(g == 1, g == 2)
    across, width = xf.shape[1], xf.shape[2]
    rows_own = fu.shape[2]
    pairs = width // LANES
    tokens = tok.shape[0]
    size = tokens // 2
    chunks = wp.shape[0]
    chunk = wp.shape[-1]
    lead = width - LANES
    per, parts = fd.shape[2], ld.shape[0]
    places = {}

    def link(name, src, dst, target):
        n = places.setdefault(name, len(places))
        return remote(src, dst, send_sem.at[n], recv_sem.at[n], target)

    def send_home(src, dst, send, recv, waiting):
        moves = [
            remote(
                src.at[pl.ds(8 * n, 8)], dst.at[p], send.at[n], recv.at[p], (b, 2 * c + n)
            )
            for n in range(2)
        ]
        away = remote(
            src.at[pl.ds(8 * (1 - c), 8)], dst.at[p], send.at[0], recv.at[p], core
        )
        stay = pltpu.make_async_copy(src.at[pl.ds(8 * c, 8)], dst.at[p], recv.at[p])

        @pl.when(inner)
        def _():
            for move in moves:
                if waiting:
                    move.wait_send()
                else:
                    move.start()

        @pl.when(jnp.logical_not(inner))
        def _():
            if waiting:
                away.wait_send()
            else:
                away.start()
                stay.start()

    def home(dst, recv):
        for n in range(2):
            pltpu.make_async_copy(dst.at[n], dst.at[n], recv.at[n]).wait()

    head, rest = pl.ds(0, lead), pl.ds(lead, LANES)

    def last_x():
        return [
            link("lu", ul_in.at[1 - p], lx_u, side),
            link("ld", dl_in.at[1 - p], lx_d, side),
        ]

    def fa_y():
        return [link("fay", fu.at[:, 1 - yb, :, head], fy_u.at[:, :, head], beside)]

    def fb_y():
        return [
            link("fby", fu.at[:, 1 - yb, :, rest], fy_u.at[:, :, rest], beside),
            link("fdy", fd.at[:, 1 - yb], fy_d, beside),
        ]

    def fa_z(d):
        return [link(f"faz{d}", fu.at[others[d], yb, :, head], fz_u.at[d - 1, :, head], far[d])]

    def fb_z(d):
        return [
            link(f"fbz{d}", fu.at[others[d], yb, :, rest], fz_u.at[d - 1, :, rest], far[d]),
            link(f"fdz{d}", fd.at[others[d], yb], fz_d.at[d - 1], far[d]),
        ]

    def f_side(mine):
        x = p if mine else 1 - p
        return [
            link("gux", fin_u.at[c, x], fin_u.at[c, x], side),
            link("gdx", fin_d.at[c, x], fin_d.at[c, x], side),
        ]

    def f_core(mine):
        x = c if mine else 1 - c
        return [
            link("guc", fin_u.at[x], fin_u.at[x], core),
            link("gdc", fin_d.at[x], fin_d.at[x], core),
        ]

    def start(moves):
        for move in moves:
            move.start()

    def come(moves):
        for move in moves:
            move.wait_recv()

    def gone(moves):
        for move in moves:
            move.wait_send()

    def place_last():
        for load in late:
            load.wait()
        come(last_x())

        def step(n, carry):
            z, y = n // 2, lax.rem(n, 2)
            fu[z, y, :, lead:] = lu[z, y] + lx_u[z, y]
            return carry

        lax.fori_loop(0, 2 * nz, step, 0)
        for t in range(parts):
            spot = 2 * nz * per - parts + t
            owner = spot // per
            fd[owner // 2, owner % 2, spot % per] = ld[t] + lx_d[t]
        start(fb_y())

    def fa_y_add():
        come(fa_y())

        def step(z, carry):
            fu[z, yb, :, :lead] = fu[z, yb, :, :lead] + fy_u[z, :, :lead]
            return carry

        lax.fori_loop(0, nz, step, 0)
        for d in range(1, nz):
            start(fa_z(d))

    def fb_y_add():
        come(fb_y())

        def step(z, carry):
            fu[z, yb, :, lead:] = fu[z, yb, :, lead:] + fy_u[z, :, lead:]
            fd[z, yb] = fd[z, yb] + fy_d[z]
            return carry

        lax.fori_loop(0, nz, step, 0)
        for d in range(1, nz):
            start(fb_z(d))

    def f_sum():
        total_u = fu[zb, yb].astype(f32)
        total_d = fd[zb, yb].astype(f32)
        for d in range(1, nz):
            come(fa_z(d))
            come(fb_z(d))
            total_u = total_u + fz_u[d - 1].astype(f32)
            total_d = total_d + fz_d[d - 1].astype(f32)
        fin_u[c, p] = total_u.astype(bf16)
        fin_d[c, p] = total_d.astype(bf16)
        start(f_side(True))

    def f_side_done():
        come(f_side(False))
        start(f_core(True))

    def f_core_done():
        come(f_core(False))
        start(f_out)

    f_out = [
        pltpu.make_async_copy(fin_u, o_fu, out_sem.at[0]),
        pltpu.make_async_copy(fin_d, o_fd, out_sem.at[1]),
    ]
    p_out = pltpu.make_async_copy(fin_p, o_fp, out_sem.at[2])
    mg_out = pltpu.make_async_copy(mg_all, o_mg, out_sem.at[3])

    def side_first(k):
        return k == 0

    def p1(k):
        return link(f"p1{k}", wp.at[k, 1 - c], p_r1.at[k], core)

    def p2(k):
        if side_first(k):
            return link(f"p2{k}", wp.at[k, c, 1 - p], p_r2x.at[k], side)
        return link(f"p2{k}", wp.at[k, c, :, :, 1 - yb], p_r2y.at[k], beside)

    def p3(k):
        if side_first(k):
            return link(f"p3{k}", wp.at[k, c, p, :, 1 - yb], p_r3.at[k], beside)
        return link(f"p3{k}", wp.at[k, c, 1 - p, :, yb], p_r3.at[k], side)

    def p4(k, d):
        return link(
            f"p4{k}{d}", wp.at[k, c, p, others[d], yb], p_r4.at[k, d - 1], far[d]
        )

    def p_side(k, mine):
        x = p if mine else 1 - p
        return link(f"p5{k}", fin_p.at[k, c, x], fin_p.at[k, c, x], side)

    def p_core(k, mine):
        x = c if mine else 1 - c
        return link(f"p6{k}", fin_p.at[k, x], fin_p.at[k, x], core)

    def p_add_1(k):
        p1(k).wait_recv()

        def step(i, carry):
            x, z, y = i // (2 * nz), lax.rem(i // 2, nz), lax.rem(i, 2)
            wp[k, c, x, z, y] = wp[k, c, x, z, y] + p_r1[k, x, z, y]
            return carry

        lax.fori_loop(0, 4 * nz, step, 0)
        p2(k).start()

    def p_add_2(k):
        p2(k).wait_recv()

        def step(i, carry):
            if side_first(k):
                z, y = i // 2, lax.rem(i, 2)
                wp[k, c, p, z, y] = wp[k, c, p, z, y] + p_r2x[k, z, y]
            else:
                x, z = i // nz, lax.rem(i, nz)
                wp[k, c, x, z, yb] = wp[k, c, x, z, yb] + p_r2y[k, x, z]
            return carry

        lax.fori_loop(0, 2 * nz, step, 0)
        p3(k).start()

    def p_add_3(k):
        p3(k).wait_recv()

        def step(z, carry):
            wp[k, c, p, z, yb] = wp[k, c, p, z, yb] + p_r3[k, z]
            return carry

        lax.fori_loop(0, nz, step, 0)
        for d in range(1, nz):
            p4(k, d).start()

    def p_add_4(k):
        total = wp[k, c, p, zb, yb].astype(f32)
        for d in range(1, nz):
            p4(k, d).wait_recv()
            total = total + p_r4[k, d - 1].astype(f32)
        fin_p[k, c, p] = total.astype(bf16)
        p_side(k, True).start()

    def p_pass(k):
        p_side(k, False).wait_recv()
        p_core(k, True).start()

    peers = [core, side, beside]

    def kern_copy(name, kk, kr, stage):
        return link(f"{name}{stage}", kk.at[stage], kr.at[stage], peers[stage])

    def kern_far(name, kk, kz, d):
        return link(f"{name}z{d}", kk.at[3], kz.at[d - 1], far[d])

    def kern_step(name, kk, kr, kz, stage):
        kern_copy(name, kk, kr, stage).wait_recv()
        kk[stage + 1] = (kk[stage].astype(f32) + kr[stage].astype(f32)).astype(bf16)
        if stage < 2:
            kern_copy(name, kk, kr, stage + 1).start()
        else:
            for d in range(1, nz):
                kern_far(name, kk, kz, d).start()

    def kern_sum(name, kk, kz, out):
        total = kk[3].astype(f32)
        for d in range(1, nz):
            kern_far(name, kk, kz, d).wait_recv()
            total = total + kz[d - 1].astype(f32)
        out[...] = total

    one = ("one", kk_1, kr_1, kz_1)
    two = ("two", kk_2, kr_2, kz_2)

    def mg_copy(stage, mine=True):
        if stage == 0:
            return link("mg0", mg_own, mg_r1, core)
        x = p if mine else 1 - p
        y = yb if mine else 1 - yb
        place = mg_all.at[zb, yb, x] if stage == 1 else mg_all.at[zb, y]
        return link(f"mg{stage}", place, place, peers[stage])

    def mg_far(d, z):
        return link(f"mgz{d}", mg_all.at[z], mg_all.at[z], far[d])

    pieces = [
        (wo_in, wo), (att_in, att), (tok_in, tok), (proj_in, proj), (wqkv_in, wqkv), (x_in, xf),
        (mid_in, mid),
    ]
    loads = [
        pltpu.make_async_copy(src, dst, load_sem.at[n]) for n, (src, dst) in enumerate(pieces)
    ]
    full = dq_in.shape[0] - parts
    early = [pltpu.make_async_copy(uq_in.at[:, :, :, head], fu.at[:, :, :, head], load_sem.at[7])]
    late = [
        pltpu.make_async_copy(ul_in.at[p], lu, load_sem.at[8]),
        pltpu.make_async_copy(dl_in.at[p], ld, load_sem.at[9]),
    ]
    for owner in range(2 * nz):
        count = min(per, full - owner * per)
        if count > 0:
            late.append(
                pltpu.make_async_copy(
                    dq_in.at[pl.ds(owner * per, count)],
                    fd.at[owner // 2, owner % 2, pl.ds(0, count)],
                    load_sem.at[10 + owner],
                )
            )
    for load in (*early, *loads, *late):
        load.start()
    kk_2[0] = kern_two[...].astype(bf16)
    meet([core, side, corner, beside, *far[1:]])
    grad_away = remote(
        rg_in.at[:, 1 - c], rows_m.at[pl.ds(8 * c, 8)], ex_send.at[0], ex_recv.at[0], core
    )
    grad_away.start()
    grad_own = pltpu.make_async_copy(rg_in.at[:, c], rows_m.at[pl.ds(8 * c, 8)], own_sem.at[0])
    grad_own.start()
    start(last_x())
    early[0].wait()
    start(fa_y())
    kern_copy("two", kk_2, kr_2, 0).start()
    perm[0] = permutation(False)
    perm[1] = permutation(True)
    grad_own.wait()
    grad_away.wait()
    grad[...] = dot_nn(perm[0], rows_m[...].reshape(tokens, width)).astype(bf16)
    loads[0].wait()
    loads[1].wait()
    datt[...] = dot_nt(grad[...], wo[...]).astype(bf16)
    out_grad = dot_tn(att[...], grad[...])
    for k in range(chunks):
        cut = slice(k * chunk, (k + 1) * chunk)
        wp[k, 1, 1] = out_grad[:, cut].reshape(nz, 2, rows_own, chunk).astype(bf16)
    loads[2].wait()
    tok_t[...] = tok[...].T
    loads[3].wait()
    place_last()
    send_home(res_in, o_res, r_send, r_recv, False)
    kern_step(*two, 0)

    low_lane = lax.broadcasted_iota(jnp.int32, (size, LANES), 1) < LANES // 2
    lane_id = lax.broadcasted_iota(jnp.int32, (size, LANES), 1)
    zero = jnp.zeros((), bf16)

    def attend(index, carry):
        pair, half = index // 2, lax.rem(index, 2)
        rows = pl.ds(pl.multiple_of(half * size, size), size)

        def cut(n):
            return pl.ds(pl.multiple_of(n * width + pair * LANES, LANES), LANES)

        q = proj[rows, cut(0)] * jnp.asarray(0.125, bf16)
        k, v, up = proj[rows, cut(1)], proj[rows, cut(2)], datt[rows, cut(0)]
        sums = lse[half]
        dq = jnp.zeros((size, LANES), f32)
        dk = jnp.zeros((size, LANES), f32)
        dv = jnp.zeros((size, LANES), f32)
        for h in range(2):
            mine = low_lane if h == 0 else jnp.logical_not(low_lane)
            key = jnp.where(mine, k, zero)
            scores = dot_nt(q, key) + bias[half]
            mass = jnp.sum(
                jnp.where(lane_id == 2 * pair + h, sums, 0.0), axis=-1, keepdims=True
            )
            weights = jnp.exp(scores - mass)
            pull = dot_nt(up, jnp.where(mine, v, zero))
            mean = jnp.sum(weights * pull, axis=-1, keepdims=True)
            spare = (weights * (pull - mean)).astype(bf16)
            dq = dq + dot_nn(spare, key)
            dk = dk + dot_tn(spare, jnp.where(mine, q, zero))
            dv = dv + dot_tn(weights.astype(bf16), jnp.where(mine, up, zero))
        dproj[rows, cut(0)] = (dq * 0.125).astype(bf16)
        dproj[rows, cut(1)] = dk.astype(bf16)
        dproj[rows, cut(2)] = dv.astype(bf16)
        return carry

    def weigh(k):
        for q in range(3):
            span = slice(q * width + k * chunk, q * width + (k + 1) * chunk)
            part = dot_nn(tok_t[...], dproj[:, span])
            wp[k, q % 2, q // 2] = part.reshape(nz, 2, rows_own, chunk).astype(bf16)
        p1(k).start()

    lax.fori_loop(0, 2, attend, 0)
    fa_y_add()
    kern_step(*two, 1)
    lax.fori_loop(2, 4, attend, 0)
    weigh(0)
    fb_y_add()
    kern_step(*two, 2)
    lax.fori_loop(4, 6, attend, 0)
    p_add_1(0)
    lax.fori_loop(6, 8, attend, 0)
    weigh(1)
    f_sum()
    kern_sum("two", kk_2, kz_2, o_two)
    lax.fori_loop(8, 10, attend, 0)
    p_add_1(1)
    p_add_2(0)
    f_side_done()
    lax.fori_loop(10, 12, attend, 0)
    weigh(2)
    loads[4].wait()
    back = dot_nt(dproj[...], wqkv[...]).astype(bf16)
    brm[...] = dot_nn(perm[1], back).astype(bf16).reshape(16, across, width)
    mixed_away = remote(
        brm.at[pl.ds(7 * (1 - c), 9)], frame.at[:, c], ex_send.at[1], ex_recv.at[1], core
    )
    mixed_away.start()
    mixed_own = pltpu.make_async_copy(brm.at[pl.ds(7 * c, 9)], frame.at[:, c], own_sem.at[1])
    mixed_own.start()
    p_add_1(2)
    p_add_3(0)
    p_add_2(1)
    f_core_done()
    loads[5].wait()
    loads[6].wait()

    shift = mod[0:1, :]
    scale_in = 1.0 + mod[1:2, :]

    def again(row, carry):
        normal, _ = normalize(xf[2 * c + row].astype(f32))
        value[row] = (normal * scale_in + shift).astype(bf16).astype(f32)
        return carry

    lax.fori_loop(0, 16, again, 0)
    mixed_own.wait()
    mixed_away.wait()

    def lay(row, carry):
        at = c + row
        line = frame[at // 2, lax.rem(at, 2)].astype(f32)
        before, after = column_shifts(line)
        gs[0, 1 - c + row] = after
        gs[1, 1 - c + row] = line
        gs[2, 1 - c + row] = before
        return carry

    lax.fori_loop(0, 17, lay, 0)
    for s in range(3):
        gs[s, 17 * c] = jnp.zeros((across, width), f32)

    kk_1[0] = jnp.zeros((16, width), bf16)

    def conv_back(lane):
        span = slice(lane, lane + LANES)
        taps = [kern[n : n + 1, span].astype(f32) for n in range(9)]

        def backward(row, sums):
            total = jnp.zeros((across, LANES), f32)
            own = value[row, :, span]
            later = []
            for r in range(3):
                for s in range(3):
                    line = gs[s, row + 2 - r, :, span]
                    total = total + taps[3 * r + s] * line
                    later.append(sums[3 * r + s] + fold(own * line))
            agrad[row, :, span] = total
            return tuple(later)

        sums = lax.fori_loop(
            0, 16, backward, tuple(jnp.zeros((8, LANES), f32) for _ in range(9))
        )
        rows9 = [jnp.sum(sums[n], axis=0, keepdims=True) for n in range(9)]
        kk_1[0, :, span] = jnp.concatenate(rows9 + [jnp.zeros((7, LANES), f32)]).astype(bf16)

    for lane in range(0, width // 2, LANES):
        conv_back(lane)
    p_add_4(0)
    p_add_3(1)
    p_add_2(2)
    for lane in range(width // 2, width, LANES):
        conv_back(lane)
    kern_copy("one", kk_1, kr_1, 0).start()

    def finish(row, sums):
        normal, scale = normalize(xf[2 * c + row].astype(f32))
        line = agrad[row]
        place = pl.ds(pl.multiple_of(row * across, across), across)
        total = mid[place, :] + normalize_back(line * scale_in, normal, scale)
        ig[row] = total.astype(bf16)
        return (sums[0] + fold(line), sums[1] + fold(line * normal))

    sums = lax.fori_loop(0, 16, finish, tuple(jnp.zeros((8, width), f32) for _ in range(2)))
    send_home(ig, o_ig, i_send, i_recv, False)
    mg_own[...] = small[...]
    for n in range(2):
        mg_own[n : n + 1, :] = jnp.sum(sums[n], axis=0, keepdims=True)
    mg_own[6:8, :] = mod[6:8, :]
    mg_copy(0).start()
    kern_step(*one, 0)
    p_pass(0)
    p_add_4(1)
    mg_copy(0).wait_recv()
    mg_all[zb, yb, p] = mg_own[...] + mg_r1[...]
    mg_copy(1).start()
    p_add_3(2)
    kern_step(*one, 1)
    mg_copy(1, False).wait_recv()
    mg_copy(2).start()
    p_pass(1)
    kern_step(*one, 2)
    mg_copy(2, False).wait_recv()
    for d in range(1, nz):
        mg_far(d, zb).start()
    p_add_4(2)
    p_core(0, False).wait_recv()
    p_core(1, False).wait_recv()
    p_pass(2)
    kern_sum("one", kk_1, kz_1, o_one)
    for d in range(1, nz):
        mg_far(d, lax.rem(zb + nz - d, nz)).wait_recv()
    mg_out.start()
    p_core(2, False).wait_recv()
    p_out.start()
    gone([*last_x(), *fa_y(), *fb_y(), *f_side(True), *f_core(True)])
    for d in range(1, nz):
        gone([*fa_z(d), *fb_z(d), mg_far(d, zb)])
        gone([kern_far("one", kk_1, kz_1, d), kern_far("two", kk_2, kz_2, d)])
    for k in range(chunks):
        gone([p1(k), p2(k), p3(k), p_side(k, True), p_core(k, True)])
        gone([p4(k, d) for d in range(1, nz)])
    for stage in range(3):
        gone([mg_copy(stage)])
        gone([kern_copy("one", kk_1, kr_1, stage), kern_copy("two", kk_2, kr_2, stage)])
    send_home(res_in, o_res, r_send, r_recv, True)
    send_home(ig, o_ig, i_send, i_recv, True)
    home(o_res, r_recv)
    home(o_ig, i_recv)
    for out in (*f_out, p_out, mg_out):
        out.wait()


def back(
    mid, rg, tok, proj, att, lse, bias, x_frame, mod, small, kern, wqkv, wo, res,
    uq, dq, ul, dl, kern_two,
):
    nb = lax.axis_size("batch")
    nz = nb // 2
    across, width = x_frame.shape[1], x_frame.shape[2]
    tokens = 16 * across
    rows = width // nb
    grain = dq.shape[1]
    parts = dl.shape[1]
    per = dq.shape[0] // nb
    chunks, chunk = 3, 2 * LANES
    many = max(nz - 1, 1)
    any_space = pl.BlockSpec(memory_space=pl.ANY)
    vmem = pl.BlockSpec(memory_space=pltpu.VMEM)
    shape = jax.ShapeDtypeStruct
    dma = pltpu.SemaphoreType.DMA
    wide = kern_two.shape[1]
    links = 80 + 12 * many

    def low(*dims):
        return pltpu.VMEM(dims, bf16)

    def high(*dims):
        return pltpu.VMEM(dims, f32)

    return pl.pallas_call(
        back_kernel,
        out_shape=(
            shape((2, 2, rows, width), bf16),
            shape((2, 2, per, grain, width), bf16),
            shape((chunks, 2, 2, rows, chunk), bf16),
            shape((2, 8, across, width), bf16),
            shape((2, 8, across, width), bf16),
            shape((16, width), f32),
            shape((16, wide), f32),
            shape((nz, 2, 2, 8, width), f32),
        ),
        in_specs=[any_space] * 5 + [vmem, vmem, any_space, vmem, vmem, vmem] + [any_space] * 7
        + [vmem],
        out_specs=[any_space] * 5 + [vmem, vmem, any_space],
        scratch_shapes=[
            high(tokens, width), low(tokens, width), low(width, tokens), low(tokens, 3 * width),
            low(tokens, width), low(18, across, width), low(*wqkv.shape), low(*wo.shape),
            low(16, across, width), low(2, tokens, tokens), low(tokens, width),
            low(tokens, width), low(tokens, 3 * width),
            low(16, across, width), low(9, 2, across, width), high(3, 18, across, width),
            high(16, across, width), high(16, across, width), low(16, across, width),
            low(chunks, 2, 2, nz, 2, rows, chunk), low(chunks, 2, nz, 2, rows, chunk),
            low(chunks, nz, 2, rows, chunk), low(chunks, 2, nz, rows, chunk),
            low(chunks, nz, rows, chunk), low(chunks, many, rows, chunk),
            low(chunks, 2, 2, rows, chunk),
            low(nz, 2, rows, width), low(nz, 2, per, grain, width),
            low(nz, rows, width), low(nz, per, grain, width),
            low(many, rows, width), low(many, per, grain, width),
            low(2, 2, rows, width), low(2, 2, per, grain, width),
            low(nz, 2, rows, LANES), low(parts, grain, width),
            low(nz, 2, rows, LANES), low(parts, grain, width),
            high(8, width), high(8, width), high(nz, 2, 2, 8, width),
            low(4, 16, width), low(3, 16, width), low(many, 16, width),
            low(4, 16, wide), low(3, 16, wide), low(many, 16, wide),
            dma((10 + nb,)), dma((2,)), dma((2,)), dma((2,)), dma((2,)), dma((2,)), dma((2,)),
            dma((2,)), dma((links,)), dma((links,)), dma((4,)),
        ],
        compiler_params=pltpu.CompilerParams(
            collective_id=2, has_side_effects=True, vmem_limit_bytes=63 << 20
        ),
        name="back",
    )(
        mid, rg, tok, proj, att, lse, bias, x_frame, mod, small, kern, wqkv, wo, res,
        uq, dq, ul, dl, kern_two,
    )


def tail_kernel(
    fu, fd, fp, mg, one, two, wm_in,
    o_class, o_time, o_mod, o_proj, o_out, o_one, o_up, o_two, o_down,
    wm, load_sem,
):
    b = lax.axis_index("batch")
    width = mg.shape[2]
    canvases = mg.shape[0]
    own = o_mod.shape[0]
    whole = wm_in.shape[0] == own
    source = wm_in if whole else wm_in.at[pl.ds(pl.multiple_of(b * own, 16), own)]
    load = pltpu.make_async_copy(source, wm, load_sem)
    load.start()
    chunks, chunk = fp.shape[0], fp.shape[4]
    per, grain = fd.shape[2], fd.shape[3]
    for q in range(4):
        for j in range(width // LANES):
            at = (4 * j + q) * LANES
            o_up[:, at : at + LANES] = fu[q % 2, q // 2, :, j * LANES : (j + 1) * LANES].astype(f32)
        for i in range(per):
            at = (4 * i + q) * grain
            o_down[at : at + grain, :] = fd[q % 2, q // 2, i].astype(f32)
        for k in range(chunks):
            part = fp[k, q % 2, q // 2].astype(f32)
            if q < 3:
                o_proj[:, q * width + k * chunk : q * width + (k + 1) * chunk] = part
            else:
                o_out[:, k * chunk : (k + 1) * chunk] = part

    def window(values, n):
        size = values.shape[1]
        return pltpu.roll(values, lax.rem(size - b * n, size), 1)[:, :n]

    o_one[...] = window(one[...], own)[0:9]
    o_two[...] = window(two[...], o_two.shape[1])[0:9]
    every = mg[...]
    cond = window(every[:, 7, :] * 0.5, own)
    sigma = 1.0 / (1.0 + jnp.exp(-cond))
    low = (cond * sigma).astype(bf16).astype(f32)
    steep = sigma * (1.0 + cond * (1.0 - sigma))
    act_grad = jnp.zeros((canvases, own), f32)
    load.wait()
    for part in range(6):
        span = slice(part * width, (part + 1) * width)
        line = every[:, part, :]
        o_mod[:, span] = lax.dot_general(
            low, line, (((0,), (0,)), ((), ())), precision=highest, preferred_element_type=f32
        )
        act_grad = act_grad + lax.dot_general(
            line, wm[:, span].astype(f32), (((1,), (1,)), ((), ())), precision=highest,
            preferred_element_type=f32,
        )
    cond_grad = act_grad * steep
    names = every[:, 6, :] * 0.5
    kinds = o_class.shape[0]
    spot = lax.broadcasted_iota(jnp.int32, (canvases, kinds), 1).astype(f32)
    for n, out in enumerate((o_class, o_time)):
        hot = jnp.where(spot == names[:, n : n + 1], 1.0, 0.0)
        out[...] = lax.dot_general(
            hot, cond_grad, (((0,), (0,)), ((), ())), precision=highest,
            preferred_element_type=f32,
        )


def tail(fu, fd, fp, mg, one, two, wmod, classes, times):
    nb = lax.axis_size("batch")
    width = mg.shape[2]
    own = width // nb
    wide = two.shape[1] // nb
    if own % 16:
        wmod = lax.dynamic_slice_in_dim(wmod, lax.axis_index("batch") * own, own, axis=0)
    any_space = pl.BlockSpec(memory_space=pl.ANY)
    vmem = pl.BlockSpec(memory_space=pltpu.VMEM)
    shape = jax.ShapeDtypeStruct
    return pl.pallas_call(
        tail_kernel,
        out_shape=(
            shape((classes, own), f32),
            shape((times, own), f32),
            shape((own, 6 * width), f32),
            shape((own, 3 * width), f32),
            shape((own, width), f32),
            shape((9, own), f32),
            shape((own, 4 * width), f32),
            shape((9, wide), f32),
            shape((4 * fd.shape[2] * fd.shape[3], width), f32),
        ),
        in_specs=[vmem] * 6 + [any_space],
        out_specs=[vmem] * 9,
        scratch_shapes=[pltpu.VMEM((own, 6 * width), bf16), pltpu.SemaphoreType.DMA],
        compiler_params=pltpu.CompilerParams(vmem_limit_bytes=60 << 20),
        name="tail",
    )(fu, fd, fp, mg, one, two, wmod)


def body(
    inputs,
    segments,
    class_labels,
    time_steps,
    class_table,
    time_table,
    modulation_weight,
    project_weight,
    output_weight,
    kernel_attention,
    up_weight,
    kernel_feed,
    down_weight,
    cotangent,
):
    across, width = inputs.shape[2], inputs.shape[3]
    nb = lax.axis_size("batch")
    nz = nb // 2
    rows = width // nb
    units = up_weight.shape[1]
    grain = 16 if (units // nb) % 64 == 0 else 8
    x_frame, cot_frame, returned, tok, proj, att, lse, bias, mod = front(
        inputs, cotangent, class_labels, time_steps, segments, kernel_attention, class_table,
        time_table, modulation_weight, project_weight, output_weight,
    )
    flat = (18 * across, width)
    uq, dq, ul, dl, kern_two, res, mid, rg, small = feed(
        x_frame.reshape(flat), returned.reshape(flat), cot_frame.reshape(flat), mod, up_weight,
        kernel_feed, down_weight, grain,
    )
    fu, fd, fp, result, inputs_gradient, one, two, gathered = back(
        mid, rg.reshape(8, 2, across, width), tok, proj, att, lse, bias, x_frame, mod, small,
        kernel_attention, project_weight, output_weight, res.reshape(16, across, width),
        uq.reshape(nz, 2, rows, width), dq, ul.reshape(2, nz, 2, rows, LANES), dl, kern_two,
    )
    (
        class_total, time_total, modulation_total, project_total, output_total,
        attention_kernel_total, up_total, feed_kernel_total, down_total,
    ) = tail(
        fu, fd, fp, gathered.reshape(2 * nb, 8, width), one, two, modulation_weight,
        class_table.shape[0], time_table.shape[0],
    )
    return (
        result,
        inputs_gradient,
        class_total,
        time_total,
        modulation_total,
        project_total,
        output_total,
        attention_kernel_total,
        up_total,
        feed_kernel_total,
        down_total,
    )


def solution(mesh):
    in_specs = (
        P("batch", "group", None, None),
        P("batch", None),
        P("batch"),
        P("batch"),
        P(),
        P(),
        P(),
        P(),
        P(),
        P(),
        P(),
        P(),
        P(),
        P("batch", "group", None, None),
    )
    out_specs = (
        P("batch", "group", None, None),
        P("batch", "group", None, None),
        P(None, "batch"),
        P(None, "batch"),
        P("batch", None),
        P("batch", None),
        P("batch", None),
        P(None, "batch"),
        P("batch", None),
        P(None, "batch"),
        P("batch", None),
    )
    return jax.shard_map(body, mesh=mesh, in_specs=in_specs, out_specs=out_specs, check_vma=False)
```

time: 300 us -> 254 us (0.85)
  local copies, waits for them, and re-layouts: 21.5 us -> 5.83 us
  matrix products: 13.9 us -> 0 us
  other arithmetic: 6.02 us -> 0 us
  Pallas kernels: 252 us -> 248 us
  between operations: 4.66 us -> 0.7 us
    pallas_call x2, Pallas kernels: 149 us -> 119 us  [the longest x1 109 us: back(): pl.pallas_call(back_kernel, out_shape=(shape((2, 2, rows, width), bf16),...]
    pallas_call x1, Pallas kernels: 69.6 us -> 94 us  [feed(): pl.pallas_call(feed_kernel, grid=(units // tile,), out_shape=(shape((widt...]
    dot_general x7 -> x0, matrix products: 13.9 us -> none  [the longest x1 4.95 us: body(): jnp.dot(cond_low, modulation_weight, preferred_element_type=f32)]
    unnamed x21 -> x8, local copies, waits for them, and re-layouts: 13.3 us -> 5.83 us
    convert_element_type x6 -> x0, other arithmetic: 5.34 us -> none  [the longest x1 1.39 us: body(): named = jnp.stack([label, moment]).astype(f32)]
    dynamic_slice x6 -> x0, local copies, waits for them, and re-layouts: 5.24 us -> none  [the longest x1 1.39 us: body(): lax.dynamic_slice(kernel_one, (0, place_b * own), (9, own)).astype(f32)]
where the time goes in v3:
time: 254 us
  Pallas kernels  248 us (98%)
  local copies, waits for them, and re-layouts  5.83 us (2%)
    pallas_call x1, Pallas kernels, back(): pl.pallas_call(back_kernel, out_shape=(shape((2, 2, rows, width), bf16),...  109 us
    pallas_call x1, Pallas kernels, feed(): pl.pallas_call(feed_kernel, grid=(units // tile,), out_shape=(shape((widt...  94 us
    pallas_call x1, Pallas kernels, front(): pl.pallas_call(front_kernel, out_shape=(shape((18, across, width), bf16),...  34.3 us
    pallas_call x1, Pallas kernels, tail(): pl.pallas_call(tail_kernel, out_shape=(shape((classes, own), f32), shape(...  10.1 us
    unnamed x8, local copies, waits for them, and re-layouts  5.83 us

profile of v3, /device:TPU:0, one launch (start us, length us, event | category | flops | bytes accessed | tf_op | source)
XLA Modules:
  0.0 254.1 jit_solution(7570858337007796966)
XLA Ops:
  0.6 34.3 %front.1 = (bf16[18,32,768]{2,1,0:T(8,128)(2,1)}, bf16[18,32,768]{2,1,0:T(8,128)(2,1)}, bf16[9,2,32,768]{3,2,1,0:T(8,128)(2,1)}, bf16[512,768]{1,0:T(8,128)(2,1)...) custom-call(bf16[2,8,32,768]{3,2,1,0:T(8,128)(2,1)} %x_in.1, ...), custom_call_target="tpu_custom_call" | custom-call | tf_op jit(solution)/shard_map/front/pallas_call | solution.py:308
  34.9 94.0 %feed.1 = (bf16[768,768]{1,0:T(8,128)(2,1)}, bf16[48,16,768]{2,1,0:T(8,128)(2,1)}, bf16[2,768,128]{2,1,0:T(8,128)(2,1)}, bf16[2,8,16,768]{3,2,1,0:T(8,128)(2,1)}...) custom-call(bf16[576,768]{1,0:T(8,128)(2,1)} %bitcast.9, ...), custom_call_target="tpu_custom_call" | custom-call | flops 14495514624 | bytes 18874368 | tf_op jit(solution)/shard_map/feed/pallas_call | solution.py:614
  129.0 109.2 %back.1 = (bf16[2,2,96,768]{3,2,1,0:T(8,128)(2,1)}, bf16[2,2,6,16,768]{4,3,2,1,0:T(8,128)(2,1)}, bf16[3,2,2,96,256]{4,3,2,1,0:T(8,128)(2,1)}, bf16[2,8,32,768]{3...) custom-call(f32[512,768]{1,0:T(8,128)} %get-tuple-element.50.mid_in,, ...), custom_call_target="tpu_custom_call" | custom-call | tf_op jit(solution)/shard_map/back/pallas_call | solution.py:1248
  238.2 10.1 %tail.1 = (f32[1000,96]{1,0:T(8,128)}, f32[1000,96]{1,0:T(8,128)}, f32[96,4608]{1,0:T(8,128)}, f32[96,2304]{1,0:T(8,128)}, f32[96,768]{1,0:T(8,128)}, /*index=5*...) custom-call(bf16[2,2,96,768]{3,2,1,0:T(8,128)(2,1)} %get-tuple-element.66.fu, ...), custom_call_target="tpu_custom_call" | custom-call | tf_op jit(solution)/shard_map/tail/pallas_call | solution.py:1370
  248.3 0.0 copy-start.1
  248.3 0.0 copy-start
  248.3 2.1 copy.25
  250.4 2.0 copy.26
  252.4 0.0 copy-done.1
  252.4 0.9 copy.29
  253.2 0.0 copy-done
  253.3 0.9 copy.30
Async XLA Ops:
  248.3 4.1 %copy-start.1 = (bf16[2,8,32,768]{3,2,1,0:T(8,128)(2,1)S(1)}, bf16[2,8,32,768]{3,2,1,0:T(8,128)(2,1)}, u32[]{:S(2)}) copy-start(bf16[2,8,32,768]{3,2,1,0:T(8,128)(2,1)} %get-tuple-element.103) | copy-start | bytes 2359300
  248.3 5.0 %copy-start = (bf16[2,8,32,768]{3,2,1,0:T(8,128)(2,1)S(1)}, bf16[2,8,32,768]{3,2,1,0:T(8,128)(2,1)}, u32[]{:S(2)}) copy-start(bf16[2,8,32,768]{3,2,1,0:T(8,128)(2,1)} %get-tuple-element.104) | copy-start | bytes 2359300

commit v4 on v3

--- a/solution.py
+++ b/solution.py
@@ -361,17 +361,23 @@
 
 def feed_kernel(
     x_in, ret_in, cot_in, mod, up, kern, down,
-    o_up, o_down, o_up_last, o_down_last, o_kern, o_res, o_mid, o_rg, o_small,
-    feed_in, feed_t, btg, out_acc, back_acc, hid, hs, gs, act, slope, hg, wu, wd, ru, rd, xu, xd,
-    u1_send, u1_recv, d1_send, d1_recv, u2_send, u2_recv, d2_send, d2_recv, u_out, d_out, l_out,
+    o_up, o_down, o_up_half, o_up_last, o_down_last, o_kern, o_res, o_mid, o_rg, o_small,
+    feed_in, feed_t, btg, out_acc, back_acc, hid, hs, gs, act, slope, hg,
+    wu, wd, ru, rd, yu, xu, zu, fin, xd,
+    u1_send, u1_recv, u2_send, u2_recv, u3_send, u3_recv, d1_send, d1_recv, d2_send, d2_recv,
+    u4_send, u4_recv, u_out, d_out, l_out,
 ):
     j = pl.program_id(0)
     tiles = pl.num_programs(0)
     b = lax.axis_index("batch")
     g = lax.axis_index("group")
     c, p = lax.rem(g, 2), g // 2
-    core, side = (b, g + 1 - 2 * c), (b, g + 2 - 4 * p)
-    parts, grain = wd.shape[3], wd.shape[4]
+    nz = wu.shape[3]
+    yb, zb = lax.rem(b, 2), b // 2
+    core, side, beside = (b, g + 1 - 2 * c), (b, g + 2 - 4 * p), (b + 1 - 2 * yb, g)
+    others = [lax.rem(zb + d, nz) for d in range(nz)]
+    far = [(2 * z + yb, g) for z in others]
+    parts = wd.shape[3]
 
     def up_1(t):
         return remote(wu.at[t, 1 - c], ru.at[t], u1_send.at[t], u1_recv.at[t], core)
@@ -380,14 +386,23 @@
         return remote(wd.at[t, 1 - c], rd.at[t], d1_send.at[t], d1_recv.at[t], core)
 
     def up_2(t):
-        return remote(wu.at[t, c, 1 - p], xu.at[t], u2_send.at[t], u2_recv.at[t], side)
+        return remote(wu.at[t, c, :, :, 1 - yb], yu.at[t], u2_send.at[t], u2_recv.at[t], beside)
 
     def down_2(t):
         return remote(wd.at[t, c, 1 - p], xd.at[t], d2_send.at[t], d2_recv.at[t], side)
 
+    def up_3(t):
+        return remote(wu.at[t, c, 1 - p, :, yb], xu.at[t], u3_send.at[t], u3_recv.at[t], side)
+
+    def up_4(t, d):
+        return remote(
+            wu.at[t, c, p, others[d], yb], zu.at[t, d - 1], u4_send.at[t, d - 1],
+            u4_recv.at[t, d - 1], far[d],
+        )
+
     def up_store(t):
         spot = pl.ds(pl.multiple_of(t * LANES, LANES), LANES)
-        return pltpu.make_async_copy(wu.at[t, c, p], o_up.at[:, spot], u_out.at[t])
+        return pltpu.make_async_copy(fin.at[t], o_up.at[:, spot], u_out.at[t])
 
     def down_store(t):
         return pltpu.make_async_copy(
@@ -399,24 +414,55 @@
         up_1(t).wait_recv()
 
         def step(i, carry):
+            x, z, y = i // (2 * nz), lax.rem(i // 2, nz), lax.rem(i, 2)
+            wu[t, c, x, z, y] = wu[t, c, x, z, y] + ru[t, x, z, y]
+            return carry
+
+        lax.fori_loop(0, 4 * nz, step, 0)
+
+        def step_down(i, carry):
             x, n = i // 8, lax.rem(i, 8)
-            spot = pl.ds(pl.multiple_of(n * 96, 32), 96)
-            wu[t, c, x, spot] = wu[t, c, x, spot] + ru[t, x, spot]
             for k in range(parts // 8):
                 wd[t, c, x, n * (parts // 8) + k] = (
                     wd[t, c, x, n * (parts // 8) + k] + rd[t, x, n * (parts // 8) + k]
                 )
             return carry
 
-        lax.fori_loop(0, 16, step, 0)
+        lax.fori_loop(0, 16, step_down, 0)
+
+    def add_beside(t):
+        up_2(t).wait_recv()
+
+        def step(i, carry):
+            x, z = i // nz, lax.rem(i, nz)
+            wu[t, c, x, z, yb] = wu[t, c, x, z, yb] + yu[t, x, z]
+            return carry
+
+        lax.fori_loop(0, 2 * nz, step, 0)
 
     def add_side(t):
+        up_3(t).wait_recv()
+
+        def step(z, carry):
+            wu[t, c, p, z, yb] = wu[t, c, p, z, yb] + xu[t, z]
+            return carry
+
+        lax.fori_loop(0, nz, step, 0)
+        for d in range(1, nz):
+            up_4(t, d).start()
+
+    def add_far(t):
+        total = wu[t, c, p, zb, yb].astype(f32)
+        for d in range(1, nz):
+            up_4(t, d).wait_recv()
+            total = total + zu[t, d - 1].astype(f32)
+        fin[t] = total.astype(bf16)
+        up_store(t).start()
+
+    def add_side_down(t):
         down_2(t).wait_recv()
-        up_2(t).wait_recv()
 
         def step(n, carry):
-            spot = pl.ds(pl.multiple_of(n * 96, 32), 96)
-            wu[t, c, p, spot] = wu[t, c, p, spot] + xu[t, spot]
             for k in range(parts // 8):
                 wd[t, c, p, n * (parts // 8) + k] = (
                     wd[t, c, p, n * (parts // 8) + k] + xd[t, n * (parts // 8) + k]
@@ -424,8 +470,8 @@
             return carry
 
         lax.fori_loop(0, 8, step, 0)
-        up_store(t).start()
         down_store(t).start()
+
     across = 32
     width = feed_in.shape[1]
     tile = up.shape[1]
@@ -439,7 +485,7 @@
 
     @pl.when(j == 0)
     def _():
-        meet([core, side])
+        meet([core, side, beside, *far[1:]])
 
         def prepare(row, carry):
             place = pl.ds(pl.multiple_of(row * across, across), across)
@@ -485,17 +531,26 @@
 
         lax.fori_loop(0, 17, forward, 0)
 
+    @pl.when(j >= 2)
+    def _():
+        add_side(j - 2)
+        add_side_down(j - 2)
+
     @pl.when(j >= 1)
     def _():
         add_core(j - 1)
         up_2(j - 1).start()
         down_2(j - 1).start()
 
+    @pl.when(j >= 3)
+    def _():
+        add_far(j - 3)
+
     inside = pl.ds(pl.multiple_of(c * across, across), 16 * across)
     around = pl.ds(pl.multiple_of(c * across, across), 17 * across)
     own_act = act[inside, :]
     out_acc[...] += dot_nn(own_act, down[...])
-    grad_down = dot_tn(own_act, btg[own, :]).reshape(parts, 4, grain, width)
+    grad_down = dot_tn(own_act, btg[own, :]).reshape(parts, 4, wd.shape[4], width)
     for q in range(4):
         wd[j, q % 2, q // 2] = grad_down[:, q].astype(bf16)
     down_1(j).start()
@@ -535,15 +590,17 @@
             o_kern[n : n + 1, cut] = jnp.sum(sums[n], axis=0, keepdims=True)
 
     o_kern[9:16, :] = jnp.zeros((7, tile), f32)
-    grad_up = dot_nn(feed_t[...], hg[...]).astype(bf16)
+    grad_up = dot_nn(feed_t[...], hg[...])
     for q in range(4):
-        wu[j, q % 2, q // 2] = grad_up[:, q * LANES : (q + 1) * LANES]
+        part = grad_up[:, q * LANES : (q + 1) * LANES]
+        wu[j, q % 2, q // 2] = part.reshape(nz, 2, wu.shape[5], LANES).astype(bf16)
     up_1(j).start()
     back_acc[...] += dot_nt(hg[...], up[...])
 
-    @pl.when(j >= 1)
+    @pl.when(jnp.logical_and(j >= 1, j < tiles - 1))
     def _():
-        add_side(j - 1)
+        add_beside(j - 1)
+        up_3(j - 1).start()
 
     @pl.when(j == tiles - 1)
     def _():
@@ -569,24 +626,37 @@
         o_small[...] = jnp.zeros((8, width), f32)
         for n in range(4):
             o_small[n + 2 : n + 3, :] = jnp.sum(sums[n], axis=0, keepdims=True)
+        add_far(j - 2)
+        add_beside(j - 1)
+        half = pltpu.make_async_copy(wu.at[j - 1, c, :, :, yb], o_up_half, l_out.at[2])
+        half.start()
+        add_side_down(j - 1)
         add_core(j)
         last = (
+            half,
             pltpu.make_async_copy(wu.at[j, c], o_up_last, l_out.at[0]),
             pltpu.make_async_copy(wd.at[j, c], o_down_last, l_out.at[1]),
         )
-        for move in last:
+        for move in last[1:]:
             move.start()
 
         def settle(t, carry):
+            up_3(t).wait_send()
+            for d in range(1, nz):
+                up_4(t, d).wait_send()
+            up_store(t).wait()
+            return carry
+
+        def settle_more(t, carry):
             up_2(t).wait_send()
             down_2(t).wait_send()
             up_1(t).wait_send()
             down_1(t).wait_send()
-            up_store(t).wait()
             down_store(t).wait()
             return carry
 
-        lax.fori_loop(0, tiles - 1, settle, 0)
+        lax.fori_loop(0, tiles - 2, settle, 0)
+        lax.fori_loop(0, tiles - 1, settle_more, 0)
         up_1(j).wait_send()
         down_1(j).wait_send()
         for move in last:
@@ -604,6 +674,10 @@
     tile = 4 * LANES
     tiles = units // tile
     parts = tile // (4 * grain)
+    nb = lax.axis_size("batch")
+    nz = nb // 2
+    own = width // nb
+    many = max(nz - 1, 1)
 
     def still(*size):
         return pl.BlockSpec(size, lambda j: (0, 0), pipeline_mode=pl.Buffered(1))
@@ -615,9 +689,10 @@
         feed_kernel,
         grid=(units // tile,),
         out_shape=(
-            shape((width, units // 4), bf16),
+            shape((own, (tiles - 2) * LANES), bf16),
             shape((tiles * parts, grain, width), bf16),
-            shape((2, width, LANES), bf16),
+            shape((2, nz, own, LANES), bf16),
+            shape((2, nz, 2, own, LANES), bf16),
             shape((2, parts, grain, width), bf16),
             shape((16, units), f32),
             shape((tokens, width), bf16),
@@ -630,7 +705,7 @@
             columns, pl.BlockSpec((9, tile), lambda j: (0, j)), rows,
         ],
         out_specs=[
-            *[any_space] * 4, pl.BlockSpec((16, tile), lambda j: (0, j)),
+            *[any_space] * 5, pl.BlockSpec((16, tile), lambda j: (0, j)),
             still(tokens, width), still(tokens, width), still(tokens, width), still(8, width),
         ],
         scratch_shapes=[
@@ -645,14 +720,17 @@
             pltpu.VMEM((17 * across, tile), bf16),
             pltpu.VMEM((17 * across, tile), f32),
             pltpu.VMEM((tokens, tile), bf16),
-            pltpu.VMEM((tiles, 2, 2, width, LANES), bf16),
+            pltpu.VMEM((tiles, 2, 2, nz, 2, own, LANES), bf16),
             pltpu.VMEM((tiles, 2, 2, parts, grain, width), bf16),
-            pltpu.VMEM((tiles, 2, width, LANES), bf16),
+            pltpu.VMEM((tiles, 2, nz, 2, own, LANES), bf16),
             pltpu.VMEM((tiles, 2, parts, grain, width), bf16),
-            pltpu.VMEM((tiles, width, LANES), bf16),
+            pltpu.VMEM((tiles, 2, nz, own, LANES), bf16),
+            pltpu.VMEM((tiles, nz, own, LANES), bf16),
+            pltpu.VMEM((tiles, many, own, LANES), bf16),
+            pltpu.VMEM((tiles, own, LANES), bf16),
             pltpu.VMEM((tiles, parts, grain, width), bf16),
             *[dma((tiles,)) for _ in range(10)],
-            dma((2,)),
+            dma((tiles, many)), dma((tiles, many)), dma((tiles,)), dma((tiles,)), dma((3,)),
         ],
         compiler_params=pltpu.CompilerParams(
             dimension_semantics=("arbitrary",), collective_id=3, has_side_effects=True,
@@ -667,13 +745,13 @@
 
 def back_kernel(
     mid_in, rg_in, tok_in, proj_in, att_in, lse, bias, x_in, mod, small, kern, wqkv_in, wo_in,
-    res_in, uq_in, dq_in, ul_in, dl_in, kern_two,
-    o_fu, o_fd, o_fp, o_res, o_ig, o_one, o_two, o_mg,
+    res_in, ud_in, dq_in, uh_in, ul_in, dl_in, kern_two,
+    o_fu, o_fd, o_fp, o_res, o_ig, o_one, o_two, o_mg, o_ml,
     mid, tok, tok_t, proj, att, xf, wqkv, wo, rows_m, perm, grad, datt, dproj,
     brm, frame, gs, value, agrad, ig,
     wp, p_r1, p_r2x, p_r2y, p_r3, p_r4, fin_p,
-    fu, fd, fy_u, fy_d, fz_u, fz_d, fin_u, fin_d, lu, ld, lx_u, lx_d,
-    mg_own, mg_r1, mg_all, kk_1, kr_1, kz_1, kk_2, kr_2, kz_2,
+    fu, fd, fz_u, fy_d, fz_d, fin_u, fin_d, ld, lx_d, hx, ly, ly_r, lx,
+    mg_own, mg_r1, mg_all, ml_own, ml_r1, ml_all, taps_sum, kk_1, kr_1, kz_1, kk_2, kr_2, kz_2,
     load_sem, r_send, r_recv, i_send, i_recv, ex_send, ex_recv, own_sem, send_sem, recv_sem, out_sem,
 ):
     b = lax.axis_index("batch")
@@ -687,13 +765,13 @@
     far = [(2 * z + yb, g) for z in others]
     inner = jnp.logical_or(g == 1, g == 2)
     across, width = xf.shape[1], xf.shape[2]
-    rows_own = fu.shape[2]
+    rows_own = fu.shape[1]
     pairs = width // LANES
     tokens = tok.shape[0]
     size = tokens // 2
     chunks = wp.shape[0]
     chunk = wp.shape[-1]
-    lead = width - LANES
+    lead = width - 2 * LANES
     per, parts = fd.shape[2], ld.shape[0]
     places = {}
 
@@ -701,159 +779,151 @@
         n = places.setdefault(name, len(places))
         return remote(src, dst, send_sem.at[n], recv_sem.at[n], target)
 
-    def send_home(src, dst, send, recv, waiting):
-        moves = [
-            remote(
-                src.at[pl.ds(8 * n, 8)], dst.at[p], send.at[n], recv.at[p], (b, 2 * c + n)
-            )
-            for n in range(2)
-        ]
-        away = remote(
-            src.at[pl.ds(8 * (1 - c), 8)], dst.at[p], send.at[0], recv.at[p], core
-        )
-        stay = pltpu.make_async_copy(src.at[pl.ds(8 * c, 8)], dst.at[p], recv.at[p])
+    def send_home(n, src, dst, send, recv, waiting):
+        move = remote(src.at[pl.ds(8 * n, 8)], dst.at[p], send.at[n], recv.at[p], (b, 2 * c + n))
+        away = remote(src.at[pl.ds(8 * n, 8)], dst.at[p], send.at[n], recv.at[p], core)
+        stay = pltpu.make_async_copy(src.at[pl.ds(8 * n, 8)], dst.at[p], recv.at[p])
 
         @pl.when(inner)
         def _():
-            for move in moves:
-                if waiting:
-                    move.wait_send()
-                else:
-                    move.start()
-
-        @pl.when(jnp.logical_not(inner))
+            if waiting:
+                move.wait_send()
+            else:
+                move.start()
+
+        @pl.when(jnp.logical_and(jnp.logical_not(inner), c != n))
         def _():
             if waiting:
                 away.wait_send()
             else:
                 away.start()
+
+        if not waiting:
+
+            @pl.when(jnp.logical_and(jnp.logical_not(inner), c == n))
+            def _():
                 stay.start()
 
     def home(dst, recv):
         for n in range(2):
             pltpu.make_async_copy(dst.at[n], dst.at[n], recv.at[n]).wait()
 
-    head, rest = pl.ds(0, lead), pl.ds(lead, LANES)
-
-    def last_x():
-        return [
-            link("lu", ul_in.at[1 - p], lx_u, side),
-            link("ld", dl_in.at[1 - p], lx_d, side),
-        ]
-
-    def fa_y():
-        return [link("fay", fu.at[:, 1 - yb, :, head], fy_u.at[:, :, head], beside)]
-
-    def fb_y():
-        return [
-            link("fby", fu.at[:, 1 - yb, :, rest], fy_u.at[:, :, rest], beside),
-            link("fdy", fd.at[:, 1 - yb], fy_d, beside),
-        ]
-
-    def fa_z(d):
-        return [link(f"faz{d}", fu.at[others[d], yb, :, head], fz_u.at[d - 1, :, head], far[d])]
-
-    def fb_z(d):
-        return [
-            link(f"fbz{d}", fu.at[others[d], yb, :, rest], fz_u.at[d - 1, :, rest], far[d]),
-            link(f"fdz{d}", fd.at[others[d], yb], fz_d.at[d - 1], far[d]),
-        ]
-
-    def f_side(mine):
-        x = p if mine else 1 - p
-        return [
-            link("gux", fin_u.at[c, x], fin_u.at[c, x], side),
-            link("gdx", fin_d.at[c, x], fin_d.at[c, x], side),
-        ]
-
-    def f_core(mine):
-        x = c if mine else 1 - c
-        return [
-            link("guc", fin_u.at[x], fin_u.at[x], core),
-            link("gdc", fin_d.at[x], fin_d.at[x], core),
-        ]
-
-    def start(moves):
-        for move in moves:
-            move.start()
-
-    def come(moves):
-        for move in moves:
-            move.wait_recv()
-
     def gone(moves):
         for move in moves:
             move.wait_send()
 
+    def half_x():
+        return link("hx", uh_in.at[1 - p], hx, side)
+
+    def last_y():
+        return link("ly", ul_in.at[:, :, 1 - yb], ly_r, beside)
+
+    def last_x():
+        return link("lx", ly.at[1 - p], lx, side)
+
+    def last_d():
+        return link("ld", dl_in.at[1 - p], lx_d, side)
+
+    def down_y():
+        return link("fdy", fd.at[:, 1 - yb], fy_d, beside)
+
+    def up_z(d):
+        return link(f"fuz{d}", fu.at[others[d]], fz_u.at[d - 1], far[d])
+
+    def down_z(d):
+        return link(f"fdz{d}", fd.at[others[d], yb], fz_d.at[d - 1], far[d])
+
+    def to_side(name, fin, mine):
+        x = p if mine else 1 - p
+        return link(f"{name}x", fin.at[c, x], fin.at[c, x], side)
+
+    def to_core(name, fin, mine):
+        x = c if mine else 1 - c
+        return link(f"{name}c", fin.at[x], fin.at[x], core)
+
+    def half_add():
+        early[0].wait()
+        half_x().wait_recv()
+
+        def step(z, carry):
+            fu[z, :, :LANES] = fu[z, :, :LANES] + hx[z]
+            return carry
+
+        lax.fori_loop(0, nz, step, 0)
+
+    def last_y_add():
+        early[1].wait()
+        last_y().wait_recv()
+
+        def step(i, carry):
+            x, z = i // nz, lax.rem(i, nz)
+            ly[x, z] = ly[x, z] + ly_r[x, z]
+            return carry
+
+        lax.fori_loop(0, 2 * nz, step, 0)
+        last_x().start()
+
+    def last_x_add():
+        last_x().wait_recv()
+
+        def step(z, carry):
+            fu[z, :, LANES:] = ly[p, z] + lx[z]
+            return carry
+
+        lax.fori_loop(0, nz, step, 0)
+        for d in range(1, nz):
+            up_z(d).start()
+
+    def up_sum():
+        early[2].wait()
+        total = fu[zb].astype(f32)
+        for d in range(1, nz):
+            up_z(d).wait_recv()
+            total = total + fz_u[d - 1].astype(f32)
+        fin_u[c, p, :, lead:] = total.astype(bf16)
+        to_side("gu", fin_u, True).start()
+
     def place_last():
         for load in late:
             load.wait()
-        come(last_x())
-
-        def step(n, carry):
-            z, y = n // 2, lax.rem(n, 2)
-            fu[z, y, :, lead:] = lu[z, y] + lx_u[z, y]
-            return carry
-
-        lax.fori_loop(0, 2 * nz, step, 0)
+        last_d().wait_recv()
         for t in range(parts):
             spot = 2 * nz * per - parts + t
             owner = spot // per
             fd[owner // 2, owner % 2, spot % per] = ld[t] + lx_d[t]
-        start(fb_y())
-
-    def fa_y_add():
-        come(fa_y())
+        down_y().start()
+
+    def down_y_add():
+        down_y().wait_recv()
 
         def step(z, carry):
-            fu[z, yb, :, :lead] = fu[z, yb, :, :lead] + fy_u[z, :, :lead]
+            fd[z, yb] = fd[z, yb] + fy_d[z]
             return carry
 
         lax.fori_loop(0, nz, step, 0)
         for d in range(1, nz):
-            start(fa_z(d))
-
-    def fb_y_add():
-        come(fb_y())
-
-        def step(z, carry):
-            fu[z, yb, :, lead:] = fu[z, yb, :, lead:] + fy_u[z, :, lead:]
-            fd[z, yb] = fd[z, yb] + fy_d[z]
-            return carry
-
-        lax.fori_loop(0, nz, step, 0)
+            down_z(d).start()
+
+    def down_sum():
+        total = fd[zb, yb].astype(f32)
         for d in range(1, nz):
-            start(fb_z(d))
-
-    def f_sum():
-        total_u = fu[zb, yb].astype(f32)
-        total_d = fd[zb, yb].astype(f32)
-        for d in range(1, nz):
-            come(fa_z(d))
-            come(fb_z(d))
-            total_u = total_u + fz_u[d - 1].astype(f32)
-            total_d = total_d + fz_d[d - 1].astype(f32)
-        fin_u[c, p] = total_u.astype(bf16)
-        fin_d[c, p] = total_d.astype(bf16)
-        start(f_side(True))
-
-    def f_side_done():
-        come(f_side(False))
-        start(f_core(True))
-
-    def f_core_done():
-        come(f_core(False))
-        start(f_out)
-
-    f_out = [
-        pltpu.make_async_copy(fin_u, o_fu, out_sem.at[0]),
-        pltpu.make_async_copy(fin_d, o_fd, out_sem.at[1]),
-    ]
+            down_z(d).wait_recv()
+            total = total + fz_d[d - 1].astype(f32)
+        fin_d[c, p] = total.astype(bf16)
+        to_side("gd", fin_d, True).start()
+
+    def pass_on(name, fin):
+        to_side(name, fin, False).wait_recv()
+        to_core(name, fin, True).start()
+
+    u_out = pltpu.make_async_copy(fin_u, o_fu, out_sem.at[0])
+    d_out = pltpu.make_async_copy(fin_d, o_fd, out_sem.at[1])
     p_out = pltpu.make_async_copy(fin_p, o_fp, out_sem.at[2])
     mg_out = pltpu.make_async_copy(mg_all, o_mg, out_sem.at[3])
+    ml_out = pltpu.make_async_copy(ml_all, o_ml, out_sem.at[4])
 
     def side_first(k):
-        return k == 0
+        return k % 2 == 0
 
     def p1(k):
         return link(f"p1{k}", wp.at[k, 1 - c], p_r1.at[k], core)
@@ -957,16 +1027,35 @@
     one = ("one", kk_1, kr_1, kz_1)
     two = ("two", kk_2, kr_2, kz_2)
 
-    def mg_copy(stage, mine=True):
+    def mg_copy(part, stage, mine=True):
+        name, own, first, every = part
         if stage == 0:
-            return link("mg0", mg_own, mg_r1, core)
+            return link(f"{name}0", own, first, core)
         x = p if mine else 1 - p
         y = yb if mine else 1 - yb
-        place = mg_all.at[zb, yb, x] if stage == 1 else mg_all.at[zb, y]
-        return link(f"mg{stage}", place, place, peers[stage])
-
-    def mg_far(d, z):
-        return link(f"mgz{d}", mg_all.at[z], mg_all.at[z], far[d])
+        place = every.at[zb, yb, x] if stage == 1 else every.at[zb, y]
+        return link(f"{name}{stage}", place, place, peers[stage])
+
+    def mg_far(part, d, z):
+        return link(f"{part[0]}z{d}", part[3].at[z], part[3].at[z], far[d])
+
+    def mg_step(part, stage):
+        name, own, first, every = part
+        mg_copy(part, stage, False).wait_recv()
+        if stage == 0:
+            every[zb, yb, p] = own[...] + first[...]
+        if stage < 2:
+            mg_copy(part, stage + 1).start()
+        else:
+            for d in range(1, nz):
+                mg_far(part, d, zb).start()
+
+    def mg_end(part):
+        for d in range(1, nz):
+            mg_far(part, d, lax.rem(zb + nz - d, nz)).wait_recv()
+
+    soon = ("mg", mg_own, mg_r1, mg_all)
+    final = ("ml", ml_own, ml_r1, ml_all)
 
     pieces = [
         (wo_in, wo), (att_in, att), (tok_in, tok), (proj_in, proj), (wqkv_in, wqkv), (x_in, xf),
@@ -976,11 +1065,12 @@
         pltpu.make_async_copy(src, dst, load_sem.at[n]) for n, (src, dst) in enumerate(pieces)
     ]
     full = dq_in.shape[0] - parts
-    early = [pltpu.make_async_copy(uq_in.at[:, :, :, head], fu.at[:, :, :, head], load_sem.at[7])]
-    late = [
-        pltpu.make_async_copy(ul_in.at[p], lu, load_sem.at[8]),
-        pltpu.make_async_copy(dl_in.at[p], ld, load_sem.at[9]),
+    early = [
+        pltpu.make_async_copy(uh_in.at[p], fu.at[:, :, pl.ds(0, LANES)], load_sem.at[7]),
+        pltpu.make_async_copy(ul_in.at[:, :, yb], ly, load_sem.at[8]),
+        pltpu.make_async_copy(ud_in, fin_u.at[c, p, :, pl.ds(0, lead)], load_sem.at[9]),
     ]
+    late = [pltpu.make_async_copy(dl_in.at[p], ld, load_sem.at[10])]
     for owner in range(2 * nz):
         count = min(per, full - owner * per)
         if count > 0:
@@ -988,12 +1078,14 @@
                 pltpu.make_async_copy(
                     dq_in.at[pl.ds(owner * per, count)],
                     fd.at[owner // 2, owner % 2, pl.ds(0, count)],
-                    load_sem.at[10 + owner],
+                    load_sem.at[11 + owner],
                 )
             )
-    for load in (*early, *loads, *late):
+    for load in (*loads[:4], *late, *early, *loads[4:]):
         load.start()
     kk_2[0] = kern_two[...].astype(bf16)
+    mg_own[...] = small[...]
+    mg_own[6:8, :] = mod[6:8, :]
     meet([core, side, corner, beside, *far[1:]])
     grad_away = remote(
         rg_in.at[:, 1 - c], rows_m.at[pl.ds(8 * c, 8)], ex_send.at[0], ex_recv.at[0], core
@@ -1001,10 +1093,11 @@
     grad_away.start()
     grad_own = pltpu.make_async_copy(rg_in.at[:, c], rows_m.at[pl.ds(8 * c, 8)], own_sem.at[0])
     grad_own.start()
-    start(last_x())
-    early[0].wait()
-    start(fa_y())
+    last_d().start()
+    last_y().start()
+    half_x().start()
     kern_copy("two", kk_2, kr_2, 0).start()
+    mg_copy(soon, 0).start()
     perm[0] = permutation(False)
     perm[1] = permutation(True)
     grad_own.wait()
@@ -1021,8 +1114,10 @@
     tok_t[...] = tok[...].T
     loads[3].wait()
     place_last()
-    send_home(res_in, o_res, r_send, r_recv, False)
+    for n in range(2):
+        send_home(n, res_in, o_res, r_send, r_recv, False)
     kern_step(*two, 0)
+    mg_step(soon, 0)
 
     low_lane = lax.broadcasted_iota(jnp.int32, (size, LANES), 1) < LANES // 2
     lane_id = lax.broadcasted_iota(jnp.int32, (size, LANES), 1)
@@ -1061,31 +1156,39 @@
         return carry
 
     def weigh(k):
+        span = slice(2 * k * chunk, 2 * (k + 1) * chunk)
         for q in range(3):
-            span = slice(q * width + k * chunk, q * width + (k + 1) * chunk)
-            part = dot_nn(tok_t[...], dproj[:, span])
-            wp[k, q % 2, q // 2] = part.reshape(nz, 2, rows_own, chunk).astype(bf16)
-        p1(k).start()
+            part = dot_nn(tok_t[...], dproj[:, q * width + span.start : q * width + span.stop])
+            part = part.reshape(nz, 2, rows_own, 2 * chunk).astype(bf16)
+            for n in range(2):
+                wp[2 * k + n, q % 2, q // 2] = part[..., n * chunk : (n + 1) * chunk]
+        p1(2 * k).start()
+        p1(2 * k + 1).start()
 
     lax.fori_loop(0, 2, attend, 0)
-    fa_y_add()
+    half_add()
     kern_step(*two, 1)
     lax.fori_loop(2, 4, attend, 0)
     weigh(0)
-    fb_y_add()
-    kern_step(*two, 2)
+    last_y_add()
+    mg_step(soon, 1)
     lax.fori_loop(4, 6, attend, 0)
     p_add_1(0)
+    p_add_1(1)
+    kern_step(*two, 2)
     lax.fori_loop(6, 8, attend, 0)
     weigh(1)
-    f_sum()
+    last_x_add()
+    mg_step(soon, 2)
+    lax.fori_loop(8, 10, attend, 0)
+    p_add_1(2)
+    p_add_1(3)
+    p_add_2(0)
+    p_add_2(1)
     kern_sum("two", kk_2, kz_2, o_two)
-    lax.fori_loop(8, 10, attend, 0)
-    p_add_1(1)
-    p_add_2(0)
-    f_side_done()
     lax.fori_loop(10, 12, attend, 0)
     weigh(2)
+    down_y_add()
     loads[4].wait()
     back = dot_nt(dproj[...], wqkv[...]).astype(bf16)
     brm[...] = dot_nn(perm[1], back).astype(bf16).reshape(16, across, width)
@@ -1095,10 +1198,12 @@
     mixed_away.start()
     mixed_own = pltpu.make_async_copy(brm.at[pl.ds(7 * c, 9)], frame.at[:, c], own_sem.at[1])
     mixed_own.start()
-    p_add_1(2)
+    p_add_1(4)
+    p_add_1(5)
     p_add_3(0)
-    p_add_2(1)
-    f_core_done()
+    p_add_3(1)
+    p_add_2(2)
+    p_add_2(3)
     loads[5].wait()
     loads[6].wait()
 
@@ -1127,9 +1232,7 @@
     for s in range(3):
         gs[s, 17 * c] = jnp.zeros((across, width), f32)
 
-    kk_1[0] = jnp.zeros((16, width), bf16)
-
-    def conv_back(lane):
+    def conv_back(lane, half):
         span = slice(lane, lane + LANES)
         taps = [kern[n : n + 1, span].astype(f32) for n in range(9)]
 
@@ -1146,19 +1249,15 @@
             return tuple(later)
 
         sums = lax.fori_loop(
-            0, 16, backward, tuple(jnp.zeros((8, LANES), f32) for _ in range(9))
+            8 * half, 8 * half + 8, backward,
+            tuple(jnp.zeros((8, LANES), f32) for _ in range(9)),
         )
         rows9 = [jnp.sum(sums[n], axis=0, keepdims=True) for n in range(9)]
-        kk_1[0, :, span] = jnp.concatenate(rows9 + [jnp.zeros((7, LANES), f32)]).astype(bf16)
-
-    for lane in range(0, width // 2, LANES):
-        conv_back(lane)
-    p_add_4(0)
-    p_add_3(1)
-    p_add_2(2)
-    for lane in range(width // 2, width, LANES):
-        conv_back(lane)
-    kern_copy("one", kk_1, kr_1, 0).start()
+        lines = jnp.concatenate(rows9 + [jnp.zeros((7, LANES), f32)])
+        if half == 0:
+            taps_sum[:, span] = lines
+        else:
+            kk_1[0, :, span] = (taps_sum[:, span] + lines).astype(bf16)
 
     def finish(row, sums):
         normal, scale = normalize(xf[2 * c + row].astype(f32))
@@ -1168,59 +1267,83 @@
         ig[row] = total.astype(bf16)
         return (sums[0] + fold(line), sums[1] + fold(line * normal))
 
-    sums = lax.fori_loop(0, 16, finish, tuple(jnp.zeros((8, width), f32) for _ in range(2)))
-    send_home(ig, o_ig, i_send, i_recv, False)
-    mg_own[...] = small[...]
+    sums = tuple(jnp.zeros((8, width), f32) for _ in range(2))
+    up_sum()
+    for lane in range(0, width, LANES):
+        conv_back(lane, 0)
+    p_add_2(4)
+    p_add_2(5)
+    p_add_3(2)
+    p_add_3(3)
+    sums = lax.fori_loop(0, 8, finish, sums)
+    send_home(0, ig, o_ig, i_send, i_recv, False)
+    p_add_4(0)
+    p_add_4(1)
+    mg_end(soon)
+    mg_out.start()
+    for lane in range(0, width, LANES):
+        conv_back(lane, 1)
+    kern_copy("one", kk_1, kr_1, 0).start()
+    p_add_3(4)
+    p_add_3(5)
+    down_sum()
+    pass_on("gu", fin_u)
+    sums = lax.fori_loop(8, 16, finish, sums)
     for n in range(2):
-        mg_own[n : n + 1, :] = jnp.sum(sums[n], axis=0, keepdims=True)
-    mg_own[6:8, :] = mod[6:8, :]
-    mg_copy(0).start()
+        ml_own[n : n + 1, :] = jnp.sum(sums[n], axis=0, keepdims=True)
+    mg_copy(final, 0).start()
+    send_home(1, ig, o_ig, i_send, i_recv, False)
     kern_step(*one, 0)
     p_pass(0)
-    p_add_4(1)
-    mg_copy(0).wait_recv()
-    mg_all[zb, yb, p] = mg_own[...] + mg_r1[...]
-    mg_copy(1).start()
-    p_add_3(2)
+    p_pass(1)
+    mg_step(final, 0)
+    p_add_4(2)
+    p_add_4(3)
     kern_step(*one, 1)
-    mg_copy(1, False).wait_recv()
-    mg_copy(2).start()
-    p_pass(1)
+    mg_step(final, 1)
+    to_core("gu", fin_u, False).wait_recv()
+    u_out.start()
+    pass_on("gd", fin_d)
     kern_step(*one, 2)
-    mg_copy(2, False).wait_recv()
+    mg_step(final, 2)
+    p_add_4(4)
+    p_add_4(5)
+    p_pass(2)
+    p_pass(3)
+    to_core("gd", fin_d, False).wait_recv()
+    d_out.start()
+    kern_sum("one", kk_1, kz_1, o_one)
+    mg_end(final)
+    ml_out.start()
+    p_pass(4)
+    p_pass(5)
+    for k in range(chunks):
+        p_core(k, False).wait_recv()
+    p_out.start()
+    gone([half_x(), last_y(), last_x(), last_d(), down_y()])
+    for name, fin in (("gu", fin_u), ("gd", fin_d)):
+        gone([to_side(name, fin, True), to_core(name, fin, True)])
     for d in range(1, nz):
-        mg_far(d, zb).start()
-    p_add_4(2)
-    p_core(0, False).wait_recv()
-    p_core(1, False).wait_recv()
-    p_pass(2)
-    kern_sum("one", kk_1, kz_1, o_one)
-    for d in range(1, nz):
-        mg_far(d, lax.rem(zb + nz - d, nz)).wait_recv()
-    mg_out.start()
-    p_core(2, False).wait_recv()
-    p_out.start()
-    gone([*last_x(), *fa_y(), *fb_y(), *f_side(True), *f_core(True)])
-    for d in range(1, nz):
-        gone([*fa_z(d), *fb_z(d), mg_far(d, zb)])
+        gone([up_z(d), down_z(d), mg_far(soon, d, zb), mg_far(final, d, zb)])
         gone([kern_far("one", kk_1, kz_1, d), kern_far("two", kk_2, kz_2, d)])
     for k in range(chunks):
         gone([p1(k), p2(k), p3(k), p_side(k, True), p_core(k, True)])
         gone([p4(k, d) for d in range(1, nz)])
     for stage in range(3):
-        gone([mg_copy(stage)])
+        gone([mg_copy(soon, stage), mg_copy(final, stage)])
         gone([kern_copy("one", kk_1, kr_1, stage), kern_copy("two", kk_2, kr_2, stage)])
-    send_home(res_in, o_res, r_send, r_recv, True)
-    send_home(ig, o_ig, i_send, i_recv, True)
+    for n in range(2):
+        send_home(n, res_in, o_res, r_send, r_recv, True)
+        send_home(n, ig, o_ig, i_send, i_recv, True)
     home(o_res, r_recv)
     home(o_ig, i_recv)
-    for out in (*f_out, p_out, mg_out):
+    for out in (u_out, d_out, p_out, mg_out, ml_out):
         out.wait()
 
 
 def back(
     mid, rg, tok, proj, att, lse, bias, x_frame, mod, small, kern, wqkv, wo, res,
-    uq, dq, ul, dl, kern_two,
+    ud, dq, uh, ul, dl, kern_two,
 ):
     nb = lax.axis_size("batch")
     nz = nb // 2
@@ -1230,14 +1353,14 @@
     grain = dq.shape[1]
     parts = dl.shape[1]
     per = dq.shape[0] // nb
-    chunks, chunk = 3, 2 * LANES
+    chunks, chunk = width // LANES, LANES
     many = max(nz - 1, 1)
     any_space = pl.BlockSpec(memory_space=pl.ANY)
     vmem = pl.BlockSpec(memory_space=pltpu.VMEM)
     shape = jax.ShapeDtypeStruct
     dma = pltpu.SemaphoreType.DMA
     wide = kern_two.shape[1]
-    links = 80 + 12 * many
+    links = 100 + 20 * many
 
     def low(*dims):
         return pltpu.VMEM(dims, bf16)
@@ -1256,10 +1379,11 @@
             shape((16, width), f32),
             shape((16, wide), f32),
             shape((nz, 2, 2, 8, width), f32),
+            shape((nz, 2, 2, 2, width), f32),
         ),
-        in_specs=[any_space] * 5 + [vmem, vmem, any_space, vmem, vmem, vmem] + [any_space] * 7
+        in_specs=[any_space] * 5 + [vmem, vmem, any_space, vmem, vmem, vmem] + [any_space] * 8
         + [vmem],
-        out_specs=[any_space] * 5 + [vmem, vmem, any_space],
+        out_specs=[any_space] * 5 + [vmem, vmem, any_space, any_space],
         scratch_shapes=[
             high(tokens, width), low(tokens, width), low(width, tokens), low(tokens, 3 * width),
             low(tokens, width), low(18, across, width), low(*wqkv.shape), low(*wo.shape),
@@ -1271,17 +1395,18 @@
             low(chunks, nz, 2, rows, chunk), low(chunks, 2, nz, rows, chunk),
             low(chunks, nz, rows, chunk), low(chunks, many, rows, chunk),
             low(chunks, 2, 2, rows, chunk),
-            low(nz, 2, rows, width), low(nz, 2, per, grain, width),
-            low(nz, rows, width), low(nz, per, grain, width),
-            low(many, rows, width), low(many, per, grain, width),
+            low(nz, rows, 2 * LANES), low(nz, 2, per, grain, width),
+            low(many, rows, 2 * LANES), low(nz, per, grain, width), low(many, per, grain, width),
             low(2, 2, rows, width), low(2, 2, per, grain, width),
-            low(nz, 2, rows, LANES), low(parts, grain, width),
-            low(nz, 2, rows, LANES), low(parts, grain, width),
+            low(parts, grain, width), low(parts, grain, width),
+            low(nz, rows, LANES), low(2, nz, rows, LANES), low(2, nz, rows, LANES),
+            low(nz, rows, LANES),
             high(8, width), high(8, width), high(nz, 2, 2, 8, width),
+            high(2, width), high(2, width), high(nz, 2, 2, 2, width), high(16, width),
             low(4, 16, width), low(3, 16, width), low(many, 16, width),
             low(4, 16, wide), low(3, 16, wide), low(many, 16, wide),
-            dma((10 + nb,)), dma((2,)), dma((2,)), dma((2,)), dma((2,)), dma((2,)), dma((2,)),
-            dma((2,)), dma((links,)), dma((links,)), dma((4,)),
+            dma((11 + nb,)), dma((2,)), dma((2,)), dma((2,)), dma((2,)), dma((2,)), dma((2,)),
+            dma((2,)), dma((links,)), dma((links,)), dma((5,)),
         ],
         compiler_params=pltpu.CompilerParams(
             collective_id=2, has_side_effects=True, vmem_limit_bytes=63 << 20
@@ -1289,14 +1414,26 @@
         name="back",
     )(
         mid, rg, tok, proj, att, lse, bias, x_frame, mod, small, kern, wqkv, wo, res,
-        uq, dq, ul, dl, kern_two,
-    )
+        ud, dq, uh, ul, dl, kern_two,
+    )
+
+
+def parts_of(values):
+    first = values.astype(bf16)
+    rest = values - first.astype(f32)
+    second = rest.astype(bf16)
+    third = (rest - second.astype(f32)).astype(bf16)
+    return jnp.concatenate([first, second, third], axis=0)
+
+
+def thrice(values):
+    return jnp.concatenate([values] * 3, axis=0).astype(bf16)
 
 
 def tail_kernel(
-    fu, fd, fp, mg, one, two, wm_in,
-    o_class, o_time, o_mod, o_proj, o_out, o_one, o_up, o_two, o_down,
-    wm, load_sem,
+    fu, fd, fp, mg, late, one, two, wm_in, res_in, ig_in,
+    o_class, o_time, o_mod, o_proj, o_out, o_one, o_up, o_two, o_down, o_res, o_ig,
+    wm, moved, load_sem, in_sem, out_sem,
 ):
     b = lax.axis_index("batch")
     width = mg.shape[2]
@@ -1306,6 +1443,14 @@
     source = wm_in if whole else wm_in.at[pl.ds(pl.multiple_of(b * own, 16), own)]
     load = pltpu.make_async_copy(source, wm, load_sem)
     load.start()
+    takes = [
+        pltpu.make_async_copy(src, moved.at[n], in_sem.at[n]) for n, src in enumerate((res_in, ig_in))
+    ]
+    gives = [
+        pltpu.make_async_copy(moved.at[n], dst, out_sem.at[n]) for n, dst in enumerate((o_res, o_ig))
+    ]
+    for take in takes:
+        take.start()
     chunks, chunk = fp.shape[0], fp.shape[4]
     per, grain = fd.shape[2], fd.shape[3]
     for q in range(4):
@@ -1321,6 +1466,9 @@
                 o_proj[:, q * width + k * chunk : q * width + (k + 1) * chunk] = part
             else:
                 o_out[:, k * chunk : (k + 1) * chunk] = part
+    for take, give in zip(takes, gives):
+        take.wait()
+        give.start()
 
     def window(values, n):
         size = values.shape[1]
@@ -1329,35 +1477,33 @@
     o_one[...] = window(one[...], own)[0:9]
     o_two[...] = window(two[...], o_two.shape[1])[0:9]
     every = mg[...]
+    begin = late[...]
     cond = window(every[:, 7, :] * 0.5, own)
     sigma = 1.0 / (1.0 + jnp.exp(-cond))
-    low = (cond * sigma).astype(bf16).astype(f32)
+    low = thrice(cond * sigma)
     steep = sigma * (1.0 + cond * (1.0 - sigma))
-    act_grad = jnp.zeros((canvases, own), f32)
+    act_grad = jnp.zeros((3 * canvases, own), f32)
     load.wait()
     for part in range(6):
         span = slice(part * width, (part + 1) * width)
-        line = every[:, part, :]
-        o_mod[:, span] = lax.dot_general(
-            low, line, (((0,), (0,)), ((), ())), precision=highest, preferred_element_type=f32
-        )
-        act_grad = act_grad + lax.dot_general(
-            line, wm[:, span].astype(f32), (((1,), (1,)), ((), ())), precision=highest,
-            preferred_element_type=f32,
-        )
-    cond_grad = act_grad * steep
+        line = parts_of(begin[:, part, :] if part < 2 else every[:, part, :])
+        o_mod[:, span] = dot_tn(low, line)
+        act_grad = act_grad + dot_nt(line, wm[:, span])
+    act_grad = (
+        act_grad[2 * canvases :] + act_grad[canvases : 2 * canvases] + act_grad[:canvases]
+    )
+    cond_grad = parts_of(act_grad * steep)
     names = every[:, 6, :] * 0.5
-    kinds = o_class.shape[0]
+    kinds = o_class.shape[1]
     spot = lax.broadcasted_iota(jnp.int32, (canvases, kinds), 1).astype(f32)
     for n, out in enumerate((o_class, o_time)):
-        hot = jnp.where(spot == names[:, n : n + 1], 1.0, 0.0)
-        out[...] = lax.dot_general(
-            hot, cond_grad, (((0,), (0,)), ((), ())), precision=highest,
-            preferred_element_type=f32,
-        )
-
-
-def tail(fu, fd, fp, mg, one, two, wmod, classes, times):
+        hot = thrice(jnp.where(spot == names[:, n : n + 1], 1.0, 0.0))
+        out[...] = dot_tn(cond_grad, hot)
+    for give in gives:
+        give.wait()
+
+
+def tail(fu, fd, fp, mg, late, one, two, wmod, res, ig, classes, times):
     nb = lax.axis_size("batch")
     width = mg.shape[2]
     own = width // nb
@@ -1367,11 +1513,12 @@
     any_space = pl.BlockSpec(memory_space=pl.ANY)
     vmem = pl.BlockSpec(memory_space=pltpu.VMEM)
     shape = jax.ShapeDtypeStruct
+    dma = pltpu.SemaphoreType.DMA
     return pl.pallas_call(
         tail_kernel,
         out_shape=(
-            shape((classes, own), f32),
-            shape((times, own), f32),
+            shape((own, classes), f32),
+            shape((own, times), f32),
             shape((own, 6 * width), f32),
             shape((own, 3 * width), f32),
             shape((own, width), f32),
@@ -1379,13 +1526,18 @@
             shape((own, 4 * width), f32),
             shape((9, wide), f32),
             shape((4 * fd.shape[2] * fd.shape[3], width), f32),
+            shape(res.shape, bf16),
+            shape(ig.shape, bf16),
         ),
-        in_specs=[vmem] * 6 + [any_space],
-        out_specs=[vmem] * 9,
-        scratch_shapes=[pltpu.VMEM((own, 6 * width), bf16), pltpu.SemaphoreType.DMA],
+        in_specs=[vmem] * 7 + [any_space] * 3,
+        out_specs=[vmem] * 9 + [any_space] * 2,
+        scratch_shapes=[
+            pltpu.VMEM((own, 6 * width), bf16), pltpu.VMEM((2, *res.shape), bf16),
+            dma, dma((2,)), dma((2,)),
+        ],
         compiler_params=pltpu.CompilerParams(vmem_limit_bytes=60 << 20),
         name="tail",
-    )(fu, fd, fp, mg, one, two, wmod)
+    )(fu, fd, fp, mg, late, one, two, wmod, res, ig)
 
 
 def body(
@@ -1406,8 +1558,6 @@
 ):
     across, width = inputs.shape[2], inputs.shape[3]
     nb = lax.axis_size("batch")
-    nz = nb // 2
-    rows = width // nb
     units = up_weight.shape[1]
     grain = 16 if (units // nb) % 64 == 0 else 8
     x_frame, cot_frame, returned, tok, proj, att, lse, bias, mod = front(
@@ -1415,27 +1565,27 @@
         time_table, modulation_weight, project_weight, output_weight,
     )
     flat = (18 * across, width)
-    uq, dq, ul, dl, kern_two, res, mid, rg, small = feed(
+    ud, dq, uh, ul, dl, kern_two, res, mid, rg, small = feed(
         x_frame.reshape(flat), returned.reshape(flat), cot_frame.reshape(flat), mod, up_weight,
         kernel_feed, down_weight, grain,
     )
-    fu, fd, fp, result, inputs_gradient, one, two, gathered = back(
+    fu, fd, fp, result, inputs_gradient, one, two, gathered, late = back(
         mid, rg.reshape(8, 2, across, width), tok, proj, att, lse, bias, x_frame, mod, small,
         kernel_attention, project_weight, output_weight, res.reshape(16, across, width),
-        uq.reshape(nz, 2, rows, width), dq, ul.reshape(2, nz, 2, rows, LANES), dl, kern_two,
+        ud, dq, uh, ul, dl, kern_two,
     )
     (
         class_total, time_total, modulation_total, project_total, output_total,
-        attention_kernel_total, up_total, feed_kernel_total, down_total,
+        attention_kernel_total, up_total, feed_kernel_total, down_total, result, inputs_gradient,
     ) = tail(
-        fu, fd, fp, gathered.reshape(2 * nb, 8, width), one, two, modulation_weight,
-        class_table.shape[0], time_table.shape[0],
+        fu, fd, fp, gathered.reshape(2 * nb, 8, width), late.reshape(2 * nb, 2, width), one, two,
+        modulation_weight, result, inputs_gradient, class_table.shape[0], time_table.shape[0],
     )
     return (
         result,
         inputs_gradient,
-        class_total,
-        time_total,
+        class_total.T,
+        time_total.T,
         modulation_total,
         project_total,
         output_total,

time: 254 us -> 220 us (0.87)
  Pallas kernels: 248 us -> 218 us
  local copies, waits for them, and re-layouts: 5.83 us -> 0 us
    pallas_call x1, Pallas kernels: 109 us -> 92.8 us  [back(): pl.pallas_call(back_kernel, out_shape=(shape((2, 2, rows, width), bf16),...]
    pallas_call x2, Pallas kernels: 104 us -> 91.1 us  [the longest x1 83.5 us: feed(): pl.pallas_call(feed_kernel, grid=(units // tile,), out_shape=(shape((own,...]
    unnamed x8 -> x0, local copies, waits for them, and re-layouts: 5.83 us -> none
where the time goes in v4:
time: 220 us; the launch traced here: 219 us
  Pallas kernels  218 us (99%)
    pallas_call x1, Pallas kernels, back(): pl.pallas_call(back_kernel, out_shape=(shape((2, 2, rows, width), bf16),...  92.8 us
    pallas_call x1, Pallas kernels, feed(): pl.pallas_call(feed_kernel, grid=(units // tile,), out_shape=(shape((own,...  83.5 us
    pallas_call x1, Pallas kernels, front(): pl.pallas_call(front_kernel, out_shape=(shape((18, across, width), bf16),...  34.3 us
    pallas_call x1, Pallas kernels, tail(): pl.pallas_call(tail_kernel, out_shape=(shape((own, classes), f32), shape(...  7.57 us

profile of v4, /device:TPU:0, one launch (start us, length us, event | category | flops | bytes accessed | tf_op | source)
XLA Modules:
  0.0 219.0 jit_solution(12910945456063065717)
XLA Ops:
  0.6 34.3 %front.1 = (bf16[18,32,768]{2,1,0:T(8,128)(2,1)}, bf16[18,32,768]{2,1,0:T(8,128)(2,1)}, bf16[9,2,32,768]{3,2,1,0:T(8,128)(2,1)}, bf16[512,768]{1,0:T(8,128)(2,1)...) custom-call(bf16[2,8,32,768]{3,2,1,0:T(8,128)(2,1)} %x_in.1, ...), custom_call_target="tpu_custom_call" | custom-call | tf_op jit(solution)/shard_map/front/pallas_call | solution.py:308
  34.9 83.5 %feed.1 = (bf16[96,512]{1,0:T(8,128)(2,1)}, bf16[48,16,768]{2,1,0:T(8,128)(2,1)}, bf16[2,4,96,128]{3,2,1,0:T(8,128)(2,1)}, bf16[2,4,2,96,128]{4,3,2,1,0:T(8,128)...) custom-call(bf16[576,768]{1,0:T(8,128)(2,1)} %bitcast.9, ...), custom_call_target="tpu_custom_call" | custom-call | flops 14495514624 | bytes 18874368 | tf_op jit(solution)/shard_map/feed/pallas_call | solution.py:688
  118.5 92.8 %back.1 = (bf16[2,2,96,768]{3,2,1,0:T(8,128)(2,1)}, bf16[2,2,6,16,768]{4,3,2,1,0:T(8,128)(2,1)}, bf16[6,2,2,96,128]{4,3,2,1,0:T(8,128)(2,1)}, bf16[2,8,32,768]{3...) custom-call(f32[512,768]{1,0:T(8,128)} %get-tuple-element.54.mid_in,, ...), custom_call_target="tpu_custom_call" | custom-call | tf_op jit(solution)/shard_map/back/pallas_call | solution.py:1371
  211.2 7.6 %tail.1 = (f32[96,1000]{1,0:T(8,128)}, f32[96,1000]{1,0:T(8,128)}, f32[96,4608]{1,0:T(8,128)}, f32[96,2304]{1,0:T(8,128)}, f32[96,768]{1,0:T(8,128)}, /*index=5*...) custom-call(bf16[2,2,96,768]{3,2,1,0:T(8,128)(2,1)} %get-tuple-eleme, ...), custom_call_target="tpu_custom_call" | custom-call | tf_op jit(solution)/shard_map/tail/pallas_call | solution.py:1517

commit v5 on v4

--- a/solution.py
+++ b/solution.py
@@ -751,7 +751,8 @@
     brm, frame, gs, value, agrad, ig,
     wp, p_r1, p_r2x, p_r2y, p_r3, p_r4, fin_p,
     fu, fd, fz_u, fy_d, fz_d, fin_u, fin_d, ld, lx_d, hx, ly, ly_r, lx,
-    mg_own, mg_r1, mg_all, ml_own, ml_r1, ml_all, taps_sum, kk_1, kr_1, kz_1, kk_2, kr_2, kz_2,
+    mg_own, mg_r1, mg_all, ml_own, ml_r1, ml_all, taps_sum, kk_1, kr_1, kz_1,
+    kt, kt_core, kt_side, kt_y, kt_sum, kt_z, fin_k,
     load_sem, r_send, r_recv, i_send, i_recv, ex_send, ex_recv, own_sem, send_sem, recv_sem, out_sem,
 ):
     b = lax.axis_index("batch")
@@ -1025,24 +1026,68 @@
         out[...] = total
 
     one = ("one", kk_1, kr_1, kz_1)
-    two = ("two", kk_2, kr_2, kz_2)
+
+    def taps_core():
+        return link("kt0", kt.at[1 - c], kt_core, core)
+
+    def taps_side():
+        return link("kt1", kt.at[c, 1 - p], kt_side, side)
+
+    def taps_y():
+        return link("kt2", kt.at[c, p], kt_y, beside)
+
+    def taps_z(d):
+        return link(f"kt3{d}", kt_sum, kt_z.at[d - 1], far[d])
+
+    def taps_core_add():
+        taps_core().wait_recv()
+        for x in range(2):
+            kt[c, x] = kt[c, x] + kt_core[x]
+        taps_side().start()
+
+    def taps_side_add():
+        taps_side().wait_recv()
+        kt[c, p] = kt[c, p] + kt_side[...]
+        taps_y().start()
+
+    def taps_y_add():
+        taps_y().wait_recv()
+        kt_sum[...] = kt[c, p] + kt_y[...]
+        for d in range(1, nz):
+            taps_z(d).start()
+
+    def taps_total():
+        total = kt_sum[...].astype(f32)
+        for d in range(1, nz):
+            taps_z(d).wait_recv()
+            total = total + kt_z[d - 1].astype(f32)
+        fin_k[c, p] = total.astype(bf16)
+        to_side("gk", fin_k, True).start()
+
+    def mg_swap(mine=True):
+        x = c if mine else 1 - c
+        return link("mgc", mg_all.at[x], mg_all.at[x], core)
 
     def mg_copy(part, stage, mine=True):
         name, own, first, every = part
         if stage == 0:
-            return link(f"{name}0", own, first, core)
+            return link(f"{name}0", own.at[1 - c] if name == "mg" else own, first, core)
+        every = every.at[c] if name == "mg" else every
         x = p if mine else 1 - p
         y = yb if mine else 1 - yb
         place = every.at[zb, yb, x] if stage == 1 else every.at[zb, y]
         return link(f"{name}{stage}", place, place, peers[stage])
 
     def mg_far(part, d, z):
-        return link(f"{part[0]}z{d}", part[3].at[z], part[3].at[z], far[d])
+        place = part[3].at[c, z] if part[0] == "mg" else part[3].at[z]
+        return link(f"{part[0]}z{d}", place, place, far[d])
 
     def mg_step(part, stage):
         name, own, first, every = part
         mg_copy(part, stage, False).wait_recv()
-        if stage == 0:
+        if stage == 0 and name == "mg":
+            every[c, zb, yb, p] = own[c] + first[...]
+        elif stage == 0:
             every[zb, yb, p] = own[...] + first[...]
         if stage < 2:
             mg_copy(part, stage + 1).start()
@@ -1083,9 +1128,14 @@
             )
     for load in (*loads[:4], *late, *early, *loads[4:]):
         load.start()
-    kk_2[0] = kern_two[...].astype(bf16)
-    mg_own[...] = small[...]
-    mg_own[6:8, :] = mod[6:8, :]
+    half_width, quarter = width // 2, kt.shape[3]
+    for x in range(2):
+        span = slice(x * half_width, (x + 1) * half_width)
+        mg_own[x] = small[:, span]
+        mg_own[x, 6:8, :] = mod[6:8, span]
+        for q in range(2):
+            at = (2 * x + q) * quarter
+            kt[x, q] = kern_two[:, at : at + quarter].astype(bf16)
     meet([core, side, corner, beside, *far[1:]])
     grad_away = remote(
         rg_in.at[:, 1 - c], rows_m.at[pl.ds(8 * c, 8)], ex_send.at[0], ex_recv.at[0], core
@@ -1096,8 +1146,8 @@
     last_d().start()
     last_y().start()
     half_x().start()
-    kern_copy("two", kk_2, kr_2, 0).start()
     mg_copy(soon, 0).start()
+    taps_core().start()
     perm[0] = permutation(False)
     perm[1] = permutation(True)
     grad_own.wait()
@@ -1113,11 +1163,8 @@
     loads[2].wait()
     tok_t[...] = tok[...].T
     loads[3].wait()
-    place_last()
     for n in range(2):
         send_home(n, res_in, o_res, r_send, r_recv, False)
-    kern_step(*two, 0)
-    mg_step(soon, 0)
 
     low_lane = lax.broadcasted_iota(jnp.int32, (size, LANES), 1) < LANES // 2
     lane_id = lax.broadcasted_iota(jnp.int32, (size, LANES), 1)
@@ -1165,30 +1212,30 @@
         p1(2 * k).start()
         p1(2 * k + 1).start()
 
-    lax.fori_loop(0, 2, attend, 0)
-    half_add()
-    kern_step(*two, 1)
-    lax.fori_loop(2, 4, attend, 0)
-    weigh(0)
-    last_y_add()
-    mg_step(soon, 1)
-    lax.fori_loop(4, 6, attend, 0)
-    p_add_1(0)
-    p_add_1(1)
-    kern_step(*two, 2)
-    lax.fori_loop(6, 8, attend, 0)
-    weigh(1)
-    last_x_add()
-    mg_step(soon, 2)
-    lax.fori_loop(8, 10, attend, 0)
-    p_add_1(2)
-    p_add_1(3)
-    p_add_2(0)
-    p_add_2(1)
-    kern_sum("two", kk_2, kz_2, o_two)
-    lax.fori_loop(10, 12, attend, 0)
-    weigh(2)
-    down_y_add()
+    hooks = {
+        0: [lambda: mg_step(soon, 0), taps_core_add],
+        1: [half_add],
+        2: [place_last],
+        3: [lambda: weigh(0), last_y_add],
+        5: [lambda: mg_step(soon, 1), taps_side_add],
+        7: [lambda: weigh(1), lambda: p_add_1(0), lambda: p_add_1(1)],
+        9: [last_x_add],
+        10: [lambda: mg_step(soon, 2), taps_y_add],
+        11: [lambda: weigh(2)],
+    }
+
+    def attend_and_pass(index, carry):
+        attend(index, carry)
+        for at, steps in hooks.items():
+
+            @pl.when(index == at)
+            def _(steps=steps):
+                for step in steps:
+                    step()
+
+        return carry
+
+    lax.fori_loop(0, 2 * pairs, attend_and_pass, 0)
     loads[4].wait()
     back = dot_nt(dproj[...], wqkv[...]).astype(bf16)
     brm[...] = dot_nn(perm[1], back).astype(bf16).reshape(16, across, width)
@@ -1198,12 +1245,10 @@
     mixed_away.start()
     mixed_own = pltpu.make_async_copy(brm.at[pl.ds(7 * c, 9)], frame.at[:, c], own_sem.at[1])
     mixed_own.start()
-    p_add_1(4)
-    p_add_1(5)
-    p_add_3(0)
-    p_add_3(1)
-    p_add_2(2)
-    p_add_2(3)
+    p_add_2(0)
+    p_add_2(1)
+    p_add_1(2)
+    p_add_1(3)
     loads[5].wait()
     loads[6].wait()
 
@@ -1216,6 +1261,8 @@
         return carry
 
     lax.fori_loop(0, 16, again, 0)
+    p_add_1(4)
+    p_add_1(5)
     mixed_own.wait()
     mixed_away.wait()
 
@@ -1268,44 +1315,55 @@
         return (sums[0] + fold(line), sums[1] + fold(line * normal))
 
     sums = tuple(jnp.zeros((8, width), f32) for _ in range(2))
-    up_sum()
+    down_y_add()
+    p_add_3(0)
+    p_add_3(1)
     for lane in range(0, width, LANES):
         conv_back(lane, 0)
+        if lane == 2 * LANES:
+            p_add_2(2)
+            p_add_2(3)
+    sums = lax.fori_loop(0, 8, finish, sums)
+    send_home(0, ig, o_ig, i_send, i_recv, False)
     p_add_2(4)
     p_add_2(5)
-    p_add_3(2)
-    p_add_3(3)
-    sums = lax.fori_loop(0, 8, finish, sums)
-    send_home(0, ig, o_ig, i_send, i_recv, False)
-    p_add_4(0)
-    p_add_4(1)
-    mg_end(soon)
-    mg_out.start()
     for lane in range(0, width, LANES):
         conv_back(lane, 1)
+        if lane == 2 * LANES:
+            p_add_3(2)
+            p_add_3(3)
     kern_copy("one", kk_1, kr_1, 0).start()
-    p_add_3(4)
-    p_add_3(5)
-    down_sum()
-    pass_on("gu", fin_u)
     sums = lax.fori_loop(8, 16, finish, sums)
     for n in range(2):
         ml_own[n : n + 1, :] = jnp.sum(sums[n], axis=0, keepdims=True)
     mg_copy(final, 0).start()
     send_home(1, ig, o_ig, i_send, i_recv, False)
+    up_sum()
+    p_add_3(4)
+    p_add_3(5)
+    p_add_4(0)
+    p_add_4(1)
+    taps_total()
+    mg_end(soon)
+    mg_swap().start()
     kern_step(*one, 0)
+    mg_step(final, 0)
+    down_sum()
+    pass_on("gu", fin_u)
     p_pass(0)
     p_pass(1)
-    mg_step(final, 0)
+    pass_on("gk", fin_k)
+    kern_step(*one, 1)
+    mg_step(final, 1)
     p_add_4(2)
     p_add_4(3)
-    kern_step(*one, 1)
-    mg_step(final, 1)
+    mg_swap(False).wait_recv()
+    mg_out.start()
     to_core("gu", fin_u, False).wait_recv()
     u_out.start()
-    pass_on("gd", fin_d)
     kern_step(*one, 2)
     mg_step(final, 2)
+    pass_on("gd", fin_d)
     p_add_4(4)
     p_add_4(5)
     p_pass(2)
@@ -1320,18 +1378,22 @@
     for k in range(chunks):
         p_core(k, False).wait_recv()
     p_out.start()
+    to_core("gk", fin_k, False).wait_recv()
+    for x in range(4):
+        o_two[:, x * quarter : (x + 1) * quarter] = fin_k[x // 2, x % 2].astype(f32)
     gone([half_x(), last_y(), last_x(), last_d(), down_y()])
-    for name, fin in (("gu", fin_u), ("gd", fin_d)):
+    gone([taps_core(), taps_side(), taps_y(), mg_swap()])
+    for name, fin in (("gu", fin_u), ("gd", fin_d), ("gk", fin_k)):
         gone([to_side(name, fin, True), to_core(name, fin, True)])
     for d in range(1, nz):
         gone([up_z(d), down_z(d), mg_far(soon, d, zb), mg_far(final, d, zb)])
-        gone([kern_far("one", kk_1, kz_1, d), kern_far("two", kk_2, kz_2, d)])
+        gone([kern_far("one", kk_1, kz_1, d), taps_z(d)])
     for k in range(chunks):
         gone([p1(k), p2(k), p3(k), p_side(k, True), p_core(k, True)])
         gone([p4(k, d) for d in range(1, nz)])
     for stage in range(3):
         gone([mg_copy(soon, stage), mg_copy(final, stage)])
-        gone([kern_copy("one", kk_1, kr_1, stage), kern_copy("two", kk_2, kr_2, stage)])
+        gone([kern_copy("one", kk_1, kr_1, stage)])
     for n in range(2):
         send_home(n, res_in, o_res, r_send, r_recv, True)
         send_home(n, ig, o_ig, i_send, i_recv, True)
@@ -1378,7 +1440,7 @@
             shape((2, 8, across, width), bf16),
             shape((16, width), f32),
             shape((16, wide), f32),
-            shape((nz, 2, 2, 8, width), f32),
+            shape((2, nz, 2, 2, 8, width // 2), f32),
             shape((nz, 2, 2, 2, width), f32),
         ),
         in_specs=[any_space] * 5 + [vmem, vmem, any_space, vmem, vmem, vmem] + [any_space] * 8
@@ -1401,10 +1463,11 @@
             low(parts, grain, width), low(parts, grain, width),
             low(nz, rows, LANES), low(2, nz, rows, LANES), low(2, nz, rows, LANES),
             low(nz, rows, LANES),
-            high(8, width), high(8, width), high(nz, 2, 2, 8, width),
+            high(2, 8, width // 2), high(8, width // 2), high(2, nz, 2, 2, 8, width // 2),
             high(2, width), high(2, width), high(nz, 2, 2, 2, width), high(16, width),
             low(4, 16, width), low(3, 16, width), low(many, 16, width),
-            low(4, 16, wide), low(3, 16, wide), low(many, 16, wide),
+            low(2, 2, 16, wide // 4), low(2, 16, wide // 4), low(16, wide // 4), low(16, wide // 4),
+            low(16, wide // 4), low(many, 16, wide // 4), low(2, 2, 16, wide // 4),
             dma((11 + nb,)), dma((2,)), dma((2,)), dma((2,)), dma((2,)), dma((2,)), dma((2,)),
             dma((2,)), dma((links,)), dma((links,)), dma((5,)),
         ],
@@ -1436,8 +1499,8 @@
     wm, moved, load_sem, in_sem, out_sem,
 ):
     b = lax.axis_index("batch")
-    width = mg.shape[2]
-    canvases = mg.shape[0]
+    width = 2 * mg.shape[3]
+    canvases = mg.shape[1]
     own = o_mod.shape[0]
     whole = wm_in.shape[0] == own
     source = wm_in if whole else wm_in.at[pl.ds(pl.multiple_of(b * own, 16), own)]
@@ -1476,7 +1539,7 @@
 
     o_one[...] = window(one[...], own)[0:9]
     o_two[...] = window(two[...], o_two.shape[1])[0:9]
-    every = mg[...]
+    every = jnp.concatenate([mg[0], mg[1]], axis=2)
     begin = late[...]
     cond = window(every[:, 7, :] * 0.5, own)
     sigma = 1.0 / (1.0 + jnp.exp(-cond))
@@ -1505,7 +1568,7 @@
 
 def tail(fu, fd, fp, mg, late, one, two, wmod, res, ig, classes, times):
     nb = lax.axis_size("batch")
-    width = mg.shape[2]
+    width = 2 * mg.shape[3]
     own = width // nb
     wide = two.shape[1] // nb
     if own % 16:
@@ -1578,7 +1641,7 @@
         class_total, time_total, modulation_total, project_total, output_total,
         attention_kernel_total, up_total, feed_kernel_total, down_total, result, inputs_gradient,
     ) = tail(
-        fu, fd, fp, gathered.reshape(2 * nb, 8, width), late.reshape(2 * nb, 2, width), one, two,
+        fu, fd, fp, gathered.reshape(2, 2 * nb, 8, width // 2), late.reshape(2 * nb, 2, width), one, two,
         modulation_weight, result, inputs_gradient, class_table.shape[0], time_table.shape[0],
     )
     return (

time: 220 us -> 204 us (0.927)
  Pallas kernels: 218 us -> 202 us
    pallas_call x1, Pallas kernels: 92.8 us -> 76.6 us  [back(): pl.pallas_call(back_kernel, out_shape=(shape((2, 2, rows, width), bf16),...]
where the time goes in v5:
time: 204 us; the launch traced here: 203 us
  Pallas kernels  202 us (99%)
    pallas_call x1, Pallas kernels, feed(): pl.pallas_call(feed_kernel, grid=(units // tile,), out_shape=(shape((own,...  83.5 us
    pallas_call x1, Pallas kernels, back(): pl.pallas_call(back_kernel, out_shape=(shape((2, 2, rows, width), bf16),...  76.6 us
    pallas_call x1, Pallas kernels, front(): pl.pallas_call(front_kernel, out_shape=(shape((18, across, width), bf16),...  34.3 us
    pallas_call x1, Pallas kernels, tail(): pl.pallas_call(tail_kernel, out_shape=(shape((own, classes), f32), shape(...  7.57 us

profile of v5, /device:TPU:0, one launch (start us, length us, event | category | flops | bytes accessed | tf_op | source)
XLA Modules:
  0.0 202.9 jit_solution(8897761616684517672)
XLA Ops:
  0.6 34.3 %front.1 = (bf16[18,32,768]{2,1,0:T(8,128)(2,1)}, bf16[18,32,768]{2,1,0:T(8,128)(2,1)}, bf16[9,2,32,768]{3,2,1,0:T(8,128)(2,1)}, bf16[512,768]{1,0:T(8,128)(2,1)...) custom-call(bf16[2,8,32,768]{3,2,1,0:T(8,128)(2,1)} %x_in.1, ...), custom_call_target="tpu_custom_call" | custom-call | tf_op jit(solution)/shard_map/front/pallas_call | solution.py:308
  34.9 83.5 %feed.1 = (bf16[96,512]{1,0:T(8,128)(2,1)}, bf16[48,16,768]{2,1,0:T(8,128)(2,1)}, bf16[2,4,96,128]{3,2,1,0:T(8,128)(2,1)}, bf16[2,4,2,96,128]{4,3,2,1,0:T(8,128)...) custom-call(bf16[576,768]{1,0:T(8,128)(2,1)} %bitcast.9, ...), custom_call_target="tpu_custom_call" | custom-call | flops 14495514624 | bytes 18874368 | tf_op jit(solution)/shard_map/feed/pallas_call | solution.py:688
  118.5 76.6 %back.1 = (bf16[2,2,96,768]{3,2,1,0:T(8,128)(2,1)}, bf16[2,2,6,16,768]{4,3,2,1,0:T(8,128)(2,1)}, bf16[6,2,2,96,128]{4,3,2,1,0:T(8,128)(2,1)}, bf16[2,8,32,768]{3...) custom-call(f32[512,768]{1,0:T(8,128)} %get-tuple-element.54.mid_in,, ...), custom_call_target="tpu_custom_call" | custom-call | tf_op jit(solution)/shard_map/back/pallas_call | solution.py:1433
  195.1 7.6 %tail.1 = (f32[96,1000]{1,0:T(8,128)}, f32[96,1000]{1,0:T(8,128)}, f32[96,4608]{1,0:T(8,128)}, f32[96,2304]{1,0:T(8,128)}, f32[96,768]{1,0:T(8,128)}, /*index=5*...) custom-call(bf16[2,2,96,768]{3,2,1,0:T(8,128)(2,1)} %get-tuple-eleme, ...), custom_call_target="tpu_custom_call" | custom-call | tf_op jit(solution)/shard_map/tail/pallas_call | solution.py:1580

commit v6 on v5

--- a/solution.py
+++ b/solution.py
@@ -67,6 +67,19 @@
 def fold(values):
     rows, width = values.shape
     return jnp.sum(values.reshape(rows // 8, 8, width), axis=0)
+
+
+def grouped(count, body, carry, size=4, begin=0):
+    def several(i, carry):
+        for n in range(size):
+            carry = body(begin + size * i + n, carry)
+        return carry
+
+    whole = count // size
+    carry = lax.fori_loop(0, whole, several, carry)
+    for n in range(whole * size, count):
+        carry = body(begin + n, carry)
+    return carry
 
 
 def permutation(inverse):
@@ -201,7 +214,7 @@
         shifts[2, 1 - c + i] = after
         return carry
 
-    lax.fori_loop(0, 17, first, 0)
+    grouped(17, first, 0)
     for s in range(3):
         shifts[s, 17 * c] = jnp.zeros((across, width), f32)
 
@@ -275,7 +288,7 @@
         return carry
 
     lse[...] = jnp.zeros(lse.shape, f32)
-    lax.fori_loop(0, 2 * pairs, attend, 0)
+    grouped(2 * pairs, attend, 0)
     att_out = pltpu.make_async_copy(att, o_att, out_sem.at[3])
     att_out.start()
     lse_out = pltpu.make_async_copy(lse, o_lse, out_sem.at[4])
@@ -359,13 +372,17 @@
     return x * mass, mass + x * bell * 0.3989422804014327
 
 
+def tile_of(step, tiles):
+    return jnp.where(lax.rem(step, 2) == 0, step // 2, tiles - 1 - step // 2)
+
+
 def feed_kernel(
     x_in, ret_in, cot_in, mod, up, kern, down,
-    o_up, o_down, o_up_half, o_up_last, o_down_last, o_kern, o_res, o_mid, o_rg, o_small,
+    o_up, o_down, o_up_half, o_down_half, o_up_last, o_down_last, o_kern, o_res, o_mid, o_rg, o_small,
     feed_in, feed_t, btg, out_acc, back_acc, hid, hs, gs, act, slope, hg,
-    wu, wd, ru, rd, yu, xu, zu, fin, xd,
+    wu, wd, ru, rd, yu, xu, zu, fin, xd, yd, zd, fin_d,
     u1_send, u1_recv, u2_send, u2_recv, u3_send, u3_recv, d1_send, d1_recv, d2_send, d2_recv,
-    u4_send, u4_recv, u_out, d_out, l_out,
+    u4_send, u4_recv, d3_send, d3_recv, d4_send, d4_recv, u_out, d_out, l_out,
 ):
     j = pl.program_id(0)
     tiles = pl.num_programs(0)
@@ -401,13 +418,50 @@
         )
 
     def up_store(t):
-        spot = pl.ds(pl.multiple_of(t * LANES, LANES), LANES)
+        spot = pl.ds(pl.multiple_of(tile_of(t, tiles) * LANES, LANES), LANES)
         return pltpu.make_async_copy(fin.at[t], o_up.at[:, spot], u_out.at[t])
 
-    def down_store(t):
-        return pltpu.make_async_copy(
-            wd.at[t, c, p], o_down.at[pl.ds(t * parts, parts)], d_out.at[t]
+    per = fin_d.shape[0]
+
+    def owner_of(t, k):
+        place = parts * tile_of(t, tiles) + k
+        return place // per, lax.rem(place, per)
+
+    def down_3(t, k):
+        return remote(
+            wd.at[t, c, p, k], yd.at[t, k], d3_send.at[t, k], d3_recv.at[t, k], beside
         )
+
+    def down_4(t, k):
+        owner, spot = owner_of(t, k)
+        slot = lax.rem(zb - owner // 2 + nz, nz) - 1
+        return remote(
+            wd.at[t, c, p, k], zd.at[spot, slot], d4_send.at[t, k], d4_recv.at[spot, slot],
+            (2 * (owner // 2) + yb, g),
+        )
+
+    def each_part(t, away, here):
+        def step(k, carry):
+            owner, spot = owner_of(t, k)
+            mine = lax.rem(owner, 2) == yb
+
+            @pl.when(jnp.logical_not(mine))
+            def _():
+                away(k)
+
+            @pl.when(mine)
+            def _():
+                here(k, owner, spot)
+
+            return carry
+
+        lax.fori_loop(0, parts, step, 0)
+
+    def nothing(*_):
+        pass
+
+    def down_store(spot):
+        return pltpu.make_async_copy(fin_d.at[spot], o_down.at[spot], d_out.at[spot])
 
     def add_core(t):
         down_1(t).wait_recv()
@@ -418,17 +472,14 @@
             wu[t, c, x, z, y] = wu[t, c, x, z, y] + ru[t, x, z, y]
             return carry
 
-        lax.fori_loop(0, 4 * nz, step, 0)
+        grouped(4 * nz, step, 0)
 
         def step_down(i, carry):
-            x, n = i // 8, lax.rem(i, 8)
-            for k in range(parts // 8):
-                wd[t, c, x, n * (parts // 8) + k] = (
-                    wd[t, c, x, n * (parts // 8) + k] + rd[t, x, n * (parts // 8) + k]
-                )
+            x, k = i // parts, lax.rem(i, parts)
+            wd[t, c, x, k] = wd[t, c, x, k] + rd[t, x, k]
             return carry
 
-        lax.fori_loop(0, 16, step_down, 0)
+        grouped(2 * parts, step_down, 0)
 
     def add_beside(t):
         up_2(t).wait_recv()
@@ -438,7 +489,7 @@
             wu[t, c, x, z, yb] = wu[t, c, x, z, yb] + yu[t, x, z]
             return carry
 
-        lax.fori_loop(0, 2 * nz, step, 0)
+        grouped(2 * nz, step, 0)
 
     def add_side(t):
         up_3(t).wait_recv()
@@ -447,7 +498,7 @@
             wu[t, c, p, z, yb] = wu[t, c, p, z, yb] + xu[t, z]
             return carry
 
-        lax.fori_loop(0, nz, step, 0)
+        grouped(nz, step, 0)
         for d in range(1, nz):
             up_4(t, d).start()
 
@@ -462,15 +513,51 @@
     def add_side_down(t):
         down_2(t).wait_recv()
 
-        def step(n, carry):
-            for k in range(parts // 8):
-                wd[t, c, p, n * (parts // 8) + k] = (
-                    wd[t, c, p, n * (parts // 8) + k] + xd[t, n * (parts // 8) + k]
-                )
+        def step(k, carry):
+            wd[t, c, p, k] = wd[t, c, p, k] + xd[t, k]
             return carry
 
-        lax.fori_loop(0, 8, step, 0)
-        down_store(t).start()
+        grouped(parts, step, 0)
+
+    def send_beside_down(t):
+        each_part(t, lambda k: down_3(t, k).start(), nothing)
+
+    def add_beside_down(t):
+        def here(k, owner, spot):
+            down_3(t, k).wait_recv()
+            wd[t, c, p, k] = wd[t, c, p, k] + yd[t, k]
+
+            @pl.when(owner // 2 != zb)
+            def _():
+                down_4(t, k).start()
+
+        each_part(t, nothing, here)
+
+    def add_far_down(t):
+        def here(k, owner, spot):
+            @pl.when(owner // 2 == zb)
+            def _():
+                total = wd[t, c, p, k].astype(f32)
+                for d in range(1, nz):
+                    place = zd.at[spot, d - 1]
+                    pltpu.make_async_copy(place, place, d4_recv.at[spot, d - 1]).wait()
+                    total = total + zd[spot, d - 1].astype(f32)
+                fin_d[spot] = total.astype(bf16)
+                down_store(spot).start()
+
+        each_part(t, nothing, here)
+
+    def settle_down(t):
+        def here(k, owner, spot):
+            @pl.when(owner // 2 != zb)
+            def _():
+                down_4(t, k).wait_send()
+
+            @pl.when(owner // 2 == zb)
+            def _():
+                down_store(spot).wait()
+
+        each_part(t, lambda k: down_3(t, k).wait_send(), here)
 
     across = 32
     width = feed_in.shape[1]
@@ -494,7 +581,7 @@
             btg[place, :] = (mod[5:6, :] * cot_in[place, :].astype(f32)).astype(bf16)
             return carry
 
-        lax.fori_loop(0, frame_rows, prepare, 0)
+        grouped(frame_rows, prepare, 0)
         feed_t[...] = feed_in[own, :].T
         out_acc[...] = jnp.zeros(out_acc.shape, f32)
         back_acc[...] = jnp.zeros(back_acc.shape, f32)
@@ -512,7 +599,7 @@
         hs[2, 1 - c + row] = after
         return carry
 
-    lax.fori_loop(0, frame_rows, lay_hidden, 0)
+    grouped(frame_rows, lay_hidden, 0)
 
     for lane in range(0, tile, LANES):
         cut = slice(lane, lane + LANES)
@@ -529,12 +616,12 @@
             slope[place, cut] = steep
             return carry
 
-        lax.fori_loop(0, 17, forward, 0)
+        grouped(17, forward, 0)
 
     @pl.when(j >= 2)
     def _():
         add_side(j - 2)
-        add_side_down(j - 2)
+        add_beside_down(j - 2)
 
     @pl.when(j >= 1)
     def _():
@@ -545,6 +632,7 @@
     @pl.when(j >= 3)
     def _():
         add_far(j - 3)
+        add_far_down(j - 3)
 
     inside = pl.ds(pl.multiple_of(c * across, across), 16 * across)
     around = pl.ds(pl.multiple_of(c * across, across), 17 * across)
@@ -565,7 +653,7 @@
         gs[2, 1 - c + row] = before
         return carry
 
-    lax.fori_loop(0, 17, lay_grad, 0)
+    grouped(17, lay_grad, 0)
 
     for lane in range(0, tile, LANES):
         cut = slice(lane, lane + LANES)
@@ -583,9 +671,7 @@
             hg[pl.ds(pl.multiple_of(row * across, across), across), cut] = total.astype(bf16)
             return tuple(later)
 
-        sums = lax.fori_loop(
-            0, 16, backward, tuple(jnp.zeros((8, LANES), f32) for _ in range(9))
-        )
+        sums = grouped(16, backward, tuple(jnp.zeros((8, LANES), f32) for _ in range(9)))
         for n in range(9):
             o_kern[n : n + 1, cut] = jnp.sum(sums[n], axis=0, keepdims=True)
 
@@ -601,6 +687,8 @@
     def _():
         add_beside(j - 1)
         up_3(j - 1).start()
+        add_side_down(j - 1)
+        send_beside_down(j - 1)
 
     @pl.when(j == tiles - 1)
     def _():
@@ -620,31 +708,34 @@
             terms = (mid * returned, grad, grad * normal, cot * branch)
             return tuple(total + fold(term) for total, term in zip(sums, terms))
 
-        sums = lax.fori_loop(
-            0, 16, finish, tuple(jnp.zeros((8, width), f32) for _ in range(4))
-        )
+        sums = grouped(16, finish, tuple(jnp.zeros((8, width), f32) for _ in range(4)))
         o_small[...] = jnp.zeros((8, width), f32)
         for n in range(4):
             o_small[n + 2 : n + 3, :] = jnp.sum(sums[n], axis=0, keepdims=True)
-        add_far(j - 2)
         add_beside(j - 1)
         half = pltpu.make_async_copy(wu.at[j - 1, c, :, :, yb], o_up_half, l_out.at[2])
         half.start()
         add_side_down(j - 1)
+        half_down = pltpu.make_async_copy(wd.at[j - 1, c, p], o_down_half, l_out.at[3])
+        half_down.start()
         add_core(j)
         last = (
             half,
+            half_down,
             pltpu.make_async_copy(wu.at[j, c], o_up_last, l_out.at[0]),
             pltpu.make_async_copy(wd.at[j, c], o_down_last, l_out.at[1]),
         )
-        for move in last[1:]:
+        for move in last[2:]:
             move.start()
+        add_far(j - 2)
+        add_far_down(j - 2)
 
         def settle(t, carry):
             up_3(t).wait_send()
             for d in range(1, nz):
                 up_4(t, d).wait_send()
             up_store(t).wait()
+            settle_down(t)
             return carry
 
         def settle_more(t, carry):
@@ -652,7 +743,6 @@
             down_2(t).wait_send()
             up_1(t).wait_send()
             down_1(t).wait_send()
-            down_store(t).wait()
             return carry
 
         lax.fori_loop(0, tiles - 2, settle, 0)
@@ -682,16 +772,18 @@
     def still(*size):
         return pl.BlockSpec(size, lambda j: (0, 0), pipeline_mode=pl.Buffered(1))
 
-    columns = pl.BlockSpec((width, tile), lambda j: (0, j))
-    rows = pl.BlockSpec((tile, width), lambda j: (j, 0))
+    columns = pl.BlockSpec((width, tile), lambda j: (0, tile_of(j, tiles)))
+    rows = pl.BlockSpec((tile, width), lambda j: (tile_of(j, tiles), 0))
+    per = tiles * parts // nb
     work = 6 * 2 * tokens * width * units
     return pl.pallas_call(
         feed_kernel,
         grid=(units // tile,),
         out_shape=(
-            shape((own, (tiles - 2) * LANES), bf16),
-            shape((tiles * parts, grain, width), bf16),
+            shape((own, tiles * LANES), bf16),
+            shape((per, grain, width), bf16),
             shape((2, nz, own, LANES), bf16),
+            shape((parts, grain, width), bf16),
             shape((2, nz, 2, own, LANES), bf16),
             shape((2, parts, grain, width), bf16),
             shape((16, units), f32),
@@ -702,10 +794,10 @@
         ),
         in_specs=[
             still(frame, width), still(frame, width), still(frame, width), still(8, width),
-            columns, pl.BlockSpec((9, tile), lambda j: (0, j)), rows,
+            columns, pl.BlockSpec((9, tile), lambda j: (0, tile_of(j, tiles))), rows,
         ],
         out_specs=[
-            *[any_space] * 5, pl.BlockSpec((16, tile), lambda j: (0, j)),
+            *[any_space] * 6, pl.BlockSpec((16, tile), lambda j: (0, tile_of(j, tiles))),
             still(tokens, width), still(tokens, width), still(tokens, width), still(8, width),
         ],
         scratch_shapes=[
@@ -729,8 +821,12 @@
             pltpu.VMEM((tiles, many, own, LANES), bf16),
             pltpu.VMEM((tiles, own, LANES), bf16),
             pltpu.VMEM((tiles, parts, grain, width), bf16),
+            pltpu.VMEM((tiles, parts, grain, width), bf16),
+            pltpu.VMEM((per, many, grain, width), bf16),
+            pltpu.VMEM((per, grain, width), bf16),
             *[dma((tiles,)) for _ in range(10)],
-            dma((tiles, many)), dma((tiles, many)), dma((tiles,)), dma((tiles,)), dma((3,)),
+            dma((tiles, many)), dma((tiles, many)), dma((tiles, parts)), dma((tiles, parts)),
+            dma((tiles, parts)), dma((per, many)), dma((tiles,)), dma((per,)), dma((4,)),
         ],
         compiler_params=pltpu.CompilerParams(
             dimension_semantics=("arbitrary",), collective_id=3, has_side_effects=True,
@@ -745,15 +841,15 @@
 
 def back_kernel(
     mid_in, rg_in, tok_in, proj_in, att_in, lse, bias, x_in, mod, small, kern, wqkv_in, wo_in,
-    res_in, ud_in, dq_in, uh_in, ul_in, dl_in, kern_two,
+    res_in, ud_in, dd_in, uh_in, dh_in, ul_in, dl_in, kern_two,
     o_fu, o_fd, o_fp, o_res, o_ig, o_one, o_two, o_mg, o_ml,
     mid, tok, tok_t, proj, att, xf, wqkv, wo, rows_m, perm, grad, datt, dproj,
     brm, frame, gs, value, agrad, ig,
     wp, p_r1, p_r2x, p_r2y, p_r3, p_r4, fin_p,
-    fu, fd, fz_u, fy_d, fz_d, fin_u, fin_d, ld, lx_d, hx, ly, ly_r, lx,
+    fu, fd, fz_u, fy_d, fz_d, fin_u, fin_d, lx_d, hx, ly, ly_r, lx,
     mg_own, mg_r1, mg_all, ml_own, ml_r1, ml_all, taps_sum, kk_1, kr_1, kz_1,
     kt, kt_core, kt_side, kt_y, kt_sum, kt_z, fin_k,
-    load_sem, r_send, r_recv, i_send, i_recv, ex_send, ex_recv, own_sem, send_sem, recv_sem, out_sem,
+    dy_send, dy_recv, dz_send, dz_recv, load_sem, r_send, r_recv, i_send, i_recv, ex_send, ex_recv, own_sem, send_sem, recv_sem, out_sem,
 ):
     b = lax.axis_index("batch")
     g = lax.axis_index("group")
@@ -772,18 +868,21 @@
     size = tokens // 2
     chunks = wp.shape[0]
     chunk = wp.shape[-1]
-    lead = width - 2 * LANES
-    per, parts = fd.shape[2], ld.shape[0]
+    tiles = width // LANES
+    lead = (tiles // 2 - 1) * LANES
+    per, parts = fin_d.shape[2], lx_d.shape[0]
     places = {}
 
     def link(name, src, dst, target):
         n = places.setdefault(name, len(places))
         return remote(src, dst, send_sem.at[n], recv_sem.at[n], target)
 
-    def send_home(n, src, dst, send, recv, waiting):
-        move = remote(src.at[pl.ds(8 * n, 8)], dst.at[p], send.at[n], recv.at[p], (b, 2 * c + n))
-        away = remote(src.at[pl.ds(8 * n, 8)], dst.at[p], send.at[n], recv.at[p], core)
-        stay = pltpu.make_async_copy(src.at[pl.ds(8 * n, 8)], dst.at[p], recv.at[p])
+    def send_home(n, src, dst, send, recv, waiting, first=0, count=8):
+        from_rows = src.at[pl.ds(8 * n + first, count)]
+        to_rows = dst.at[p, pl.ds(first, count)]
+        move = remote(from_rows, to_rows, send.at[n], recv.at[p], (b, 2 * c + n))
+        away = remote(from_rows, to_rows, send.at[n], recv.at[p], core)
+        stay = pltpu.make_async_copy(from_rows, to_rows, recv.at[p])
 
         @pl.when(inner)
         def _():
@@ -825,14 +924,43 @@
     def last_d():
         return link("ld", dl_in.at[1 - p], lx_d, side)
 
-    def down_y():
-        return link("fdy", fd.at[:, 1 - yb], fy_d, beside)
+    def owner_of(k):
+        place = parts * (tiles // 2 - 1) + k
+        return place // per, lax.rem(place, per)
+
+    def down_y(k):
+        return remote(fd.at[k], fy_d.at[k], dy_send.at[k], dy_recv.at[k], beside)
+
+    def down_z(k):
+        owner, spot = owner_of(k)
+        slot = lax.rem(zb - owner // 2 + nz, nz) - 1
+        return remote(
+            fd.at[k], fz_d.at[spot, slot], dz_send.at[k], dz_recv.at[spot, slot],
+            (2 * (owner // 2) + yb, g),
+        )
+
+    def each_part(begin, away, here):
+        def step(k, carry):
+            owner, spot = owner_of(k)
+            mine = lax.rem(owner, 2) == yb
+
+            @pl.when(jnp.logical_not(mine))
+            def _():
+                away(k)
+
+            @pl.when(mine)
+            def _():
+                here(k, owner, spot)
+
+            return carry
+
+        lax.fori_loop(begin, begin + parts, step, 0)
+
+    def nothing(*_):
+        pass
 
     def up_z(d):
         return link(f"fuz{d}", fu.at[others[d]], fz_u.at[d - 1], far[d])
-
-    def down_z(d):
-        return link(f"fdz{d}", fd.at[others[d], yb], fz_d.at[d - 1], far[d])
 
     def to_side(name, fin, mine):
         x = p if mine else 1 - p
@@ -850,7 +978,7 @@
             fu[z, :, :LANES] = fu[z, :, :LANES] + hx[z]
             return carry
 
-        lax.fori_loop(0, nz, step, 0)
+        grouped(nz, step, 0)
 
     def last_y_add():
         early[1].wait()
@@ -861,7 +989,7 @@
             ly[x, z] = ly[x, z] + ly_r[x, z]
             return carry
 
-        lax.fori_loop(0, 2 * nz, step, 0)
+        grouped(2 * nz, step, 0)
         last_x().start()
 
     def last_x_add():
@@ -871,47 +999,71 @@
             fu[z, :, LANES:] = ly[p, z] + lx[z]
             return carry
 
-        lax.fori_loop(0, nz, step, 0)
+        grouped(nz, step, 0)
         for d in range(1, nz):
             up_z(d).start()
 
     def up_sum():
         early[2].wait()
+        early[3].wait()
         total = fu[zb].astype(f32)
         for d in range(1, nz):
             up_z(d).wait_recv()
             total = total + fz_u[d - 1].astype(f32)
-        fin_u[c, p, :, lead:] = total.astype(bf16)
+        fin_u[c, p, :, lead : lead + 2 * LANES] = total.astype(bf16)
         to_side("gu", fin_u, True).start()
 
+    def place_half():
+        late[0].wait()
+        each_part(0, lambda k: down_y(k).start(), nothing)
+
     def place_last():
-        for load in late:
-            load.wait()
+        late[1].wait()
         last_d().wait_recv()
-        for t in range(parts):
-            spot = 2 * nz * per - parts + t
-            owner = spot // per
-            fd[owner // 2, owner % 2, spot % per] = ld[t] + lx_d[t]
-        down_y().start()
-
-    def down_y_add():
-        down_y().wait_recv()
-
-        def step(z, carry):
-            fd[z, yb] = fd[z, yb] + fy_d[z]
+
+        def step(k, carry):
+            fd[parts + k] = fd[parts + k] + lx_d[k]
             return carry
 
-        lax.fori_loop(0, nz, step, 0)
-        for d in range(1, nz):
-            down_z(d).start()
+        grouped(parts, step, 0)
+        each_part(parts, lambda k: down_y(k).start(), nothing)
+
+    def down_y_add(begin):
+        def here(k, owner, spot):
+            down_y(k).wait_recv()
+            fd[k] = fd[k] + fy_d[k]
+
+            @pl.when(owner // 2 != zb)
+            def _():
+                down_z(k).start()
+
+        each_part(begin, nothing, here)
 
     def down_sum():
-        total = fd[zb, yb].astype(f32)
-        for d in range(1, nz):
-            down_z(d).wait_recv()
-            total = total + fz_d[d - 1].astype(f32)
-        fin_d[c, p] = total.astype(bf16)
+        early[4].wait()
+
+        def here(k, owner, spot):
+            @pl.when(owner // 2 == zb)
+            def _():
+                total = fd[k].astype(f32)
+                for d in range(1, nz):
+                    place = fz_d.at[spot, d - 1]
+                    pltpu.make_async_copy(place, place, dz_recv.at[spot, d - 1]).wait()
+                    total = total + fz_d[spot, d - 1].astype(f32)
+                fin_d[c, p, spot] = total.astype(bf16)
+
+        for begin in (0, parts):
+            each_part(begin, nothing, here)
         to_side("gd", fin_d, True).start()
+
+    def down_gone():
+        def here(k, owner, spot):
+            @pl.when(owner // 2 != zb)
+            def _():
+                down_z(k).wait_send()
+
+        for begin in (0, parts):
+            each_part(begin, lambda k: down_y(k).wait_send(), here)
 
     def pass_on(name, fin):
         to_side(name, fin, False).wait_recv()
@@ -960,7 +1112,7 @@
             wp[k, c, x, z, y] = wp[k, c, x, z, y] + p_r1[k, x, z, y]
             return carry
 
-        lax.fori_loop(0, 4 * nz, step, 0)
+        grouped(4 * nz, step, 0)
         p2(k).start()
 
     def p_add_2(k):
@@ -975,7 +1127,7 @@
                 wp[k, c, x, z, yb] = wp[k, c, x, z, yb] + p_r2y[k, x, z]
             return carry
 
-        lax.fori_loop(0, 2 * nz, step, 0)
+        grouped(2 * nz, step, 0)
         p3(k).start()
 
     def p_add_3(k):
@@ -985,7 +1137,7 @@
             wp[k, c, p, z, yb] = wp[k, c, p, z, yb] + p_r3[k, z]
             return carry
 
-        lax.fori_loop(0, nz, step, 0)
+        grouped(nz, step, 0)
         for d in range(1, nz):
             p4(k, d).start()
 
@@ -1002,9 +1154,10 @@
         p_core(k, True).start()
 
     peers = [core, side, beside]
+    order = [core, beside, side]
 
     def kern_copy(name, kk, kr, stage):
-        return link(f"{name}{stage}", kk.at[stage], kr.at[stage], peers[stage])
+        return link(f"{name}{stage}", kk.at[stage], kr.at[stage], order[stage])
 
     def kern_far(name, kk, kz, d):
         return link(f"{name}z{d}", kk.at[3], kz.at[d - 1], far[d])
@@ -1100,7 +1253,34 @@
             mg_far(part, d, lax.rem(zb + nz - d, nz)).wait_recv()
 
     soon = ("mg", mg_own, mg_r1, mg_all)
-    final = ("ml", ml_own, ml_r1, ml_all)
+
+    def ml_copy(stage, mine=True):
+        if stage == 0:
+            return link("ml0", ml_own, ml_r1, core)
+        if stage == 1:
+            place = ml_all.at[zb, yb if mine else 1 - yb, p]
+            return link("ml1", place, place, beside)
+        place = ml_all.at[:, :, p if mine else 1 - p]
+        return link("ml2", place, place, side)
+
+    def ml_far(d, z):
+        return link(f"mlz{d}", ml_all.at[z, :, p], ml_all.at[z, :, p], far[d])
+
+    def ml_step(stage):
+        if stage == 0:
+            ml_copy(0).wait_recv()
+            ml_all[zb, yb, p] = ml_own[...] + ml_r1[...]
+            ml_copy(1).start()
+        elif stage == 1:
+            ml_copy(1, False).wait_recv()
+            for d in range(1, nz):
+                ml_far(d, zb).start()
+        elif stage == 2:
+            for d in range(1, nz):
+                ml_far(d, lax.rem(zb + nz - d, nz)).wait_recv()
+            ml_copy(2).start()
+        else:
+            ml_copy(2, False).wait_recv()
 
     pieces = [
         (wo_in, wo), (att_in, att), (tok_in, tok), (proj_in, proj), (wqkv_in, wqkv), (x_in, xf),
@@ -1109,23 +1289,21 @@
     loads = [
         pltpu.make_async_copy(src, dst, load_sem.at[n]) for n, (src, dst) in enumerate(pieces)
     ]
-    full = dq_in.shape[0] - parts
     early = [
         pltpu.make_async_copy(uh_in.at[p], fu.at[:, :, pl.ds(0, LANES)], load_sem.at[7]),
         pltpu.make_async_copy(ul_in.at[:, :, yb], ly, load_sem.at[8]),
-        pltpu.make_async_copy(ud_in, fin_u.at[c, p, :, pl.ds(0, lead)], load_sem.at[9]),
+        *[
+            pltpu.make_async_copy(
+                ud_in.at[:, pl.ds(at, lead)], fin_u.at[c, p, :, pl.ds(at, lead)], load_sem.at[n]
+            )
+            for n, at in ((9, 0), (10, lead + 2 * LANES))
+        ],
+        pltpu.make_async_copy(dd_in, fin_d.at[c, p], load_sem.at[11]),
     ]
-    late = [pltpu.make_async_copy(dl_in.at[p], ld, load_sem.at[10])]
-    for owner in range(2 * nz):
-        count = min(per, full - owner * per)
-        if count > 0:
-            late.append(
-                pltpu.make_async_copy(
-                    dq_in.at[pl.ds(owner * per, count)],
-                    fd.at[owner // 2, owner % 2, pl.ds(0, count)],
-                    load_sem.at[11 + owner],
-                )
-            )
+    late = [
+        pltpu.make_async_copy(dh_in, fd.at[pl.ds(0, parts)], load_sem.at[12]),
+        pltpu.make_async_copy(dl_in.at[p], fd.at[pl.ds(parts, parts)], load_sem.at[13]),
+    ]
     for load in (*loads[:4], *late, *early, *loads[4:]):
         load.start()
     half_width, quarter = width // 2, kt.shape[3]
@@ -1163,9 +1341,6 @@
     loads[2].wait()
     tok_t[...] = tok[...].T
     loads[3].wait()
-    for n in range(2):
-        send_home(n, res_in, o_res, r_send, r_recv, False)
-
     low_lane = lax.broadcasted_iota(jnp.int32, (size, LANES), 1) < LANES // 2
     lane_id = lax.broadcasted_iota(jnp.int32, (size, LANES), 1)
     zero = jnp.zeros((), bf16)
@@ -1212,14 +1387,23 @@
         p1(2 * k).start()
         p1(2 * k + 1).start()
 
+    def res_home(n, i):
+        return lambda: send_home(n, res_in, o_res, r_send, r_recv, False, 2 * i, 2)
+
+    def ig_home(n, i):
+        send_home(n, ig, o_ig, i_send, i_recv, False, 2 * i, 2)
+
     hooks = {
         0: [lambda: mg_step(soon, 0), taps_core_add],
-        1: [half_add],
-        2: [place_last],
-        3: [lambda: weigh(0), last_y_add],
+        1: [half_add, place_half],
+        2: [place_last, res_home(0, 0)],
+        3: [lambda: weigh(0), last_y_add, res_home(0, 1)],
+        4: [res_home(0, 2)],
         5: [lambda: mg_step(soon, 1), taps_side_add],
+        6: [lambda: down_y_add(0), res_home(0, 3)],
         7: [lambda: weigh(1), lambda: p_add_1(0), lambda: p_add_1(1)],
-        9: [last_x_add],
+        8: [last_x_add, res_home(1, 0)],
+        9: [lambda: down_y_add(parts), res_home(1, 1)],
         10: [lambda: mg_step(soon, 2), taps_y_add],
         11: [lambda: weigh(2)],
     }
@@ -1249,6 +1433,7 @@
     p_add_2(1)
     p_add_1(2)
     p_add_1(3)
+    res_home(1, 2)()
     loads[5].wait()
     loads[6].wait()
 
@@ -1260,9 +1445,11 @@
         value[row] = (normal * scale_in + shift).astype(bf16).astype(f32)
         return carry
 
-    lax.fori_loop(0, 16, again, 0)
+    grouped(16, again, 0)
     p_add_1(4)
     p_add_1(5)
+    res_home(1, 3)()
+    up_sum()
     mixed_own.wait()
     mixed_away.wait()
 
@@ -1275,7 +1462,7 @@
         gs[2, 1 - c + row] = before
         return carry
 
-    lax.fori_loop(0, 17, lay, 0)
+    grouped(17, lay, 0)
     for s in range(3):
         gs[s, 17 * c] = jnp.zeros((across, width), f32)
 
@@ -1315,84 +1502,89 @@
         return (sums[0] + fold(line), sums[1] + fold(line * normal))
 
     sums = tuple(jnp.zeros((8, width), f32) for _ in range(2))
-    down_y_add()
     p_add_3(0)
     p_add_3(1)
+    down_sum()
     for lane in range(0, width, LANES):
         conv_back(lane, 0)
         if lane == 2 * LANES:
             p_add_2(2)
             p_add_2(3)
     sums = lax.fori_loop(0, 8, finish, sums)
-    send_home(0, ig, o_ig, i_send, i_recv, False)
+    ig_home(0, 0)
     p_add_2(4)
+    ig_home(0, 1)
     p_add_2(5)
+    ig_home(0, 2)
+    ig_home(0, 3)
+    pass_on("gu", fin_u)
+    taps_total()
     for lane in range(0, width, LANES):
         conv_back(lane, 1)
         if lane == 2 * LANES:
             p_add_3(2)
             p_add_3(3)
+            pass_on("gd", fin_d)
+            p_add_4(0)
+            p_add_4(1)
     kern_copy("one", kk_1, kr_1, 0).start()
     sums = lax.fori_loop(8, 16, finish, sums)
     for n in range(2):
         ml_own[n : n + 1, :] = jnp.sum(sums[n], axis=0, keepdims=True)
-    mg_copy(final, 0).start()
-    send_home(1, ig, o_ig, i_send, i_recv, False)
-    up_sum()
+    ml_copy(0).start()
+    ig_home(1, 0)
     p_add_3(4)
     p_add_3(5)
-    p_add_4(0)
-    p_add_4(1)
-    taps_total()
+    ig_home(1, 1)
     mg_end(soon)
     mg_swap().start()
     kern_step(*one, 0)
-    mg_step(final, 0)
-    down_sum()
-    pass_on("gu", fin_u)
+    ml_step(0)
+    ig_home(1, 2)
     p_pass(0)
     p_pass(1)
     pass_on("gk", fin_k)
-    kern_step(*one, 1)
-    mg_step(final, 1)
     p_add_4(2)
     p_add_4(3)
+    ig_home(1, 3)
+    kern_step(*one, 1)
+    ml_step(1)
     mg_swap(False).wait_recv()
     mg_out.start()
     to_core("gu", fin_u, False).wait_recv()
     u_out.start()
-    kern_step(*one, 2)
-    mg_step(final, 2)
-    pass_on("gd", fin_d)
+    to_core("gd", fin_d, False).wait_recv()
+    d_out.start()
     p_add_4(4)
     p_add_4(5)
+    kern_step(*one, 2)
+    ml_step(2)
     p_pass(2)
     p_pass(3)
-    to_core("gd", fin_d, False).wait_recv()
-    d_out.start()
-    kern_sum("one", kk_1, kz_1, o_one)
-    mg_end(final)
-    ml_out.start()
     p_pass(4)
     p_pass(5)
+    ml_step(3)
+    ml_out.start()
+    kern_sum("one", kk_1, kz_1, o_one)
     for k in range(chunks):
         p_core(k, False).wait_recv()
     p_out.start()
     to_core("gk", fin_k, False).wait_recv()
     for x in range(4):
         o_two[:, x * quarter : (x + 1) * quarter] = fin_k[x // 2, x % 2].astype(f32)
-    gone([half_x(), last_y(), last_x(), last_d(), down_y()])
+    gone([half_x(), last_y(), last_x(), last_d()])
+    down_gone()
     gone([taps_core(), taps_side(), taps_y(), mg_swap()])
     for name, fin in (("gu", fin_u), ("gd", fin_d), ("gk", fin_k)):
         gone([to_side(name, fin, True), to_core(name, fin, True)])
     for d in range(1, nz):
-        gone([up_z(d), down_z(d), mg_far(soon, d, zb), mg_far(final, d, zb)])
+        gone([up_z(d), mg_far(soon, d, zb), ml_far(d, zb)])
         gone([kern_far("one", kk_1, kz_1, d), taps_z(d)])
     for k in range(chunks):
         gone([p1(k), p2(k), p3(k), p_side(k, True), p_core(k, True)])
         gone([p4(k, d) for d in range(1, nz)])
     for stage in range(3):
-        gone([mg_copy(soon, stage), mg_copy(final, stage)])
+        gone([mg_copy(soon, stage), ml_copy(stage)])
         gone([kern_copy("one", kk_1, kr_1, stage)])
     for n in range(2):
         send_home(n, res_in, o_res, r_send, r_recv, True)
@@ -1405,16 +1597,16 @@
 
 def back(
     mid, rg, tok, proj, att, lse, bias, x_frame, mod, small, kern, wqkv, wo, res,
-    ud, dq, uh, ul, dl, kern_two,
+    ud, dd, uh, dh, ul, dl, kern_two,
 ):
     nb = lax.axis_size("batch")
     nz = nb // 2
     across, width = x_frame.shape[1], x_frame.shape[2]
     tokens = 16 * across
     rows = width // nb
-    grain = dq.shape[1]
+    grain = dd.shape[1]
     parts = dl.shape[1]
-    per = dq.shape[0] // nb
+    per = dd.shape[0]
     chunks, chunk = width // LANES, LANES
     many = max(nz - 1, 1)
     any_space = pl.BlockSpec(memory_space=pl.ANY)
@@ -1443,7 +1635,7 @@
             shape((2, nz, 2, 2, 8, width // 2), f32),
             shape((nz, 2, 2, 2, width), f32),
         ),
-        in_specs=[any_space] * 5 + [vmem, vmem, any_space, vmem, vmem, vmem] + [any_space] * 8
+        in_specs=[any_space] * 5 + [vmem, vmem, any_space, vmem, vmem, vmem] + [any_space] * 9
         + [vmem],
         out_specs=[any_space] * 5 + [vmem, vmem, any_space, any_space],
         scratch_shapes=[
@@ -1457,10 +1649,9 @@
             low(chunks, nz, 2, rows, chunk), low(chunks, 2, nz, rows, chunk),
             low(chunks, nz, rows, chunk), low(chunks, many, rows, chunk),
             low(chunks, 2, 2, rows, chunk),
-            low(nz, rows, 2 * LANES), low(nz, 2, per, grain, width),
-            low(many, rows, 2 * LANES), low(nz, per, grain, width), low(many, per, grain, width),
-            low(2, 2, rows, width), low(2, 2, per, grain, width),
-            low(parts, grain, width), low(parts, grain, width),
+            low(nz, rows, 2 * LANES), low(2 * parts, grain, width),
+            low(many, rows, 2 * LANES), low(2 * parts, grain, width), low(per, many, grain, width),
+            low(2, 2, rows, width), low(2, 2, per, grain, width), low(parts, grain, width),
             low(nz, rows, LANES), low(2, nz, rows, LANES), low(2, nz, rows, LANES),
             low(nz, rows, LANES),
             high(2, 8, width // 2), high(8, width // 2), high(2, nz, 2, 2, 8, width // 2),
@@ -1468,7 +1659,7 @@
             low(4, 16, width), low(3, 16, width), low(many, 16, width),
             low(2, 2, 16, wide // 4), low(2, 16, wide // 4), low(16, wide // 4), low(16, wide // 4),
             low(16, wide // 4), low(many, 16, wide // 4), low(2, 2, 16, wide // 4),
-            dma((11 + nb,)), dma((2,)), dma((2,)), dma((2,)), dma((2,)), dma((2,)), dma((2,)),
+            dma((2 * parts,)), dma((2 * parts,)), dma((2 * parts,)), dma((per, many)), dma((14,)), dma((2,)), dma((2,)), dma((2,)), dma((2,)), dma((2,)), dma((2,)),
             dma((2,)), dma((links,)), dma((links,)), dma((5,)),
         ],
         compiler_params=pltpu.CompilerParams(
@@ -1477,7 +1668,7 @@
         name="back",
     )(
         mid, rg, tok, proj, att, lse, bias, x_frame, mod, small, kern, wqkv, wo, res,
-        ud, dq, uh, ul, dl, kern_two,
+        ud, dd, uh, dh, ul, dl, kern_two,
     )
 
 
@@ -1622,20 +1813,21 @@
     across, width = inputs.shape[2], inputs.shape[3]
     nb = lax.axis_size("batch")
     units = up_weight.shape[1]
-    grain = 16 if (units // nb) % 64 == 0 else 8
+    share = units // nb
+    grain = 32 if share % 128 == 0 else 16 if share % 64 == 0 else 8
     x_frame, cot_frame, returned, tok, proj, att, lse, bias, mod = front(
         inputs, cotangent, class_labels, time_steps, segments, kernel_attention, class_table,
         time_table, modulation_weight, project_weight, output_weight,
     )
     flat = (18 * across, width)
-    ud, dq, uh, ul, dl, kern_two, res, mid, rg, small = feed(
+    ud, dd, uh, dh, ul, dl, kern_two, res, mid, rg, small = feed(
         x_frame.reshape(flat), returned.reshape(flat), cot_frame.reshape(flat), mod, up_weight,
         kernel_feed, down_weight, grain,
     )
     fu, fd, fp, result, inputs_gradient, one, two, gathered, late = back(
         mid, rg.reshape(8, 2, across, width), tok, proj, att, lse, bias, x_frame, mod, small,
         kernel_attention, project_weight, output_weight, res.reshape(16, across, width),
-        ud, dq, uh, ul, dl, kern_two,
+        ud, dd, uh, dh, ul, dl, kern_two,
     )
     (
         class_total, time_total, modulation_total, project_total, output_total,

time: 204 us -> 182 us (0.89)
  Pallas kernels: 202 us -> 181 us
    pallas_call x1, Pallas kernels: 83.5 us -> 72 us  [feed(): pl.pallas_call(feed_kernel, grid=(units // tile,), out_shape=(shape((own,...]
    pallas_call x1, Pallas kernels: 76.6 us -> 70.6 us  [back(): pl.pallas_call(back_kernel, out_shape=(shape((2, 2, rows, width), bf16),...]
    pallas_call x1, Pallas kernels: 34.3 us -> 30.6 us  [front(): pl.pallas_call(front_kernel, out_shape=(shape((18, across, width), bf16),...]
where the time goes in v6:
time: 182 us
  Pallas kernels  181 us (99%)
    pallas_call x1, Pallas kernels, feed(): pl.pallas_call(feed_kernel, grid=(units // tile,), out_shape=(shape((own,...  72 us
    pallas_call x1, Pallas kernels, back(): pl.pallas_call(back_kernel, out_shape=(shape((2, 2, rows, width), bf16),...  70.6 us
    pallas_call x1, Pallas kernels, front(): pl.pallas_call(front_kernel, out_shape=(shape((18, across, width), bf16),...  30.6 us
    pallas_call x1, Pallas kernels, tail(): pl.pallas_call(tail_kernel, out_shape=(shape((own, classes), f32), shape(...  7.57 us

profile of v6, /device:TPU:0, one launch (start us, length us, event | category | flops | bytes accessed | tf_op | source)
XLA Modules:
  0.0 181.6 jit_solution(17423954006950777398)
XLA Ops:
  0.6 30.6 %front.1 = (bf16[18,32,768]{2,1,0:T(8,128)(2,1)}, bf16[18,32,768]{2,1,0:T(8,128)(2,1)}, bf16[9,2,32,768]{3,2,1,0:T(8,128)(2,1)}, bf16[512,768]{1,0:T(8,128)(2,1)...) custom-call(bf16[2,8,32,768]{3,2,1,0:T(8,128)(2,1)} %x_in.1, ...), custom_call_target="tpu_custom_call" | custom-call | tf_op jit(solution)/shard_map/front/pallas_call | solution.py:321
  31.2 72.0 %feed.1 = (bf16[96,768]{1,0:T(8,128)(2,1)}, bf16[3,32,768]{2,1,0:T(8,128)(2,1)}, bf16[2,4,96,128]{3,2,1,0:T(8,128)(2,1)}, bf16[4,32,768]{2,1,0:T(8,128)(2,1)}, b...) custom-call(bf16[576,768]{1,0:T(8,128)(2,1)} %bitcast.9, ...), custom_call_target="tpu_custom_call" | custom-call | flops 14495514624 | bytes 18874368 | tf_op jit(solution)/shard_map/feed/pallas_call | solution.py:779
  103.2 70.6 %back.1 = (bf16[2,2,96,768]{3,2,1,0:T(8,128)(2,1)}, bf16[2,2,3,32,768]{4,3,2,1,0:T(8,128)(2,1)}, bf16[6,2,2,96,128]{4,3,2,1,0:T(8,128)(2,1)}, bf16[2,8,32,768]{3...) custom-call(f32[512,768]{1,0:T(8,128)} %get-tuple-element.55.mid_in,, ...), custom_call_target="tpu_custom_call" | custom-call | tf_op jit(solution)/shard_map/back/pallas_call | solution.py:1625
  173.8 7.6 %tail.1 = (f32[96,1000]{1,0:T(8,128)}, f32[96,1000]{1,0:T(8,128)}, f32[96,4608]{1,0:T(8,128)}, f32[96,2304]{1,0:T(8,128)}, f32[96,768]{1,0:T(8,128)}, /*index=5*...) custom-call(bf16[2,2,96,768]{3,2,1,0:T(8,128)(2,1)} %get-tuple-eleme, ...), custom_call_target="tpu_custom_call" | custom-call | tf_op jit(solution)/shard_map/tail/pallas_call | solution.py:1771

commit v7 on v6

--- a/solution.py
+++ b/solution.py
@@ -1686,8 +1686,8 @@
 
 def tail_kernel(
     fu, fd, fp, mg, late, one, two, wm_in, res_in, ig_in,
-    o_class, o_time, o_mod, o_proj, o_out, o_one, o_up, o_two, o_down, o_res, o_ig,
-    wm, moved, load_sem, in_sem, out_sem,
+    o_class, o_time, mod_out, proj_out, o_out, o_one, up_out, o_two, down_out, o_res, o_ig,
+    wm, moved, o_mod, o_proj, o_up, o_down, load_sem, in_sem, out_sem, big_sem,
 ):
     b = lax.axis_index("batch")
     width = 2 * mg.shape[3]
@@ -1705,6 +1705,12 @@
     ]
     for take in takes:
         take.start()
+    big = [
+        pltpu.make_async_copy(src, dst, big_sem.at[n])
+        for n, (src, dst) in enumerate(
+            ((o_up, up_out), (o_down, down_out), (o_proj, proj_out), (o_mod, mod_out))
+        )
+    ]
     chunks, chunk = fp.shape[0], fp.shape[4]
     per, grain = fd.shape[2], fd.shape[3]
     for q in range(4):
@@ -1720,6 +1726,8 @@
                 o_proj[:, q * width + k * chunk : q * width + (k + 1) * chunk] = part
             else:
                 o_out[:, k * chunk : (k + 1) * chunk] = part
+    for move in big[:3]:
+        move.start()
     for take, give in zip(takes, gives):
         take.wait()
         give.start()
@@ -1743,6 +1751,7 @@
         line = parts_of(begin[:, part, :] if part < 2 else every[:, part, :])
         o_mod[:, span] = dot_tn(low, line)
         act_grad = act_grad + dot_nt(line, wm[:, span])
+    big[3].start()
     act_grad = (
         act_grad[2 * canvases :] + act_grad[canvases : 2 * canvases] + act_grad[:canvases]
     )
@@ -1753,7 +1762,7 @@
     for n, out in enumerate((o_class, o_time)):
         hot = thrice(jnp.where(spot == names[:, n : n + 1], 1.0, 0.0))
         out[...] = dot_tn(cond_grad, hot)
-    for give in gives:
+    for give in (*gives, *big):
         give.wait()
 
 
@@ -1784,10 +1793,16 @@
             shape(ig.shape, bf16),
         ),
         in_specs=[vmem] * 7 + [any_space] * 3,
-        out_specs=[vmem] * 9 + [any_space] * 2,
+        out_specs=[
+            vmem, vmem, any_space, any_space, vmem, vmem, any_space, vmem, any_space, any_space,
+            any_space,
+        ],
         scratch_shapes=[
             pltpu.VMEM((own, 6 * width), bf16), pltpu.VMEM((2, *res.shape), bf16),
-            dma, dma((2,)), dma((2,)),
+            pltpu.VMEM((own, 6 * width), f32), pltpu.VMEM((own, 3 * width), f32),
+            pltpu.VMEM((own, 4 * width), f32),
+            pltpu.VMEM((4 * fd.shape[2] * fd.shape[3], width), f32),
+            dma, dma((2,)), dma((2,)), dma((4,)),
         ],
         compiler_params=pltpu.CompilerParams(vmem_limit_bytes=60 << 20),
         name="tail",

time: 182 us -> 182 us (level)
  no operation moved by 1% of the time
where the time goes in v7:
time: 182 us
  Pallas kernels  181 us (99%)
    pallas_call x1, Pallas kernels, feed(): pl.pallas_call(feed_kernel, grid=(units // tile,), out_shape=(shape((own,...  72 us
    pallas_call x1, Pallas kernels, back(): pl.pallas_call(back_kernel, out_shape=(shape((2, 2, rows, width), bf16),...  70.6 us
    pallas_call x1, Pallas kernels, front(): pl.pallas_call(front_kernel, out_shape=(shape((18, across, width), bf16),...  30.6 us
    pallas_call x1, Pallas kernels, tail(): pl.pallas_call(tail_kernel, out_shape=(shape((own, classes), f32), shape(...  8.12 us

profile of v7, /device:TPU:0, one launch (start us, length us, event | category | flops | bytes accessed | tf_op | source)
XLA Modules:
  0.0 182.1 jit_solution(16883000050205842580)
XLA Ops:
  0.6 30.6 %front.1 = (bf16[18,32,768]{2,1,0:T(8,128)(2,1)}, bf16[18,32,768]{2,1,0:T(8,128)(2,1)}, bf16[9,2,32,768]{3,2,1,0:T(8,128)(2,1)}, bf16[512,768]{1,0:T(8,128)(2,1)...) custom-call(bf16[2,8,32,768]{3,2,1,0:T(8,128)(2,1)} %x_in.1, ...), custom_call_target="tpu_custom_call" | custom-call | tf_op jit(solution)/shard_map/front/pallas_call | solution.py:321
  31.2 72.0 %feed.1 = (bf16[96,768]{1,0:T(8,128)(2,1)}, bf16[3,32,768]{2,1,0:T(8,128)(2,1)}, bf16[2,4,96,128]{3,2,1,0:T(8,128)(2,1)}, bf16[4,32,768]{2,1,0:T(8,128)(2,1)}, b...) custom-call(bf16[576,768]{1,0:T(8,128)(2,1)} %bitcast.9, ...), custom_call_target="tpu_custom_call" | custom-call | flops 14495514624 | bytes 18874368 | tf_op jit(solution)/shard_map/feed/pallas_call | solution.py:779
  103.2 70.6 %back.1 = (bf16[2,2,96,768]{3,2,1,0:T(8,128)(2,1)}, bf16[2,2,3,32,768]{4,3,2,1,0:T(8,128)(2,1)}, bf16[6,2,2,96,128]{4,3,2,1,0:T(8,128)(2,1)}, bf16[2,8,32,768]{3...) custom-call(f32[512,768]{1,0:T(8,128)} %get-tuple-element.55.mid_in,, ...), custom_call_target="tpu_custom_call" | custom-call | tf_op jit(solution)/shard_map/back/pallas_call | solution.py:1625
  173.8 8.1 %tail.1 = (f32[96,1000]{1,0:T(8,128)}, f32[96,1000]{1,0:T(8,128)}, f32[96,4608]{1,0:T(8,128)}, f32[96,2304]{1,0:T(8,128)}, f32[96,768]{1,0:T(8,128)}, /*index=5*...) custom-call(bf16[2,2,96,768]{3,2,1,0:T(8,128)(2,1)} %get-tuple-eleme, ...), custom_call_target="tpu_custom_call" | custom-call | tf_op jit(solution)/shard_map/tail/pallas_call | solution.py:1780
